TPU v7x, 256 devices: a whole 4x4x8 slice. The times are simulated.
256 devices in a mesh: load: 8 (over z), dom: 32 (over x, y, core).
Axes of the slice: x: 4, y: 4, z: 8, core: 2. Of those that a mesh axis runs over, the one named last changes fastest.
Arguments:
- displacement: float32 [8, 6, 262144], P('load', None, 'dom'), may hold values from -6 to 6
- adjoint: float32 [8, 6, 262144], P('load', None, 'dom'), may hold values from -0.12 to 0.12
- send_list: int32 [32, 32, 512], P('dom'), may hold values from 0 to 8191
- connect: int32 [4, 262144], P(None, 'dom'), may hold values from 0 to 11263, as said below
- elem_comp: int32 [262144], P('dom'), may hold values from 0 to 399, as said below
- elem_dv: int32 [262144], P('dom'), may hold values from 0 to 65535, as said below
- thickness: float32 [65536], P('dom'), may hold values from 0.5 to 1.5
- multiplier: float32 [8, 400], P('load'), may hold values from 0.2 to 2
- k_memb: float32 [24, 24], replicated, may hold values from -1.25 to 1.25
- k_bend: float32 [24, 24], replicated, may hold values from -1.25 to 1.25
- s_memb: float32 [8, 24], replicated, may hold values from -1.25 to 1.25
- s_bend: float32 [8, 24], replicated, may hold values from -1.25 to 1.25
Outputs:
- ks_value: float32 [8, 400], P('load')
- sensitivity: float32 [65536], P('dom')
Inputs may be any that keep to these rules, and one draw needn't show every extreme that they name: `connect`: an entry below 8192 is an own node of the element's partition; an entry v of 8192 or more refers to row (v - 8192) % 512 of the interface block received from a partition at most 3 places away in cyclic partition order. Some block is referenced up to its last row. `elem_comp`: every component has elements. `elem_dv`: in each aligned block of 1024 elements, at most 64 elements name variables of one owner partition (variables d with the same d // 2048); in every block some owner has exactly 64.
All inputs are finite; a program needn't handle non-finite values.
Results may differ from a plain program's by a relative error of at most 0.0003.
Values sent between devices are 32-bit elements; how exact they have to be, the bound alone decides.
No kernel may reach another device: no remote copies, remote signals or barrier semaphores. Data moves between devices by JAX's collectives and lax.ppermute only.
A program may use at most 64 MiB of HBM per device.

v0:
```python
import jax
import jax.numpy as jnp
from jax import lax
from jax.sharding import PartitionSpec as P

NBR = 3


sharpness = 50.0
block_rows = 2048
floor_value = -1e30


def shifted(block, axis, distance):
    devices = range(lax.axis_size(axis))
    route = [((i - distance) % len(devices), i) for i in devices]
    return lax.ppermute(block, axis, route)


def laid_out(tiles, dim):
    lengths = list(tiles.shape[1:])
    lengths[dim] *= tiles.shape[0]
    return jnp.moveaxis(tiles, 0, dim).reshape(lengths)


def from_everyone(x, axis):
    count = lax.axis_size(axis)
    return lax.all_to_all(jnp.broadcast_to(x[None], (count, *x.shape)), axis, 0, 0, tiled=True)


def collect(x, axis, dim):
    return laid_out(from_everyone(x, axis), dim)


def gathered_once(x, axis):
    leaves = jax.tree.leaves(x)
    order = sorted(range(len(leaves)), key=lambda k: -leaves[k].size)
    width = (1, *leaves[order[0]].shape)[-1]
    lines = [
        jnp.pad(leaves[k].reshape(-1), (0, -leaves[k].size % width)).reshape(-1, width)
        for k in order
    ]
    both, at, found = (from_everyone(jnp.concatenate(lines), axis), 0, {})
    for k, line in zip(order, lines):
        section = both[:, at : at + len(line)].reshape(len(both), -1)
        found[k] = section[:, : leaves[k].size].reshape(-1, *leaves[k].shape)
        at += len(line)
    numbers = iter(range(len(leaves)))
    return jax.tree.map(lambda _: found[next(numbers)], x)


def folded_in_pairs(pieces, combine):
    while len(jax.tree.leaves(pieces)[0]) > 1:
        pieces = jax.vmap(combine)(
            *(jax.tree.map(lambda part: part[side::2], pieces) for side in (0, 1))
        )
    return jax.tree.map(lambda part: part[0], pieces)


def joined_all(x, axis, combine):
    pieces = gathered_once(x, axis)
    return folded_in_pairs(pieces, combine)


def split_up(x, dim, count):
    before, after = (x.shape[:dim], x.shape[dim + 1 :])
    return jnp.moveaxis(x.reshape(*before, count, -1, *after), dim, 0)


def sent_and_summed(x, axis, dim):
    tiles = split_up(x, dim, lax.axis_size(axis))
    arrived = lax.all_to_all(tiles, axis, split_axis=0, concat_axis=0, tiled=True)
    return arrived.sum(axis=0)


def over_copies(x, axis):
    return from_everyone(x, axis).sum(axis=0)


def cycle_offsets(reach):
    return [j - reach if j < reach else j - reach + 1 for j in range(2 * reach)]


def split_width():
    return 128


def pick_columns(table, index):
    height = table.shape[0]
    count = table.shape[1]
    inner = split_width()
    outer = count // inner
    folded = table.reshape(height, outer, inner)
    total = index.shape[0]
    rows = min(total, block_rows)
    idx_blocks = index.reshape(-1, rows)
    inner_ids = jnp.arange(inner, dtype=jnp.int32)
    outer_ids = jnp.arange(outer, dtype=jnp.int32)

    def pick_one_block(block_index):
        low_hot = ((block_index % inner)[:, None] == inner_ids[None, :]).astype(jnp.float32)
        chosen = jnp.einsum("rhl,bl->rhb", folded, low_hot, precision=lax.Precision.HIGHEST)
        high_hit = outer_ids[:, None] == (block_index // inner)[None, :]
        return jnp.sum(jnp.where(high_hit[None], chosen, 0.0), axis=1)

    picked = lax.map(pick_one_block, idx_blocks)
    return jnp.moveaxis(picked, 1, 0).reshape(height, total)


def sum_to_slots(values, index, count):
    inner = split_width()
    outer = count // inner
    total = index.shape[0]
    rows = min(total, block_rows)
    idx_blocks = index.reshape(-1, rows)
    val_blocks = values.reshape(-1, rows)
    inner_ids = jnp.arange(inner, dtype=jnp.int32)
    outer_ids = jnp.arange(outer, dtype=jnp.int32)

    def step(carry, pair):
        block_index, block_values = pair
        low_part = jnp.where(
            (block_index % inner)[:, None] == inner_ids[None, :], block_values[:, None], 0.0
        )
        high_hot = ((block_index // inner)[:, None] == outer_ids[None, :]).astype(jnp.float32)
        added = jnp.einsum("bh,bl->hl", high_hot, low_part, precision=lax.Precision.HIGHEST)
        return (carry + added, None)

    start = jnp.zeros((outer, inner), jnp.float32)
    return lax.scan(step, start, (idx_blocks, val_blocks))[0].reshape(count)


def blocked(values, labels):
    rows = min(values.shape[-1], block_rows)
    return (values.reshape(-1, rows), labels.reshape(-1, rows))


def component_peak(failure, labels, comps):
    vals, labs = blocked(failure, labels)
    idents = jnp.arange(comps, dtype=jnp.int32)

    def step(carry, pair):
        hit = pair[1][:, None] == idents[None, :]
        return (
            jnp.maximum(carry, jnp.max(jnp.where(hit, pair[0][:, None], floor_value), axis=0)),
            None,
        )

    start = jnp.full((comps,), floor_value, jnp.float32)
    return lax.scan(step, start, (vals, labs))[0]


def component_total(failure, labels, peak):
    vals, labs = blocked(failure, labels)
    idents = jnp.arange(peak.shape[0], dtype=jnp.int32)

    def step(carry, pair):
        hit = pair[1][:, None] == idents[None, :]
        term = jnp.where(hit, jnp.exp(sharpness * (pair[0][:, None] - peak[None, :])), 0.0)
        return (carry + jnp.sum(term, axis=0), None)

    return lax.scan(step, jnp.zeros_like(peak), (vals, labs))[0]


def component_lookup(table, labels):
    rows = min(labels.shape[0], block_rows)
    labs = labels.reshape(-1, rows)
    idents = jnp.arange(table.shape[1], dtype=jnp.int32)

    def component_one_block(block_labels):
        hit = block_labels[:, None] == idents[None, :]
        return jnp.sum(jnp.where(hit[None], table[:, None, :], 0.0), axis=2)

    picked = lax.map(component_one_block, labs)
    return jnp.moveaxis(picked, 1, 0).reshape(table.shape[0], -1)


def send_block(states, targets, domains, here, offset):
    listed = lax.dynamic_index_in_dim(targets, (here - offset) % domains, 0, keepdims=False)
    outgoing = pick_columns(states, listed)
    return shifted(outgoing, "dom", -offset)


def per_device(
    displacement,
    adjoint,
    send_list,
    connect,
    elem_comp,
    elem_dv,
    thickness,
    multiplier,
    k_memb,
    k_bend,
    s_memb,
    s_bend,
):
    domains = lax.axis_size("dom")
    here = lax.axis_index("dom")
    comps = multiplier.shape[1]
    states = jnp.concatenate([displacement[0], adjoint[0]], axis=0)
    targets = send_list[0]
    offsets = cycle_offsets(NBR)
    blocks = [send_block(states, targets, domains, here, offset) for offset in offsets]
    extended = jnp.concatenate([states] + blocks, axis=1)
    elems = connect.shape[1]
    local = pick_columns(extended, connect.reshape(-1)).reshape(2, -1, elems)
    motion = local[0]
    costate = local[1]
    every_value = collect(thickness, "dom", 0)
    panel = pick_columns(every_value[None, :], elem_dv)[0]
    high = lax.Precision.HIGHEST
    bending = jnp.dot(s_bend, motion, precision=high)
    stress = jnp.dot(s_memb, motion, precision=high) + panel * bending
    failure = jnp.sum(stress * stress, axis=0) / stress.shape[0]
    own_peak = component_peak(failure, elem_comp, comps)
    own_total = component_total(failure, elem_comp, own_peak)

    def combine(first, second):
        top = jnp.maximum(first[0], second[0])
        summed = first[1] * jnp.exp(sharpness * (first[0] - top)) + second[1] * jnp.exp(
            sharpness * (second[0] - top)
        )
        return (top, summed)

    peak, total = joined_all((own_peak, own_total), "dom", combine)
    ks_value = peak + jnp.log(total) / sharpness
    looked = component_lookup(jnp.stack([peak, total, multiplier[0]]), elem_comp)
    scaled = jnp.exp(sharpness * (failure - looked[0]))
    explicit = (
        looked[2] * scaled / looked[1] * (2.0 / stress.shape[0]) * jnp.sum(stress * bending, axis=0)
    )
    stiff = jnp.dot(k_memb, motion, precision=high) + 3.0 * panel * panel * jnp.dot(
        k_bend, motion, precision=high
    )
    implicit = jnp.sum(costate * stiff, axis=0)
    element_terms = explicit + implicit
    partial_sum = sum_to_slots(element_terms, elem_dv, every_value.shape[0])
    owned = sent_and_summed(partial_sum, "dom", 0)
    sensitivity = over_copies(owned, "load")
    return (ks_value[None, :], sensitivity)


def solution(mesh):
    in_specs = (
        P("load", None, "dom"),
        P("load", None, "dom"),
        P("dom", None, None),
        P(None, "dom"),
        P("dom"),
        P("dom"),
        P("dom"),
        P("load", None),
        P(),
        P(),
        P(),
        P(),
    )
    out_specs = (P("load", None), P("dom"))
    return jax.shard_map(
        per_device, mesh=mesh, in_specs=in_specs, out_specs=out_specs, check_vma=False
    )
```

profile of v0, /device:TPU:1, one launch (start us, length us, event | category | flops | bytes accessed | tf_op | source)
XLA Modules:
  0.0 216.3 jit_solution(15626011711740196402)
XLA Ops:
  15.2 4.8 %collective-permute-start.4 = (f32[12,512]{1,0:T(8,128)S(1)}, f32[12,512]{1,0:T(8,128)S(1)}, u32[]{:S(2)}, u32[]{:S(2)}) collective-permute-start(f32[12,512]{1,0:T(8,128)S(1)} %select_reduce_fusion.4), channel_id=1, source_target_pairs={{2,0},{3,1},{4,2},{5,3},{6,4},{7,5},{8,6},{9,7},{10,8},{11,9},{12,... | collective-permute-start | bytes 73736 | tf_op jit(solution)/shard_map/ppermute | solution.py:17
  20.9 5.2 %all-to-all-start = ((f32[32,1,2048]{2,1,0:T(1,128)}), f32[32,1,2048]{2,1,0:T(1,128)}, u32[]{:S(2)}, u32[]{:S(2)}) async-start(f32[32,1,2048]{2,1,0:T(1,128)} %broadcast_in_dim.315), calls=%async_computation | async-start | bytes 524288 | tf_op jit(solution)/shard_map/all_to_all | solution.py:28
  27.7 5.3 %collective-permute-start.5 = (f32[12,512]{1,0:T(8,128)S(1)}, f32[12,512]{1,0:T(8,128)S(1)}, u32[]{:S(2)}, u32[]{:S(2)}) collective-permute-start(f32[12,512]{1,0:T(8,128)S(1)} %select_reduce_fusion.3), channel_id=1, source_target_pairs={{3,0},{4,1},{5,2},{6,3},{7,4},{8,5},{9,6},{10,7},{11,8},{12,9},{13... | collective-permute-start | bytes 73736 | tf_op jit(solution)/shard_map/ppermute | solution.py:17
  34.3 84.5 %while.96 = (s32[]{:T(128)}, f32[16,12,2048]{2,1,0:T(8,128)}, s32[16,2048]{1,0:T(8,128)S(1)}, f32[12,88,128]{2,1,0:T(8,128)S(1)}, s32[]{:T(128)}) while((s32[]{:T(128)}, f32[16,12,2048]{2,1,0:T(8,128)}, s32[16,2048]{1,0:T(8,128)S(1)}, f32[12,88,128]{2,1,0:T(8,128)S(1)}, s32[]{:T(128)}) %tuple.180), condition=%wide.region_8.9_spmd.clone, body=%wide.region_6.8_spmd.clone.sunk | while | flops 3326685184 | bytes 1286721 | solution.py:106
  34.5 4.4 %fusion.100 = f32[12,2048]{1,0:T(8,128)S(1)} fusion(f32[12,88,128]{2,1,0:T(8,128)S(1)} %get-tuple-element.810, pred[88,2048]{1,0:T(8,128)(4,1)S(1)} %iota_compare_fusion.30, s32[2048]{0:T(1024)S(1)} %add_select_fusion.19), kind=kOutput, calls=%fused_computation.10.clone.1 | convolution fusion | flops 3326451712 | bytes 827392 | tf_op jit(solution)/shard_map/while/body/eval_jaxpr/rhl,bl->rhb/dot_general | solution.py:102
  39.7 4.4 %fusion.100 = f32[12,2048]{1,0:T(8,128)S(1)} fusion(f32[12,88,128]{2,1,0:T(8,128)S(1)} %get-tuple-element.810, pred[88,2048]{1,0:T(8,128)(4,1)S(1)} %iota_compare_fusion.30, s32[2048]{0:T(1024)S(1)} %add_select_fusion.19), kind=kOutput, calls=%fused_computation.10.clone.1 | convolution fusion | flops 3326451712 | bytes 827392 | tf_op jit(solution)/shard_map/while/body/eval_jaxpr/rhl,bl->rhb/dot_general | solution.py:102
  45.0 4.4 %fusion.100 = f32[12,2048]{1,0:T(8,128)S(1)} fusion(f32[12,88,128]{2,1,0:T(8,128)S(1)} %get-tuple-element.810, pred[88,2048]{1,0:T(8,128)(4,1)S(1)} %iota_compare_fusion.30, s32[2048]{0:T(1024)S(1)} %add_select_fusion.19), kind=kOutput, calls=%fused_computation.10.clone.1 | convolution fusion | flops 3326451712 | bytes 827392 | tf_op jit(solution)/shard_map/while/body/eval_jaxpr/rhl,bl->rhb/dot_general | solution.py:102
  50.3 4.4 %fusion.100 = f32[12,2048]{1,0:T(8,128)S(1)} fusion(f32[12,88,128]{2,1,0:T(8,128)S(1)} %get-tuple-element.810, pred[88,2048]{1,0:T(8,128)(4,1)S(1)} %iota_compare_fusion.30, s32[2048]{0:T(1024)S(1)} %add_select_fusion.19), kind=kOutput, calls=%fused_computation.10.clone.1 | convolution fusion | flops 3326451712 | bytes 827392 | tf_op jit(solution)/shard_map/while/body/eval_jaxpr/rhl,bl->rhb/dot_general | solution.py:102
  55.6 4.4 %fusion.100 = f32[12,2048]{1,0:T(8,128)S(1)} fusion(f32[12,88,128]{2,1,0:T(8,128)S(1)} %get-tuple-element.810, pred[88,2048]{1,0:T(8,128)(4,1)S(1)} %iota_compare_fusion.30, s32[2048]{0:T(1024)S(1)} %add_select_fusion.19), kind=kOutput, calls=%fused_computation.10.clone.1 | convolution fusion | flops 3326451712 | bytes 827392 | tf_op jit(solution)/shard_map/while/body/eval_jaxpr/rhl,bl->rhb/dot_general | solution.py:102
  60.9 4.4 %fusion.100 = f32[12,2048]{1,0:T(8,128)S(1)} fusion(f32[12,88,128]{2,1,0:T(8,128)S(1)} %get-tuple-element.810, pred[88,2048]{1,0:T(8,128)(4,1)S(1)} %iota_compare_fusion.30, s32[2048]{0:T(1024)S(1)} %add_select_fusion.19), kind=kOutput, calls=%fused_computation.10.clone.1 | convolution fusion | flops 3326451712 | bytes 827392 | tf_op jit(solution)/shard_map/while/body/eval_jaxpr/rhl,bl->rhb/dot_general | solution.py:102
  66.1 4.4 %fusion.100 = f32[12,2048]{1,0:T(8,128)S(1)} fusion(f32[12,88,128]{2,1,0:T(8,128)S(1)} %get-tuple-element.810, pred[88,2048]{1,0:T(8,128)(4,1)S(1)} %iota_compare_fusion.30, s32[2048]{0:T(1024)S(1)} %add_select_fusion.19), kind=kOutput, calls=%fused_computation.10.clone.1 | convolution fusion | flops 3326451712 | bytes 827392 | tf_op jit(solution)/shard_map/while/body/eval_jaxpr/rhl,bl->rhb/dot_general | solution.py:102
  71.4 4.4 %fusion.100 = f32[12,2048]{1,0:T(8,128)S(1)} fusion(f32[12,88,128]{2,1,0:T(8,128)S(1)} %get-tuple-element.810, pred[88,2048]{1,0:T(8,128)(4,1)S(1)} %iota_compare_fusion.30, s32[2048]{0:T(1024)S(1)} %add_select_fusion.19), kind=kOutput, calls=%fused_computation.10.clone.1 | convolution fusion | flops 3326451712 | bytes 827392 | tf_op jit(solution)/shard_map/while/body/eval_jaxpr/rhl,bl->rhb/dot_general | solution.py:102
  76.7 4.4 %fusion.100 = f32[12,2048]{1,0:T(8,128)S(1)} fusion(f32[12,88,128]{2,1,0:T(8,128)S(1)} %get-tuple-element.810, pred[88,2048]{1,0:T(8,128)(4,1)S(1)} %iota_compare_fusion.30, s32[2048]{0:T(1024)S(1)} %add_select_fusion.19), kind=kOutput, calls=%fused_computation.10.clone.1 | convolution fusion | flops 3326451712 | bytes 827392 | tf_op jit(solution)/shard_map/while/body/eval_jaxpr/rhl,bl->rhb/dot_general | solution.py:102
  82.0 4.4 %fusion.100 = f32[12,2048]{1,0:T(8,128)S(1)} fusion(f32[12,88,128]{2,1,0:T(8,128)S(1)} %get-tuple-element.810, pred[88,2048]{1,0:T(8,128)(4,1)S(1)} %iota_compare_fusion.30, s32[2048]{0:T(1024)S(1)} %add_select_fusion.19), kind=kOutput, calls=%fused_computation.10.clone.1 | convolution fusion | flops 3326451712 | bytes 827392 | tf_op jit(solution)/shard_map/while/body/eval_jaxpr/rhl,bl->rhb/dot_general | solution.py:102
  87.3 4.4 %fusion.100 = f32[12,2048]{1,0:T(8,128)S(1)} fusion(f32[12,88,128]{2,1,0:T(8,128)S(1)} %get-tuple-element.810, pred[88,2048]{1,0:T(8,128)(4,1)S(1)} %iota_compare_fusion.30, s32[2048]{0:T(1024)S(1)} %add_select_fusion.19), kind=kOutput, calls=%fused_computation.10.clone.1 | convolution fusion | flops 3326451712 | bytes 827392 | tf_op jit(solution)/shard_map/while/body/eval_jaxpr/rhl,bl->rhb/dot_general | solution.py:102
  92.5 4.4 %fusion.100 = f32[12,2048]{1,0:T(8,128)S(1)} fusion(f32[12,88,128]{2,1,0:T(8,128)S(1)} %get-tuple-element.810, pred[88,2048]{1,0:T(8,128)(4,1)S(1)} %iota_compare_fusion.30, s32[2048]{0:T(1024)S(1)} %add_select_fusion.19), kind=kOutput, calls=%fused_computation.10.clone.1 | convolution fusion | flops 3326451712 | bytes 827392 | tf_op jit(solution)/shard_map/while/body/eval_jaxpr/rhl,bl->rhb/dot_general | solution.py:102
  97.8 4.4 %fusion.100 = f32[12,2048]{1,0:T(8,128)S(1)} fusion(f32[12,88,128]{2,1,0:T(8,128)S(1)} %get-tuple-element.810, pred[88,2048]{1,0:T(8,128)(4,1)S(1)} %iota_compare_fusion.30, s32[2048]{0:T(1024)S(1)} %add_select_fusion.19), kind=kOutput, calls=%fused_computation.10.clone.1 | convolution fusion | flops 3326451712 | bytes 827392 | tf_op jit(solution)/shard_map/while/body/eval_jaxpr/rhl,bl->rhb/dot_general | solution.py:102
  103.1 4.4 %fusion.100 = f32[12,2048]{1,0:T(8,128)S(1)} fusion(f32[12,88,128]{2,1,0:T(8,128)S(1)} %get-tuple-element.810, pred[88,2048]{1,0:T(8,128)(4,1)S(1)} %iota_compare_fusion.30, s32[2048]{0:T(1024)S(1)} %add_select_fusion.19), kind=kOutput, calls=%fused_computation.10.clone.1 | convolution fusion | flops 3326451712 | bytes 827392 | tf_op jit(solution)/shard_map/while/body/eval_jaxpr/rhl,bl->rhb/dot_general | solution.py:102
  108.4 4.4 %fusion.100 = f32[12,2048]{1,0:T(8,128)S(1)} fusion(f32[12,88,128]{2,1,0:T(8,128)S(1)} %get-tuple-element.810, pred[88,2048]{1,0:T(8,128)(4,1)S(1)} %iota_compare_fusion.30, s32[2048]{0:T(1024)S(1)} %add_select_fusion.19), kind=kOutput, calls=%fused_computation.10.clone.1 | convolution fusion | flops 3326451712 | bytes 827392 | tf_op jit(solution)/shard_map/while/body/eval_jaxpr/rhl,bl->rhb/dot_general | solution.py:102
  113.6 4.4 %fusion.100 = f32[12,2048]{1,0:T(8,128)S(1)} fusion(f32[12,88,128]{2,1,0:T(8,128)S(1)} %get-tuple-element.810, pred[88,2048]{1,0:T(8,128)(4,1)S(1)} %iota_compare_fusion.30, s32[2048]{0:T(1024)S(1)} %add_select_fusion.19), kind=kOutput, calls=%fused_computation.10.clone.1 | convolution fusion | flops 3326451712 | bytes 827392 | tf_op jit(solution)/shard_map/while/body/eval_jaxpr/rhl,bl->rhb/dot_general | solution.py:102
  123.8 14.0 %while.97 = (s32[]{:T(128)}, f32[4,1,2048]{2,1,0:T(1,128)S(1)}, s32[4,2048]{1,0:T(4,128)S(1)}, f32[1,512,128]{2,1,0:T(8,128)}, s32[]{:T(128)}) while((s32[]{:T(128)}, f32[4,1,2048]{2,1,0:T(1,128)S(1)}, s32[4,2048]{1,0:T(4,128)S(1)}, f32[1,512,128]{2,1,0:T(8,128)}, s32[]{:T(128)}) %tuple.183), condition=%wide.region_11.12_spmd.clone, body=%wide.region_9.11_spmd.clone.sunk | while | flops 1614071808 | bytes 344133 | solution.py:106
  140.5 3.9 %while.100 = (s32[]{:T(128)}, f32[400]{0:T(512)S(1)}, s32[4,2048]{1,0:T(4,128)S(1)}, f32[4,2048]{1,0:T(4,128)S(1)}, f32[400]{0:T(512)S(1)}, /*index=5*/s32[]{:T(128)}, s32[]{:T(128)}) while((s32[]{:T(128)}, f32[400]{0:T(512)S(1)}, s32[4,2048]{1,0:T(4,128)S(1)}, f32[4,2048]{1,0:T(4,128)S(1)}, f32[400]{0:T(512)S(1)}, ...), condition=%wide.region_18.19_spmd.clone, body=%wide.region_16.18_spmd.clone.sunk | while | flops 4096403 | bytes 57247 | solution.py:162
  145.1 7.8 %all-to-all-start.1 = ((f32[32,2,400]{2,1,0:T(2,128)}), f32[32,2,400]{2,1,0:T(2,128)S(1)}, u32[]{:S(2)}, u32[]{:S(2)}) async-start(f32[32,2,400]{2,1,0:T(2,128)} %broadcast_in_dim.317), calls=%async_computation.1 | async-start | bytes 262144 | tf_op jit(solution)/shard_map/all_to_all | solution.py:28
  153.9 6.7 %all-to-all-done.1 = f32[32,2,400]{2,1,0:T(2,128)S(1)} async-done(((f32[32,2,400]{2,1,0:T(2,128)}), f32[32,2,400]{2,1,0:T(2,128)S(1)}, u32[]{:S(2)}, u32[]{:S(2)}) %all-to-all-start.1) | async-done | bytes 102432 | tf_op jit(solution)/shard_map/all_to_all | solution.py:28
  161.9 8.2 %while.98 = (s32[]{:T(128)}, f32[4,3,2048]{2,0,1:T(4,128)S(1)}, s32[4,2048]{1,0:T(4,128)S(1)}, f32[3,400]{1,0:T(4,128)S(1)}, s32[]{:T(128)}, /*index=5*/s32[]{:T(128)}) while((s32[]{:T(128)}, f32[4,3,2048]{2,0,1:T(4,128)S(1)}, s32[4,2048]{1,0:T(4,128)S(1)}, f32[3,400]{1,0:T(4,128)S(1)}, s32[]{:T(128)}, ...), condition=%wide.region_21.22_spmd.clone, body=%wide.region_19.21_spmd.clone.sunk | while | flops 5728258 | bytes 1790733 | solution.py:174
  170.2 17.6 %while.101 = (s32[]{:T(128)}, f32[512,128]{1,0:T(8,128)S(1)}, s32[4,2048]{1,0:T(4,128)S(1)}, f32[4,2048]{1,0:T(4,128)S(1)}, s32[]{:T(128)}, /*index=5*/s32[]{:T(128)}) while((s32[]{:T(128)}, f32[512,128]{1,0:T(8,128)S(1)}, s32[4,2048]{1,0:T(4,128)S(1)}, f32[4,2048]{1,0:T(4,128)S(1)}, s32[]{:T(128)}, /*index=5*/s32[]{:T(128)}) %tuple.202), condition=%wide.region_25.26_spmd.clone, body=%wide.region_24.25_spmd.clone.sunk | while | flops 1612355584 | bytes 606295 | solution.py:130
  170.3 4.3 %fusion.104 = f32[512,128]{1,0:T(8,128)S(1)} fusion(s32[2048]{0:T(1024)S(1)} %get-tuple-element.795, f32[2048]{0:T(1024)S(1)} %bitcast.177, s32[2048]{0:T(1024)S(1)} %get-tuple-element.796, f32[512,128]{1,0:T(8,128)S(1)} %get-tuple-element.891, pred[]{:T(512)S(6)} %compare.113), kind=kOutput, calls=%fused_computation.57.clone.1 | convolution fusion | flops 1612316672 | bytes 548865 | tf_op jit(solution)/shard_map/while/body/eval_jaxpr/bh,bl->hl/dot_general | solution.py:126
  174.6 4.3 %fusion.104 = f32[512,128]{1,0:T(8,128)S(1)} fusion(s32[2048]{0:T(1024)S(1)} %get-tuple-element.795, f32[2048]{0:T(1024)S(1)} %bitcast.177, s32[2048]{0:T(1024)S(1)} %get-tuple-element.796, f32[512,128]{1,0:T(8,128)S(1)} %get-tuple-element.891, pred[]{:T(512)S(6)} %compare.113), kind=kOutput, calls=%fused_computation.57.clone.1 | convolution fusion | flops 1612316672 | bytes 548865 | tf_op jit(solution)/shard_map/while/body/eval_jaxpr/bh,bl->hl/dot_general | solution.py:126
  179.0 4.3 %fusion.104 = f32[512,128]{1,0:T(8,128)S(1)} fusion(s32[2048]{0:T(1024)S(1)} %get-tuple-element.795, f32[2048]{0:T(1024)S(1)} %bitcast.177, s32[2048]{0:T(1024)S(1)} %get-tuple-element.796, f32[512,128]{1,0:T(8,128)S(1)} %get-tuple-element.891, pred[]{:T(512)S(6)} %compare.113), kind=kOutput, calls=%fused_computation.57.clone.1 | convolution fusion | flops 1612316672 | bytes 548865 | tf_op jit(solution)/shard_map/while/body/eval_jaxpr/bh,bl->hl/dot_general | solution.py:126
  183.4 4.3 %fusion.104 = f32[512,128]{1,0:T(8,128)S(1)} fusion(s32[2048]{0:T(1024)S(1)} %get-tuple-element.795, f32[2048]{0:T(1024)S(1)} %bitcast.177, s32[2048]{0:T(1024)S(1)} %get-tuple-element.796, f32[512,128]{1,0:T(8,128)S(1)} %get-tuple-element.891, pred[]{:T(512)S(6)} %compare.113), kind=kOutput, calls=%fused_computation.57.clone.1 | convolution fusion | flops 1612316672 | bytes 548865 | tf_op jit(solution)/shard_map/while/body/eval_jaxpr/bh,bl->hl/dot_general | solution.py:126
  187.8 12.5 %all_to_all.26 = f32[32,1,2048]{2,1,0:T(1,128)S(1)} all-to-all(f32[32,1,2048]{2,1,0:T(1,128)S(1)} %bitcast.171), channel_id=1, replica_groups=mesh['load'=8,'dom'=32] {'dom'}, dimensions={0} | all-to-all | bytes 524288 | tf_op jit(solution)/shard_map/all_to_all | solution.py:72
  200.5 15.2 %all_to_all.27 = f32[8,1,2048]{2,1,0:T(1,128)S(1)} all-to-all(f32[8,1,2048]{2,1,0:T(1,128)S(1)} %broadcast_in_dim.320), channel_id=1, replica_groups=mesh['load'=8,'dom'=32] {'load'}, dimensions={0} | all-to-all | bytes 131072 | tf_op jit(solution)/shard_map/all_to_all | solution.py:28
  (263 shorter events, 70.0 us)
Async XLA Ops:
  0.6 121.0 %copy-start = (f32[24,24]{1,0:T(8,128)S(1)}, f32[24,24]{1,0:T(8,128)}, u32[]{:S(2)}) copy-start(f32[24,24]{1,0:T(8,128)} %param.32) | copy-start | bytes 6916
  0.6 8.5 %copy-start.3 = (f32[1,6,8192]{2,0,1:T(1,128)S(1)}, f32[1,6,8192]{2,0,1:T(1,128)}, u32[]{:S(2)}) copy-start(f32[1,6,8192]{2,0,1:T(1,128)} %param.24) | copy-start | bytes 589828
  0.7 8.5 %copy-start.2 = (f32[1,6,8192]{2,0,1:T(1,128)S(1)}, f32[1,6,8192]{2,0,1:T(1,128)}, u32[]{:S(2)}) copy-start(f32[1,6,8192]{2,0,1:T(1,128)} %param.25) | copy-start | bytes 589828
  3.7 29.3 %collective-permute-start.3 = (f32[12,512]{1,0:T(8,128)S(1)}, f32[12,512]{1,0:T(8,128)S(1)}, u32[]{:S(2)}, u32[]{:S(2)}) collective-permute-start(f32[12,512]{1,0:T(8,128)S(1)} %select_reduce_fusion.5), channel_id=1, source_target_pairs={{1,0},{2,1},{3,2},{4,3},{5,4},{6,5},{7,6},{8,7},{9,8},{10,9},{11,1... | collective-permute-start | bytes 73736 | tf_op jit(solution)/shard_map/ppermute | solution.py:17
  9.0 24.0 %collective-permute-start.2 = (f32[12,512]{1,0:T(8,128)S(1)}, f32[12,512]{1,0:T(8,128)S(1)}, u32[]{:S(2)}, u32[]{:S(2)}) collective-permute-start(f32[12,512]{1,0:T(8,128)S(1)} %select_reduce_fusion.6), channel_id=1, source_target_pairs={{31,0},{0,1},{1,2},{2,3},{3,4},{4,5},{5,6},{6,7},{7,8},{8,9},{9,10... | collective-permute-start | bytes 73736 | tf_op jit(solution)/shard_map/ppermute | solution.py:17
  9.2 10.9 %copy-start.9 = (f32[2048]{0:T(1024)S(1)}, f32[2048]{0:T(1024)}, u32[]{:S(2)}) copy-start(f32[2048]{0:T(1024)} %param.30) | copy-start | bytes 24580
  10.2 22.8 %collective-permute-start.1 = (f32[12,512]{1,0:T(8,128)S(1)}, f32[12,512]{1,0:T(8,128)S(1)}, u32[]{:S(2)}, u32[]{:S(2)}) collective-permute-start(f32[12,512]{1,0:T(8,128)S(1)} %select_reduce_fusion.7), channel_id=1, source_target_pairs={{30,0},{31,1},{0,2},{1,3},{2,4},{3,5},{4,6},{5,7},{6,8},{7,9},{8,1... | collective-permute-start | bytes 73736 | tf_op jit(solution)/shard_map/ppermute | solution.py:17
  12.1 15.6 %collective-permute-start = (f32[12,512]{1,0:T(8,128)S(1)}, f32[12,512]{1,0:T(8,128)S(1)}, u32[]{:S(2)}, u32[]{:S(2)}) collective-permute-start(f32[12,512]{1,0:T(8,128)S(1)} %select_reduce_fusion.8), channel_id=1, source_target_pairs={{29,0},{30,1},{31,2},{0,3},{1,4},{2,5},{3,6},{4,7},{5,8},{6,9},{7,... | collective-permute-start | bytes 73736 | tf_op jit(solution)/shard_map/ppermute | solution.py:17
  15.2 17.8 %collective-permute-start.4 = (f32[12,512]{1,0:T(8,128)S(1)}, f32[12,512]{1,0:T(8,128)S(1)}, u32[]{:S(2)}, u32[]{:S(2)}) collective-permute-start(f32[12,512]{1,0:T(8,128)S(1)} %select_reduce_fusion.4), channel_id=1, source_target_pairs={{2,0},{3,1},{4,2},{5,3},{6,4},{7,5},{8,6},{9,7},{10,8},{11,9},{12,... | collective-permute-start | bytes 73736 | tf_op jit(solution)/shard_map/ppermute | solution.py:17
  20.9 6.6 %copy-start.4 = (s32[4,8192]{1,0:T(4,128)S(1)}, s32[4,8192]{1,0:T(4,128)}, u32[]{:S(2)}) copy-start(s32[4,8192]{1,0:T(4,128)} %param.27) | copy-start | bytes 393220
  20.9 6.7 %copy-start.6 = (s32[8192]{0:T(1024)S(1)}, s32[8192]{0:T(1024)}, u32[]{:S(2)}) copy-start(s32[8192]{0:T(1024)} %param.29) | copy-start | bytes 98308
  20.9 6.7 %copy-start.7 = (s32[8192]{0:T(1024)S(1)}, s32[8192]{0:T(1024)}, u32[]{:S(2)}) copy-start(s32[8192]{0:T(1024)} %param.28) | copy-start | bytes 98308
  20.9 102.9 %all-to-all-start = ((f32[32,1,2048]{2,1,0:T(1,128)}), f32[32,1,2048]{2,1,0:T(1,128)}, u32[]{:S(2)}, u32[]{:S(2)}) async-start(f32[32,1,2048]{2,1,0:T(1,128)} %broadcast_in_dim.315), calls=%async_computation | async-start | bytes 524288 | tf_op jit(solution)/shard_map/all_to_all | solution.py:28
  27.7 6.4 %collective-permute-start.5 = (f32[12,512]{1,0:T(8,128)S(1)}, f32[12,512]{1,0:T(8,128)S(1)}, u32[]{:S(2)}, u32[]{:S(2)}) collective-permute-start(f32[12,512]{1,0:T(8,128)S(1)} %select_reduce_fusion.3), channel_id=1, source_target_pairs={{3,0},{4,1},{5,2},{6,3},{7,4},{8,5},{9,6},{10,7},{11,8},{12,9},{13... | collective-permute-start | bytes 73736 | tf_op jit(solution)/shard_map/ppermute | solution.py:17
  122.4 0.8 copy-start.10
  123.8 14.1 %copy-start.11 = (f32[8,24]{1,0:T(8,128)S(1)}, f32[8,24]{1,0:T(8,128)}, u32[]{:S(2)}) copy-start(f32[8,24]{1,0:T(8,128)} %param.34) | copy-start | bytes 2308
  140.5 12.4 %copy-start.8 = (f32[24,24]{1,0:T(8,128)S(1)}, f32[24,24]{1,0:T(8,128)}, u32[]{:S(2)}) copy-start(f32[24,24]{1,0:T(8,128)} %param.33) | copy-start | bytes 6916
  145.1 16.7 %copy-start.12 = (f32[1,400]{1,0:T(1,128)S(1)}, f32[1,400]{1,0:T(1,128)}, u32[]{:S(2)}) copy-start(f32[1,400]{1,0:T(1,128)} %param.31) | copy-start | bytes 4804
  145.1 16.7 %copy-start.5 = (f32[4,3,2048]{2,0,1:T(4,128)S(1)}, f32[4,3,2048]{2,0,1:T(4,128)}, u32[]{:S(2)}) copy-start(f32[4,3,2048]{2,0,1:T(4,128)} %custom-call.6) | copy-start | bytes 294916
  145.1 15.5 %all-to-all-start.1 = ((f32[32,2,400]{2,1,0:T(2,128)}), f32[32,2,400]{2,1,0:T(2,128)S(1)}, u32[]{:S(2)}, u32[]{:S(2)}) async-start(f32[32,2,400]{2,1,0:T(2,128)} %broadcast_in_dim.317), calls=%async_computation.1 | async-start | bytes 262144 | tf_op jit(solution)/shard_map/all_to_all | solution.py:28
  161.9 8.3 %copy-start.1 = (f32[512,128]{1,0:T(8,128)S(1)}, f32[512,128]{1,0:T(8,128)}, u32[]{:S(2)}) copy-start(f32[512,128]{1,0:T(8,128)} %custom-call.2) | copy-start | bytes 786436
where the time goes:
time: 217 us; the launch traced here: 216 us
  matrix products  112 us (52%)
  starting transfers between devices  29.5 us (14%)
  blocking collectives  27.7 us (13%)
  local copies, waits for them, and re-layouts  19.2 us (9%)
  other arithmetic  17.1 us (8%)
  waiting for transfers between devices  7.72 us (4%)
    dot_general x26, matrix products, pick_one_block(): jnp.einsum('rhl,bl->rhb', folded, low_hot, precision=lax.Precision.HIGHEST)  92.3 us
    dot_general x4, matrix products, step(): jnp.einsum('bh,bl->hl', high_hot, low_part, precision=lax.Precision.HIGHEST)  17.2 us
    ppermute x6, starting transfers between devices, shifted(): return lax.ppermute(block, axis, route)  16.5 us
    all_to_all x1, blocking collectives, from_everyone(): lax.all_to_all(jnp.broadcast_to(x[None], (count, *x.shape)), axis, 0, 0,...  15.2 us
    all_to_all x2, starting transfers between devices, from_everyone(): lax.all_to_all(jnp.broadcast_to(x[None], (count, *x.shape)), axis, 0, 0,...  13 us
    all_to_all x1, blocking collectives, sent_and_summed(): lax.all_to_all(tiles, axis, split_axis=0, concat_axis=0, tiled=True)  12.5 us
    dynamic_update_slice x20, local copies, waits for them, and re-layouts, pick_columns(): picked = lax.map(pick_one_block, idx_blocks)  10.7 us
    all_to_all x2, waiting for transfers between devices, from_everyone(): lax.all_to_all(jnp.broadcast_to(x[None], (count, *x.shape)), axis, 0, 0,...  6.68 us
  transfers between devices with their start and end apart: 8, of which 2 were waited for; matrix products, arithmetic and copies ran while one was open for 45% of the time, Pallas kernels for 0%

commit v1 on v0

v1 whole, which is shorter than its diff:
```python
import functools

import jax
import jax.numpy as jnp
from jax import lax
from jax.experimental import pallas as pl
from jax.experimental.pallas import tpu as pltpu
from jax.sharding import PartitionSpec as P

NBR = 3
SHARP = 50.0
LOW = -1e30
LANES = 128
DISP_TOP = 8388600.0
ADJ_TOP = 131000.0
ADJ_MID = 131072
OFFSETS = tuple(j - NBR if j < NBR else j - NBR + 1 for j in range(2 * NBR))
I32 = jnp.int32
F32 = jnp.float32


def from_everyone(x, axis):
    count = lax.axis_size(axis)
    return lax.all_to_all(jnp.broadcast_to(x[None], (count, *x.shape)), axis, 0, 0, tiled=True)


def lane_pick(table, index):
    return jnp.take_along_axis(table, index, axis=1, mode="promise_in_bounds")


def row_shifts(rows):
    row = lax.broadcasted_iota(I32, (rows, LANES), 0)
    return (row % 3) * 10


def scales_of(x_of, count, top):
    best = jnp.abs(x_of(0))
    for h in range(1, count):
        best = jnp.maximum(best, jnp.abs(x_of(h)))
    most = jnp.maximum(jnp.max(best, axis=1, keepdims=True), 1e-30)
    return top / most, most / top


def pack_tile(x, y, x_inv, y_inv, store):
    q = jnp.floor(x * x_inv + 0.5).astype(I32)
    u = jnp.floor(y * y_inv + 0.5).astype(I32) + ADJ_MID
    store(0, 6, (q << 8) | (u & 255))
    high = (u >> 8) << row_shifts(6)
    store(6, 1, high[0:1] + high[1:2] + high[2:3])
    store(7, 1, high[3:4] + high[4:5] + high[5:6])


def unpack_tile(word, x_scale, y_scale):
    x = (word >> 8).astype(F32) * x_scale
    row = lax.broadcasted_iota(I32, (8, LANES), 0)
    first = jnp.broadcast_to(word[6:7], (8, LANES))
    second = jnp.broadcast_to(word[7:8], (8, LANES))
    high = (jnp.where(row < 3, first, second) >> row_shifts(8)) & 1023
    y = (((high << 8) | (word & 255)) - ADJ_MID).astype(F32) * y_scale
    return x, y


def pad_rows(column):
    return jnp.concatenate([jnp.broadcast_to(column, (6, LANES)), jnp.zeros((2, LANES), F32)], axis=0)


def pick_pair(table_of, count, first_high, indices, starts):
    lows = [i & 127 for i in indices]
    highs = [(i >> 7) - first_high for i in indices]
    found = list(starts)
    for h in range(count):
        tile = table_of(h)
        for u in range(len(indices)):
            found[u] = jnp.where(highs[u] == h, lane_pick(tile, lows[u]), found[u])
    return found


def send_kernel(here_ref, disp_ref, adj_ref, list_ref, thick_ref, packed_ref, scale_ref, send_ref, *, chunks, domains, iface):
    rows = iface // LANES
    cut = lambda ref, h: ref[:, h * LANES : (h + 1) * LANES]
    x_inv, x_scale = scales_of(lambda h: cut(disp_ref, h), chunks, DISP_TOP)
    y_inv, y_scale = scales_of(lambda h: cut(adj_ref, h), chunks, ADJ_TOP)
    scale_ref[0:8] = jnp.zeros((8, LANES), F32)
    scale_ref[8:16] = jnp.zeros((8, LANES), F32)
    scale_ref[0:6] = jnp.broadcast_to(x_scale, (6, LANES))
    scale_ref[8:14] = jnp.broadcast_to(y_scale, (6, LANES))
    xs = scale_ref[0:8]
    ys = scale_ref[8:16]
    x_inv = jnp.broadcast_to(x_inv, (6, LANES))
    y_inv = jnp.broadcast_to(y_inv, (6, LANES))
    for h in range(chunks):

        def store(row, many, value, h=h):
            packed_ref[h * 8 + row : h * 8 + row + many] = value

        pack_tile(cut(disp_ref, h), cut(adj_ref, h), x_inv, y_inv, store)

    def thickness_rows(k, half):
        return thick_ref[k * 4 + half * 2 : k * 4 + half * 2 + 2]

    @pl.loop(0, domains)
    def _(d):
        for k in range(rows):
            for half in range(2):
                at = k * 16 + half * 8
                send_ref[d, at : at + 6] = jnp.zeros((6, LANES), F32)
                send_ref[d, at + 6 : at + 8] = thickness_rows(k, half)

    here = here_ref[0]
    row_ids = lax.broadcasted_iota(I32, (8, LANES), 0)

    def listed(target, k):
        base = pl.multiple_of(target // 8 * 8, 8)
        tile = list_ref[pl.ds(base, 8), k * LANES : (k + 1) * LANES]
        row = jnp.sum(jnp.where(row_ids == target - base, tile, 0), axis=0, keepdims=True)
        return jnp.broadcast_to(row, (8, LANES))

    for offset in OFFSETS:
        target = lax.rem(here - offset + domains, domains)
        for k in range(0, rows, 2):
            picked = pick_pair(
                lambda h: packed_ref[h * 8 : h * 8 + 8],
                chunks,
                0,
                [listed(target, k + u) for u in range(2)],
                [jnp.zeros((8, LANES), I32)] * 2,
            )
            for u in range(2):
                x, y = unpack_tile(picked[u], xs, ys)
                at = (k + u) * 16
                send_ref[target, at : at + 6] = x[0:6]
                send_ref[target, at + 8 : at + 14] = y[0:6]


def own_kernel(packed_ref, connect_ref, got_ref, *, chunks, groups):
    @pl.loop(0, groups)
    def _(b):
        lanes = pl.ds(pl.multiple_of(b * LANES, LANES), LANES)
        for a in range(0, 4, 2):
            found = pick_pair(
                lambda h: packed_ref[h * 8 : h * 8 + 8],
                chunks,
                0,
                [jnp.broadcast_to(connect_ref[a + u : a + u + 1, lanes], (8, LANES)) for u in range(2)],
                [jnp.zeros((8, LANES), I32)] * 2,
            )
            for u in range(2):
                got_ref[pl.ds(pl.multiple_of(b * 32 + (a + u) * 8, 8), 8)] = found[u]


def spread_matrix(flip):
    shape = (24, 32) if not flip else (32, 24)
    narrow = lax.broadcasted_iota(I32, shape, 1 if flip else 0)
    wide = lax.broadcasted_iota(I32, shape, 0 if flip else 1)
    hit = (narrow // 4 == wide % 8) & (narrow % 4 == wide // 8)
    return jnp.where(hit, 1.0, 0.0).astype(F32)


def dot(a, b):
    return jnp.dot(a, b, precision=lax.Precision.HIGHEST, preferred_element_type=F32)


def main_kernel(
    here_ref,
    recv_ref,
    packed_scale_ref,
    got_ref,
    connect_ref,
    comp_ref,
    dv_ref,
    s_memb_ref,
    s_bend_ref,
    k_memb_ref,
    k_bend_ref,
    stats_ref,
    slope_ref,
    fixed_ref,
    ghost_ref,
    move_ref,
    cost_ref,
    panel_ref,
    fail_ref,
    *,
    own,
    groups,
    domains,
    iface,
    comps,
):
    rows = iface // LANES
    ghosts = len(OFFSETS) * rows
    here = here_ref[0]
    sources = [lax.rem(here + offset + domains, domains) for offset in OFFSETS]

    def x_of(h):
        return recv_ref[sources[h // rows], (h % rows) * 16 : (h % rows) * 16 + 6]

    def y_of(h):
        return recv_ref[sources[h // rows], (h % rows) * 16 + 8 : (h % rows) * 16 + 14]

    x_inv, x_scale = scales_of(x_of, ghosts, DISP_TOP)
    y_inv, y_scale = scales_of(y_of, ghosts, ADJ_TOP)
    gx = pad_rows(x_scale)
    gy = pad_rows(y_scale)
    x_inv = jnp.broadcast_to(x_inv, (6, LANES))
    y_inv = jnp.broadcast_to(y_inv, (6, LANES))
    for h in range(ghosts):

        def store(row, many, value, h=h):
            ghost_ref[h * 8 + row : h * 8 + row + many] = value

        pack_tile(x_of(h), y_of(h), x_inv, y_inv, store)
    ox = packed_scale_ref[0:8]
    oy = packed_scale_ref[8:16]

    @pl.loop(0, groups)
    def _(b):
        lanes = pl.ds(pl.multiple_of(b * LANES, LANES), LANES)
        for a in range(0, 4, 2):
            indices = [jnp.broadcast_to(connect_ref[a + u : a + u + 1, lanes], (8, LANES)) for u in range(2)]
            found = pick_pair(
                lambda h: ghost_ref[h * 8 : h * 8 + 8],
                ghosts,
                own,
                indices,
                [got_ref[pl.ds(pl.multiple_of(b * 32 + (a + u) * 8, 8), 8)] for u in range(2)],
            )
            for u in range(2):
                far = indices[u] >= own * LANES
                x, y = unpack_tile(found[u], jnp.where(far, gx, ox), jnp.where(far, gy, oy))
                move_ref[(a + u) * 8 : (a + u) * 8 + 8, lanes] = x
                cost_ref[(a + u) * 8 : (a + u) * 8 + 8, lanes] = y

    tiles = groups // 8
    panel_ref[...] = jnp.zeros(panel_ref.shape, F32)

    @pl.loop(0, domains)
    def _(s):
        for t in range(0, tiles, 2):
            indices = [dv_ref[(t + u) * 8 : (t + u) * 8 + 8] for u in range(2)]
            lows = [i & 127 for i in indices]
            highs = [(i >> 7) - s * 16 for i in indices]
            found = [panel_ref[(t + u) * 8 : (t + u) * 8 + 8] for u in range(2)]
            for h in range(16):
                row = (h // 4) * 16 + (h % 4 // 2) * 8 + 6 + h % 2
                tile = jnp.broadcast_to(recv_ref[s, row : row + 1], (8, LANES))
                for u in range(2):
                    found[u] = jnp.where(highs[u] == h, lane_pick(tile, lows[u]), found[u])
            for u in range(2):
                panel_ref[(t + u) * 8 : (t + u) * 8 + 8] = found[u]

    wide = spread_matrix(False)
    tall = spread_matrix(True)
    weights = jnp.concatenate(
        [
            dot(s_memb_ref[...], wide),
            dot(s_bend_ref[...], wide),
            dot(tall, dot(k_memb_ref[...], wide)),
            dot(tall, dot(k_bend_ref[...], wide)),
        ],
        axis=0,
    )

    @pl.loop(0, tiles)
    def _(t):
        lanes = pl.ds(pl.multiple_of(t * 8 * LANES, 8 * LANES), 8 * LANES)
        all_parts = dot(weights, move_ref[:, lanes])
        cost = cost_ref[:, lanes]
        for j in range(8):
            part = all_parts[:, j * LANES : (j + 1) * LANES]
            panel = panel_ref[pl.ds(t * 8 + j, 1)]
            bending = part[8:16]
            stress = part[0:8] + panel * bending
            failure = jnp.sum(stress * stress, axis=0, keepdims=True) / 8.0
            slope = jnp.sum(stress * bending, axis=0, keepdims=True) * (2.0 / 8.0)
            stiff = part[16:48] + (3.0 * panel * panel) * part[48:80]
            implicit = jnp.sum(cost[:, j * LANES : (j + 1) * LANES] * stiff, axis=0, keepdims=True)
            fail_ref[pl.ds(t * 8 + j, 1)] = failure
            slope_ref[pl.ds(t * 8 + j, 1)] = slope
            fixed_ref[pl.ds(t * 8 + j, 1)] = implicit

    stats_ref[0] = jnp.zeros((8, LANES), F32)
    names = lax.broadcasted_iota(I32, (LANES, LANES), 0)
    bands = (comps + LANES - 1) // LANES
    diagonal = lax.broadcasted_iota(I32, (LANES, LANES), 0) == lax.broadcasted_iota(I32, (LANES, LANES), 1)

    def to_row(column):
        return jnp.sum(jnp.where(diagonal, column, 0.0), axis=0, keepdims=True)

    for band in range(bands):

        def peak_step(g, best):
            hit = comp_ref[pl.ds(g, 1)] == names + band * LANES
            return jnp.maximum(best, jnp.where(hit, fail_ref[pl.ds(g, 1)], LOW))

        best = lax.fori_loop(0, groups, peak_step, jnp.full((LANES, LANES), LOW, F32))
        stats_ref[0, band : band + 1] = to_row(jnp.max(best, axis=1, keepdims=True))

    for t in range(tiles):
        block = slice(t * 8, t * 8 + 8)
        comp = comp_ref[block]
        low = comp & 127
        high = comp >> 7
        top = jnp.zeros((8, LANES), F32)
        for band in range(bands):
            tile = jnp.broadcast_to(stats_ref[0, band : band + 1], (8, LANES))
            top = jnp.where(high == band, lane_pick(tile, low), top)
        scaled = jnp.exp(SHARP * (fail_ref[block] - top))
        fail_ref[block] = scaled
        slope_ref[block] = slope_ref[block] * scaled

    for band in range(bands):

        def total_step(g, total):
            hit = comp_ref[pl.ds(g, 1)] == names + band * LANES
            return total + jnp.where(hit, fail_ref[pl.ds(g, 1)], 0.0)

        total = lax.fori_loop(0, groups, total_step, jnp.zeros((LANES, LANES), F32))
        stats_ref[0, 4 + band : 5 + band] = to_row(jnp.sum(total, axis=1, keepdims=True))
    mine = stats_ref[0]
    for d in range(1, domains):
        stats_ref[d] = mine


def last_kernel(
    here_ref, stats_ref, mult_ref, comp_ref, dv_ref, slope_ref, fixed_ref, ks_ref, sum_ref, term_ref, *, domains, comps, groups, slots
):
    here = here_ref[0]
    peak = stats_ref[0, 0:4]
    for s in range(1, domains):
        peak = jnp.maximum(peak, stats_ref[s, 0:4])
    total = jnp.zeros_like(peak)
    for s in range(domains):
        total = total + stats_ref[s, 4:8] * jnp.exp(SHARP * (stats_ref[s, 0:4] - peak))
    ks = peak + jnp.log(total) / SHARP
    share = jnp.exp(SHARP * (stats_ref[here, 0:4] - peak)) / total
    bands = (comps + LANES - 1) // LANES
    weights = []
    for band in range(bands):
        many = min(LANES, comps - band * LANES)
        ks_ref[0:1, band * LANES : band * LANES + many] = ks[band : band + 1, 0:many]
        weights.append(jnp.broadcast_to(share[band : band + 1] * mult_ref[band : band + 1], (8, LANES)))
    tiles = groups // 8
    for t in range(tiles):
        block = slice(t * 8, t * 8 + 8)
        comp = comp_ref[block]
        low = comp & 127
        high = comp >> 7
        weight = jnp.zeros((8, LANES), F32)
        for band in range(bands):
            weight = jnp.where(high == band, lane_pick(weights[band], low), weight)
        term_ref[block] = weight * slope_ref[block] + fixed_ref[block]
    sum_ref[...] = jnp.zeros(sum_ref.shape, F32)
    outer = slots // LANES
    outer_ids = lax.broadcasted_iota(I32, (outer, LANES), 0)
    inner_ids = lax.broadcasted_iota(I32, (LANES, LANES), 0)
    zero = jnp.zeros((), F32)

    @pl.loop(0, tiles)
    def _(t):
        highs = []
        lows = []
        for j in range(8):
            place = dv_ref[pl.ds(t * 8 + j, 1)]
            value = term_ref[pl.ds(t * 8 + j, 1)]
            highs.append(jnp.where(outer_ids == (place >> 7), 1.0, zero).astype(jnp.bfloat16))
            rough = value.astype(jnp.bfloat16).astype(F32)
            fine = value - rough
            hit = inner_ids == (place & 127)
            lows.append(
                jnp.concatenate(
                    [
                        jnp.where(hit, rough, 0.0).astype(jnp.bfloat16),
                        jnp.where(hit, fine, 0.0).astype(jnp.bfloat16),
                    ],
                    axis=0,
                )
            )
        both = lax.dot_general(
            jnp.concatenate(highs, axis=1),
            jnp.concatenate(lows, axis=1),
            (((1,), (1,)), ((), ())),
            preferred_element_type=F32,
        )
        sum_ref[...] += both[:, 0:LANES] + both[:, LANES : 2 * LANES]


def vmem():
    return pl.BlockSpec(memory_space=pltpu.VMEM)


def smem():
    return pl.BlockSpec(memory_space=pltpu.SMEM)


def per_device(
    displacement, adjoint, send_list, connect, elem_comp, elem_dv, thickness, multiplier, k_memb, k_bend, s_memb, s_bend
):
    domains = lax.axis_size("dom")
    here = lax.axis_index("dom").astype(I32).reshape(1)
    comps = multiplier.shape[1]
    nodes = displacement.shape[2]
    elems = connect.shape[1]
    iface = send_list.shape[2]
    own = nodes // LANES
    groups = elems // LANES
    slots = thickness.shape[0] * domains
    block = 4 * iface // LANES * 4
    sds = jax.ShapeDtypeStruct

    packed, scale, send = pl.pallas_call(
        functools.partial(send_kernel, chunks=own, domains=domains, iface=iface),
        out_shape=(sds((own * 8, LANES), I32), sds((16, LANES), F32), sds((domains, block, LANES), F32)),
        in_specs=[smem()] + [vmem()] * 4,
        out_specs=(vmem(),) * 3,
        name="send_pick",
    )(here, displacement[0], adjoint[0], send_list[0], thickness.reshape(-1, LANES))
    recv = lax.all_to_all(send, "dom", 0, 0, tiled=True)
    got = pl.pallas_call(
        functools.partial(own_kernel, chunks=own, groups=groups),
        out_shape=sds((groups * 32, LANES), I32),
        in_specs=[vmem()] * 2,
        out_specs=vmem(),
        name="own_pick",
        cost_estimate=pl.CostEstimate(flops=0, transcendentals=0, bytes_accessed=60_000_000),
    )(packed, connect)
    comp = elem_comp.reshape(-1, LANES)
    dv = elem_dv.reshape(-1, LANES)
    stats, slope, fixed = pl.pallas_call(
        functools.partial(main_kernel, own=own, groups=groups, domains=domains, iface=iface, comps=comps),
        out_shape=(sds((domains, 8, LANES), F32), sds((groups, LANES), F32), sds((groups, LANES), F32)),
        in_specs=[smem()] + [vmem()] * 10,
        out_specs=(vmem(),) * 3,
        scratch_shapes=[
            pltpu.VMEM((len(OFFSETS) * iface // LANES * 8, LANES), I32),
            pltpu.VMEM((32, elems), F32),
            pltpu.VMEM((32, elems), F32),
            pltpu.VMEM((groups, LANES), F32),
            pltpu.VMEM((groups, LANES), F32),
        ],
        name="element_work",
    )(here, recv, scale, got, connect, comp, dv, s_memb, s_bend, k_memb, k_bend)
    everyone = lax.all_to_all(stats, "dom", 0, 0, tiled=True)
    mult = jnp.pad(multiplier[0], (0, 4 * LANES - comps)).reshape(4, LANES)
    ks_value, sums = pl.pallas_call(
        functools.partial(last_kernel, domains=domains, comps=comps, groups=groups, slots=slots),
        out_shape=(sds((1, comps), F32), sds((slots // LANES, LANES), F32)),
        in_specs=[smem()] + [vmem()] * 6,
        out_specs=(vmem(),) * 2,
        scratch_shapes=[pltpu.VMEM((groups, LANES), F32)],
        name="weigh_and_sum",
    )(here, everyone, mult, comp, dv, slope, fixed)
    arrived = lax.all_to_all(sums.reshape(domains, -1, LANES), "dom", 0, 0, tiled=True)
    owned = arrived.sum(axis=0)
    sensitivity = from_everyone(owned, "load").sum(axis=0).reshape(-1)
    return ks_value, sensitivity


def solution(mesh):
    in_specs = (
        P("load", None, "dom"),
        P("load", None, "dom"),
        P("dom", None, None),
        P(None, "dom"),
        P("dom"),
        P("dom"),
        P("dom"),
        P("load", None),
        P(),
        P(),
        P(),
        P(),
    )
    return jax.shard_map(
        per_device, mesh=mesh, in_specs=in_specs, out_specs=(P("load", None), P("dom")), check_vma=False
    )
```

time: 217 us -> 141 us (0.65)
  matrix products: 112 us -> 0 us
  Pallas kernels: 0 us -> 83.3 us
  other arithmetic: 17.1 us -> 0.64 us
  local copies, waits for them, and re-layouts: 19.2 us -> 4.3 us
  starting transfers between devices: 29.5 us -> 16.1 us
    dot_general x34 -> x0, matrix products: 112 us -> none  [the longest x26 92.3 us: pick_one_block(): jnp.einsum('rhl,bl->rhb', folded, low_hot, precision=lax.Precision.HIGHEST)]
    pallas_call x0 -> x4, Pallas kernels: none -> 83.3 us  [the longest x1 38.6 us: per_device(): pl.pallas_call(functools.partial(main_kernel, own=own, groups=groups, dom...]
    ppermute x6 -> x0, starting transfers between devices: 16.5 us -> none  [shifted(): return lax.ppermute(block, axis, route)]
    dynamic_update_slice x28 -> x0, local copies, waits for them, and re-layouts: 11.7 us -> none  [the longest x20 10.7 us: pick_columns(): picked = lax.map(pick_one_block, idx_blocks)]
    reduce_sum x10 -> x2, other arithmetic: 9.54 us -> 0.64 us  [the longest x1 0.61 us: per_device(): sensitivity = from_everyone(owned, 'load').sum(axis=0).reshape(-1)]
    eq x26 -> x0, other arithmetic: 3.68 us -> none  [the longest x4 1.91 us: component_one_block(): hit = block_labels[:, None] == idents[None, :]]
    slice x20 -> x0, local copies, waits for them, and re-layouts: 3.41 us -> none  [the longest x2 2.5 us: per_device(): costate = local[1]]
    unnamed x35 -> x7, local copies, waits for them, and re-layouts: 0.49 us -> 3.72 us
  transfers between devices with their start and end apart: 8 -> 2, of which waited for: 2 -> 1; matrix products, arithmetic and copies ran while one was open for 45% -> 0% of each run, Pallas kernels for 0% -> 23%
where the time goes in v1:
time: 141 us; the launch traced here: 140 us
  Pallas kernels  83.3 us (59%)
  blocking collectives  28.1 us (20%)
  starting transfers between devices  16.1 us (11%)
  waiting for transfers between devices  7.09 us (5%)
  local copies, waits for them, and re-layouts  4.3 us (3%)
    pallas_call x1, Pallas kernels, per_device(): pl.pallas_call(functools.partial(main_kernel, own=own, groups=groups, dom...  38.6 us
    pallas_call x1, Pallas kernels, per_device(): pl.pallas_call(functools.partial(own_kernel, chunks=own, groups=groups),...  32.8 us
    all_to_all x1, blocking collectives, from_everyone(): lax.all_to_all(jnp.broadcast_to(x[None], (count, *x.shape)), axis, 0, 0,...  15.1 us
    all_to_all x1, blocking collectives, per_device(): lax.all_to_all(sums.reshape(domains, -1, LANES), 'dom', 0, 0, tiled=True)  13 us
    all_to_all x1, starting transfers between devices, per_device(): recv = lax.all_to_all(send, 'dom', 0, 0, tiled=True)  8.58 us
    all_to_all x1, starting transfers between devices, per_device(): everyone = lax.all_to_all(stats, 'dom', 0, 0, tiled=True)  7.51 us
    all_to_all x1, waiting for transfers between devices, per_device(): everyone = lax.all_to_all(stats, 'dom', 0, 0, tiled=True)  7.08 us
    pallas_call x1, Pallas kernels, per_device(): pl.pallas_call(functools.partial(last_kernel, domains=domains, comps=comp...  5.98 us
  transfers between devices with their start and end apart: 2, of which 1 were waited for; matrix products, arithmetic and copies ran while one was open for 0% of the time, Pallas kernels for 23%

profile of v1, /device:TPU:1, one launch (start us, length us, event | category | flops | bytes accessed | tf_op | source)
XLA Modules:
  0.0 140.2 jit_solution(15845451224005629559)
XLA Ops:
  0.6 2.0 %copy_bitcast_fusion = (f32[6,8192]{1,0:T(8,128)}, f32[6,8192]{1,0:T(8,128)}) fusion(f32[1,6,8192]{2,0,1:T(1,128)} %param.13, f32[1,6,8192]{2,0,1:T(1,128)} %param.12), kind=kLoop, calls=%fused_computation | loop fusion | bytes 786432
  2.7 5.8 %send_pick.1 = (s32[512,128]{1,0:T(8,128)}, f32[16,128]{1,0:T(8,128)}, f32[32,64,128]{2,1,0:T(8,128)}) custom-call(s32[1]{0:T(128)} %bitcast.here_ref, f32[6,8192]{1,0:T(8,128)} %get-tuple-element.19.disp_ref, f32[6,8192]{1,0:T(8,128)} %get-tuple-element.18.adj_ref, s32[32,512]{1,0:T(8,128)} %bitcast.19, f32[16,128]{1,0:T(8,128)} %bitcast.20), custom_call_target="tpu_custom_call" | custom-call | tf_op jit(solution)/shard_map/send_pick/pallas_call | solution.py:411
  8.5 8.6 %all-to-all-start = ((f32[32,64,128]{2,1,0:T(8,128)}), f32[32,64,128]{2,1,0:T(8,128)S(1)}, u32[]{:S(2)}, u32[]{:S(2)}) async-start(f32[32,64,128]{2,1,0:T(8,128)} %get-tuple-element.10), calls=%async_computation | async-start | bytes 2097152 | tf_op jit(solution)/shard_map/all_to_all | solution.py:418
  17.1 32.8 %own_pick.1.got_ref = s32[2048,128]{1,0:T(8,128)} custom-call(s32[512,128]{1,0:T(8,128)} %get-tuple-element.12.packed_ref, s32[4,8192]{1,0:T(4,128)} %connect_ref.3), custom_call_target="tpu_custom_call" | custom-call | bytes 60000000 | tf_op jit(solution)/shard_map/own_pick/pallas_call | solution.py:419
  49.9 0.0 all-to-all-done.recv_ref
  49.9 0.0 copy-start
  49.9 1.0 copy-done
  50.9 38.6 %element_work.1 = (f32[32,8,128]{2,1,0:T(8,128)}, f32[64,128]{1,0:T(8,128)}, f32[64,128]{1,0:T(8,128)}) custom-call(s32[1]{0:T(128)} %bitcast.here_ref, f32[32,64,128]{2,1,0:T(8,128)} %copy-done, f32[16,128]{1,0:T(8,128)} %get-tuple-element.11.packed_scale_ref, s32[2048,128]{1,0:T(8,128)} %own_pick.1.got_ref, s32[4,8192]{1,0:T(4,128)} %connect_ref.3, ...), custom_call_target="tpu_custom_call" | custom-call | tf_op jit(solution)/shard_map/element_work/pallas_call | solution.py:429
  89.6 0.0 copy-start.2
  89.6 7.5 %all-to-all-start.1 = ((f32[32,8,128]{2,1,0:T(8,128)}), f32[32,8,128]{2,1,0:T(8,128)S(1)}, u32[]{:S(2)}, u32[]{:S(2)}) async-start(f32[32,8,128]{2,1,0:T(8,128)} %get-tuple-element.13), calls=%async_computation.1 | async-start | bytes 262144 | tf_op jit(solution)/shard_map/all_to_all | solution.py:443
  97.1 0.0 copy-done.2
  97.1 0.6 pad_bitcast_fusion.mult_ref
  97.7 7.1 %all-to-all-done.1.stats_ref = f32[32,8,128]{2,1,0:T(8,128)S(1)} async-done(((f32[32,8,128]{2,1,0:T(8,128)}), f32[32,8,128]{2,1,0:T(8,128)S(1)}, u32[]{:S(2)}, u32[]{:S(2)}) %all-to-all-start.1) | async-done | bytes 131104 | tf_op jit(solution)/shard_map/all_to_all | solution.py:443
  104.8 0.0 copy-start.1
  104.8 0.6 copy-done.1
  105.4 6.0 %weigh_and_sum.1 = (f32[1,400]{1,0:T(1,128)}, f32[512,128]{1,0:T(8,128)}) custom-call(s32[1]{0:T(128)} %bitcast.here_ref, f32[32,8,128]{2,1,0:T(8,128)} %copy-done.1, f32[4,128]{1,0:T(4,128)} %pad_bitcast_fusion.mult_ref, s32[64,128]{1,0:T(8,128)} %bitcast.16, s32[64,128]{1,0:T(8,128)} %bitcast.18, f32[64,128]{1,0:T(8,128)} %get-tuple-element.14.slope_ref, ...), custom_call_target="tpu_custom_call" | custom-call | tf_op jit(solution)/shard_map/weigh_and_sum/pallas_call | solution.py:445
  111.4 13.0 %all_to_all.20 = f32[32,16,128]{2,1,0:T(8,128)S(1)} all-to-all(f32[32,16,128]{2,1,0:T(8,128)} %bitcast.14), channel_id=1, replica_groups=mesh['load'=8,'dom'=32] {'dom'}, dimensions={0} | all-to-all | bytes 524288 | tf_op jit(solution)/shard_map/all_to_all | solution.py:453
  124.5 15.1 %all_to_all.21 = f32[8,16,128]{2,1,0:T(8,128)S(1)} all-to-all(f32[8,16,128]{2,1,0:T(8,128)S(1)} %broadcast_in_dim.2), channel_id=1, replica_groups=mesh['load'=8,'dom'=32] {'load'}, dimensions={0} | all-to-all | bytes 131072 | tf_op jit(solution)/shard_map/all_to_all | solution.py:24
  139.6 0.6 reduce_sum.19
  (2 shorter events, 0.0 us)
Async XLA Ops:
  8.5 41.4 %all-to-all-start = ((f32[32,64,128]{2,1,0:T(8,128)}), f32[32,64,128]{2,1,0:T(8,128)S(1)}, u32[]{:S(2)}, u32[]{:S(2)}) async-start(f32[32,64,128]{2,1,0:T(8,128)} %get-tuple-element.10), calls=%async_computation | async-start | bytes 2097152 | tf_op jit(solution)/shard_map/all_to_all | solution.py:418
  49.9 1.0 copy-start
  89.6 7.5 %copy-start.2 = (f32[1,400]{1,0:T(1,128)S(1)}, f32[1,400]{1,0:T(1,128)}, u32[]{:S(2)}) copy-start(f32[1,400]{1,0:T(1,128)} %param.19) | copy-start | bytes 4804
  89.6 15.2 %all-to-all-start.1 = ((f32[32,8,128]{2,1,0:T(8,128)}), f32[32,8,128]{2,1,0:T(8,128)S(1)}, u32[]{:S(2)}, u32[]{:S(2)}) async-start(f32[32,8,128]{2,1,0:T(8,128)} %get-tuple-element.13), calls=%async_computation.1 | async-start | bytes 262144 | tf_op jit(solution)/shard_map/all_to_all | solution.py:443
  104.8 0.6 copy-start.1

commit v2 on v1

v2 whole, which is shorter than its diff:
```python
import functools

import jax
import jax.numpy as jnp
from jax import lax
from jax.experimental import pallas as pl
from jax.experimental.pallas import tpu as pltpu
from jax.sharding import PartitionSpec as P

NBR = 3
ROWS = 24
HIGHS = 14
SHARP = 50.0
LOW = -1e30
LANES = 128
DISP_TOP = 8388600.0
ADJ_TOP = 131000.0
ADJ_MID = 131072
OFFSETS = tuple(j - NBR if j < NBR else j - NBR + 1 for j in range(2 * NBR))
I32 = jnp.int32
F32 = jnp.float32
BF16 = jnp.bfloat16


def from_everyone(x, axis):
    count = lax.axis_size(axis)
    return lax.all_to_all(jnp.broadcast_to(x[None], (count, *x.shape)), axis, 0, 0, tiled=True)


def lane_pick(table, index):
    return jnp.take_along_axis(table, index, axis=1, mode="promise_in_bounds")


def row_shifts(rows):
    row = lax.broadcasted_iota(I32, (rows, LANES), 0)
    return (row % 3) * 10


def scales_of(x_of, count, top):
    best = jnp.abs(x_of(0))
    for h in range(1, count):
        best = jnp.maximum(best, jnp.abs(x_of(h)))
    most = jnp.maximum(jnp.max(best, axis=1, keepdims=True), 1e-30)
    return top / most, most / top


def pack_tile(x, y, x_inv, y_inv, store):
    q = jnp.floor(x * x_inv + 0.5).astype(I32)
    u = jnp.floor(y * y_inv + 0.5).astype(I32) + ADJ_MID
    store(0, 6, (q << 8) | (u & 255))
    high = (u >> 8) << row_shifts(6)
    store(6, 1, high[0:1] + high[1:2] + high[2:3])
    store(7, 1, high[3:4] + high[4:5] + high[5:6])


def unpack_tile(word, x_scale, y_scale):
    x = (word >> 8).astype(F32) * x_scale
    row = lax.broadcasted_iota(I32, (8, LANES), 0)
    first = jnp.broadcast_to(word[6:7], (8, LANES))
    second = jnp.broadcast_to(word[7:8], (8, LANES))
    high = (jnp.where(row < 3, first, second) >> row_shifts(8)) & 1023
    y = (((high << 8) | (word & 255)) - ADJ_MID).astype(F32) * y_scale
    return x, y


def pad_rows(column):
    return jnp.concatenate([jnp.broadcast_to(column, (6, LANES)), jnp.zeros((2, LANES), F32)], axis=0)


def pick(table_of, count, first_high, indices, starts, by_index):
    lows = [i & 127 for i in indices]
    highs = [(i >> 7) - first_high for i in indices]
    found = list(starts)
    steps = [(u, h) for h in range(count) for u in range(len(indices))]
    if by_index:
        steps = [(u, h) for u in range(len(indices)) for h in range(count)]
    for u, h in steps:
        found[u] = jnp.where(highs[u] == h, lane_pick(table_of(h), lows[u]), found[u])
    return found


def send_kernel(here_ref, disp_ref, adj_ref, list_ref, thick_ref, packed_ref, scale_ref, send_ref, *, chunks, domains, iface):
    rows = iface // LANES
    cut = lambda ref, h: ref[pl.ds(h, 6, stride=chunks)]
    x_inv, x_scale = scales_of(lambda h: cut(disp_ref, h), chunks, DISP_TOP)
    y_inv, y_scale = scales_of(lambda h: cut(adj_ref, h), chunks, ADJ_TOP)
    scale_ref[0:8] = pad_rows(x_scale)
    scale_ref[8:16] = pad_rows(y_scale)
    xs = scale_ref[0:8]
    ys = scale_ref[8:16]
    x_inv = jnp.broadcast_to(x_inv, (6, LANES))
    y_inv = jnp.broadcast_to(y_inv, (6, LANES))
    for h in range(chunks):

        def store(row, many, value, h=h):
            packed_ref[h * 8 + row : h * 8 + row + many] = value

        pack_tile(cut(disp_ref, h), cut(adj_ref, h), x_inv, y_inv, store)

    def thickness_rows(k, half):
        return thick_ref[k * 4 + half * 2 : k * 4 + half * 2 + 2]

    @pl.loop(0, domains)
    def _(d):
        for k in range(rows):
            for half in range(2):
                at = k * 16 + half * 8
                send_ref[d, at : at + 6] = jnp.zeros((6, LANES), F32)
                send_ref[d, at + 6 : at + 8] = thickness_rows(k, half)

    here = here_ref[0]
    row_ids = lax.broadcasted_iota(I32, (8, LANES), 0)
    turns = len(OFFSETS) * rows // 2

    def target_of(turn):
        j = turn // (rows // 2)
        offset = j - NBR + jnp.where(j >= NBR, 1, 0)
        return lax.rem(here - offset + domains, domains)

    def fetch(turn):
        target = target_of(turn)
        base = pl.multiple_of(target // 8 * 8, 8)
        found = []
        for u in range(2):
            k = lax.rem(turn, rows // 2) * 2 + u
            tile = list_ref[0, pl.ds(base, 8), pl.ds(pl.multiple_of(k * LANES, LANES), LANES)]
            row = jnp.sum(jnp.where(row_ids == target - base, tile, 0), axis=0, keepdims=True)
            found.append(jnp.broadcast_to(row, (8, LANES)))
        return tuple(found)

    def body(turn, indices):
        target = target_of(turn)
        picked = pick(
            lambda h: packed_ref[h * 8 : h * 8 + 8], chunks, 0, indices, [jnp.zeros((8, LANES), I32)] * 2, False
        )
        for u in range(2):
            k = lax.rem(turn, rows // 2) * 2 + u
            for half, value in enumerate(unpack_tile(picked[u], xs, ys)):
                at = pl.ds(pl.multiple_of(k * 16 + half * 8, 8), 8)
                send_ref[target, at] = jnp.where(row_ids < 6, value, send_ref[target, at])
        return fetch(jnp.minimum(turn + 1, turns - 1))

    lax.fori_loop(0, turns, body, fetch(jnp.int32(0)))


def own_kernel(
    packed_ref, disp_ref, adj_ref, connect_ref, got_ref, near_x_ref, near_y_ref, wide_ref, table_ref, *, chunks, groups, highs
):
    for high in range(highs):
        for half in range(2):
            lanes = slice(half * LANES, half * LANES + LANES)
            x = disp_ref[pl.ds(high * 2 + half, 6, stride=chunks)]
            y = adj_ref[pl.ds(high * 2 + half, 6, stride=chunks)]
            xh = x.astype(BF16).astype(F32)
            yh = y.astype(BF16).astype(F32)
            xl = x - xh
            yl = y - yh
            pieces = (xh, yh[0:2], yl[4:6], yh[2:6], yl[2:4], xl, yl[0:2])
            at = high * ROWS
            for piece in pieces:
                wide_ref[at : at + piece.shape[0], lanes] = piece
                at += piece.shape[0]
    table_ref[...] = wide_ref[...].astype(BF16)
    row_ids = lax.broadcasted_iota(I32, (8, LANES), 0)
    names = lax.broadcasted_iota(I32, (256, LANES), 0).astype(F32).astype(BF16)
    one = jnp.ones((256, LANES), BF16)
    none = jnp.zeros((256, LANES), BF16)

    def one_hot(index):
        tile = jnp.broadcast_to((index[0:1] & 255).astype(F32), (16, LANES)).astype(BF16)
        return jnp.where(names == jnp.concatenate([tile] * 16, axis=0), one, none)

    def fetch(b):
        rows = connect_ref[:, pl.ds(pl.multiple_of(b * LANES, LANES), LANES)]
        return tuple(jnp.broadcast_to(rows[a : a + 1], (8, LANES)) for a in range(4))

    def body(b, indices):
        hot = jnp.concatenate([one_hot(i) for i in indices], axis=1)
        every = jnp.dot(table_ref[...], hot, preferred_element_type=F32)
        for a in range(4):
            held = [jnp.zeros((8, LANES), F32)] * 3
            for high in range(highs):
                hit = (indices[a] >> 8) == high
                for v in range(3):
                    at = high * ROWS + v * 8
                    held[v] = jnp.where(hit, every[at : at + 8, a * LANES : (a + 1) * LANES], held[v])
            first = held[0] + held[2]
            second = held[1] + jnp.roll(held[1], 4, axis=0)
            at = pl.ds(pl.multiple_of(b * 32 + a * 8, 8), 8)
            near_x_ref[at] = first
            near_y_ref[at] = jnp.where(row_ids < 2, jnp.roll(first, 2, axis=0), second)
        found = pick(
            lambda h: packed_ref[(2 * highs + h) * 8 : (2 * highs + h) * 8 + 8],
            chunks - 2 * highs,
            2 * highs,
            indices,
            [jnp.zeros((8, LANES), I32)] * 4,
            True,
        )
        for a in range(4):
            got_ref[pl.ds(pl.multiple_of(b * 32 + a * 8, 8), 8)] = found[a]
        return fetch(jnp.minimum(b + 1, groups - 1))

    lax.fori_loop(0, groups, body, fetch(jnp.int32(0)))


def spread_matrix(flip):
    shape = (24, 32) if not flip else (32, 24)
    narrow = lax.broadcasted_iota(I32, shape, 1 if flip else 0)
    wide = lax.broadcasted_iota(I32, shape, 0 if flip else 1)
    hit = (narrow // 4 == wide % 8) & (narrow % 4 == wide // 8)
    return jnp.where(hit, 1.0, 0.0).astype(F32)


def three_parts(x):
    parts = []
    for _ in range(3):
        part = x.astype(BF16)
        parts.append(part)
        x = x - part.astype(F32)
    return parts


def dot(a, b):
    return jnp.dot(a, b, precision=lax.Precision.HIGHEST, preferred_element_type=F32)


def main_kernel(
    here_ref,
    recv_ref,
    packed_scale_ref,
    got_ref,
    near_x_ref,
    near_y_ref,
    connect_ref,
    comp_ref,
    dv_ref,
    s_memb_ref,
    s_bend_ref,
    k_memb_ref,
    k_bend_ref,
    stats_ref,
    slope_ref,
    fixed_ref,
    ghost_ref,
    move_ref,
    cost_ref,
    panel_ref,
    fail_ref,
    best_ref,
    *,
    own,
    groups,
    domains,
    iface,
    comps,
    highs,
):
    rows = iface // LANES
    ghosts = len(OFFSETS) * rows
    here = here_ref[0]
    sources = [lax.rem(here + offset + domains, domains) for offset in OFFSETS]

    def x_of(h):
        return recv_ref[sources[h // rows], (h % rows) * 16 : (h % rows) * 16 + 6]

    def y_of(h):
        return recv_ref[sources[h // rows], (h % rows) * 16 + 8 : (h % rows) * 16 + 14]

    x_inv, x_scale = scales_of(x_of, ghosts, DISP_TOP)
    y_inv, y_scale = scales_of(y_of, ghosts, ADJ_TOP)
    gx = pad_rows(x_scale)
    gy = pad_rows(y_scale)
    x_inv = jnp.broadcast_to(x_inv, (6, LANES))
    y_inv = jnp.broadcast_to(y_inv, (6, LANES))
    for h in range(ghosts):

        def store(row, many, value, h=h):
            ghost_ref[h * 8 + row : h * 8 + row + many] = value

        pack_tile(x_of(h), y_of(h), x_inv, y_inv, store)
    ox = packed_scale_ref[0:8]
    oy = packed_scale_ref[8:16]
    tiles = groups // 8
    panel_ref[...] = jnp.zeros(panel_ref.shape, F32)
    span = 8

    @pl.loop(0, tiles // 2 * (domains // span))
    def _(turn):
        first = turn // (tiles // 2) * span
        block = lax.rem(turn, tiles // 2) * 16
        at = [pl.ds(pl.multiple_of(block + u * 8, 8), 8) for u in range(2)]

        def row_of(h):
            k = h % 16
            row = (k // 4) * 16 + (k % 4 // 2) * 8 + 6 + k % 2
            return jnp.broadcast_to(recv_ref[first + h // 16, row : row + 1], (8, LANES))

        found = pick(
            row_of, span * 16, first * 16, [dv_ref[at[u]] for u in range(2)], [panel_ref[at[u]] for u in range(2)], False
        )
        for u in range(2):
            panel_ref[at[u]] = found[u]

    wide = spread_matrix(False)
    tall = spread_matrix(True)
    weights = jnp.concatenate(
        [
            dot(s_memb_ref[...], wide),
            dot(s_bend_ref[...], wide),
            dot(tall, dot(k_memb_ref[...], wide)),
            dot(tall, dot(k_bend_ref[...], wide)),
        ],
        axis=0,
    )
    w = three_parts(weights)
    stacked_weights = jnp.concatenate([w[0], w[0], w[1], w[0], w[1], w[2]], axis=1)
    names = lax.broadcasted_iota(I32, (8, LANES), 0)
    combs = comps // 8
    best_ref[...] = jnp.full(best_ref.shape, LOW, F32)

    def gather(b):
        lanes = pl.ds(pl.multiple_of(b * LANES, LANES), LANES)
        rows = connect_ref[:, lanes]
        indices = [jnp.broadcast_to(rows[a : a + 1], (8, LANES)) for a in range(4)]
        found = pick(
            lambda h: ghost_ref[h * 8 : h * 8 + 8],
            ghosts,
            own,
            indices,
            [got_ref[pl.ds(pl.multiple_of(b * 32 + a * 8, 8), 8)] for a in range(4)],
            True,
        )
        for a in range(4):
            far = indices[a] >= own * LANES
            x, y = unpack_tile(found[a], jnp.where(far, gx, ox), jnp.where(far, gy, oy))
            near = indices[a] < highs * 256
            at = pl.ds(pl.multiple_of(b * 32 + a * 8, 8), 8)
            move_ref[a * 8 : a * 8 + 8] = jnp.where(near, near_x_ref[at], x)
            cost_ref[a * 8 : a * 8 + 8] = jnp.where(near, near_y_ref[at], y)

    def dense(b):
        x = three_parts(move_ref[...])
        part = jnp.dot(
            stacked_weights,
            jnp.concatenate([x[0], x[1], x[0], x[2], x[1], x[0]], axis=0),
            preferred_element_type=F32,
        )
        row = pl.ds(b, 1)
        panel = panel_ref[row]
        bending = part[8:16]
        stress = part[0:8] + panel * bending
        failure = jnp.sum(stress * stress, axis=0, keepdims=True) / 8.0
        slope_ref[row] = jnp.sum(stress * bending, axis=0, keepdims=True) * (2.0 / 8.0)
        stiff = part[16:48] + (3.0 * panel * panel) * part[48:80]
        fixed_ref[row] = jnp.sum(cost_ref[...] * stiff, axis=0, keepdims=True)
        fail_ref[row] = failure
        away = comp_ref[row] - names
        for c in range(combs):
            held = best_ref[c * 8 : c * 8 + 8]
            best_ref[c * 8 : c * 8 + 8] = jnp.maximum(held, jnp.where(away == c * 8, failure, LOW))

    gather(0)

    @pl.loop(1, groups)
    def _(b):
        dense(b - 1)
        gather(b)

    dense(groups - 1)

    stats_ref[0] = jnp.zeros((8, LANES), F32)
    bands = (comps + LANES - 1) // LANES
    diagonal = lax.broadcasted_iota(I32, (LANES, LANES), 0) == lax.broadcasted_iota(I32, (LANES, LANES), 1)

    def to_rows(reduce, start):
        for band in range(bands):
            many = min(LANES, comps - band * LANES)
            column = reduce(best_ref[band * LANES : band * LANES + many], axis=1, keepdims=True)
            row = jnp.sum(jnp.where(diagonal[0:many], column, 0.0), axis=0, keepdims=True)
            stats_ref[0, start + band : start + band + 1] = row

    to_rows(jnp.max, 0)
    for t in range(tiles):
        block = slice(t * 8, t * 8 + 8)
        comp = comp_ref[block]
        low = comp & 127
        high = comp >> 7
        top = jnp.zeros((8, LANES), F32)
        for band in range(bands):
            tile = jnp.broadcast_to(stats_ref[0, band : band + 1], (8, LANES))
            top = jnp.where(high == band, lane_pick(tile, low), top)
        scaled = jnp.exp(SHARP * (fail_ref[block] - top))
        fail_ref[block] = scaled
        slope_ref[block] = slope_ref[block] * scaled

    part_of = combs // 2
    for half in range(2):

        def total_step(step, totals, half=half):
            totals = list(totals)
            for g in range(2):
                row = pl.ds(step * 2 + g, 1)
                away = comp_ref[row] - names
                value = fail_ref[row]
                for c in range(part_of):
                    totals[c] = totals[c] + jnp.where(away == (half * part_of + c) * 8, value, 0.0)
            return tuple(totals)

        totals = lax.fori_loop(0, groups // 2, total_step, (jnp.zeros((8, LANES), F32),) * part_of)
        for c in range(part_of):
            at = (half * part_of + c) * 8
            best_ref[at : at + 8] = totals[c]
    to_rows(jnp.sum, 4)
    mine = stats_ref[0]
    for d in range(1, domains):
        stats_ref[d] = mine


def last_kernel(
    here_ref, stats_ref, mult_ref, comp_ref, dv_ref, slope_ref, fixed_ref, ks_ref, sum_ref, term_ref, *, domains, comps, groups, slots
):
    here = here_ref[0]
    peak = stats_ref[0, 0:4]
    for s in range(1, domains):
        peak = jnp.maximum(peak, stats_ref[s, 0:4])
    total = jnp.zeros_like(peak)
    for s in range(domains):
        total = total + stats_ref[s, 4:8] * jnp.exp(SHARP * (stats_ref[s, 0:4] - peak))
    ks = peak + jnp.log(total) / SHARP
    share = jnp.exp(SHARP * (stats_ref[here, 0:4] - peak)) / total
    bands = (comps + LANES - 1) // LANES
    weights = []
    for band in range(bands):
        many = min(LANES, comps - band * LANES)
        span = slice(band * LANES, band * LANES + many)
        ks_ref[0:1, span] = ks[band : band + 1, 0:many]
        mult = mult_ref[0:1, span]
        if many < LANES:
            mult = jnp.concatenate([mult, jnp.zeros((1, LANES - many), F32)], axis=1)
        weights.append(jnp.broadcast_to(share[band : band + 1] * mult, (8, LANES)))
    tiles = groups // 8
    for t in range(tiles):
        block = slice(t * 8, t * 8 + 8)
        comp = comp_ref[block]
        low = comp & 127
        high = comp >> 7
        weight = jnp.zeros((8, LANES), F32)
        for band in range(bands):
            weight = jnp.where(high == band, lane_pick(weights[band], low), weight)
        term_ref[block] = weight * slope_ref[block] + fixed_ref[block]
    sum_ref[...] = jnp.zeros(sum_ref.shape, F32)
    outer = slots // 256
    outer_ids = lax.broadcasted_iota(I32, (outer, LANES), 0).astype(F32).astype(BF16)
    inner_ids = lax.broadcasted_iota(I32, (256, LANES), 0).astype(F32).astype(BF16)

    def tall(row, many):
        tile = jnp.broadcast_to(row.astype(F32), (16, LANES)).astype(BF16)
        return jnp.concatenate([tile] * (many // 16), axis=0)

    @pl.loop(0, tiles)
    def _(t):
        highs = []
        lows = []
        for j in range(8):
            place = dv_ref[pl.ds(t * 8 + j, 1)]
            value = term_ref[pl.ds(t * 8 + j, 1)]
            rough = value.astype(BF16).astype(F32)
            one = jnp.ones((outer, LANES), BF16)
            highs.append(jnp.where(outer_ids == tall(place >> 8, outer), one, jnp.zeros_like(one)))
            hit = inner_ids == tall(place & 255, 256)
            none = jnp.zeros((256, LANES), BF16)
            lows.append(
                jnp.concatenate(
                    [jnp.where(hit, tall(rough, 256), none), jnp.where(hit, tall(value - rough, 256), none)], axis=0
                )
            )
        both = lax.dot_general(
            jnp.concatenate(highs, axis=1),
            jnp.concatenate(lows, axis=1),
            (((1,), (1,)), ((), ())),
            preferred_element_type=F32,
        )
        sum_ref[...] += both[:, 0:256] + both[:, 256:512]


def vmem():
    return pl.BlockSpec(memory_space=pltpu.VMEM)


def smem():
    return pl.BlockSpec(memory_space=pltpu.SMEM)


def per_device(
    displacement, adjoint, send_list, connect, elem_comp, elem_dv, thickness, multiplier, k_memb, k_bend, s_memb, s_bend
):
    domains = lax.axis_size("dom")
    here = lax.axis_index("dom").astype(I32).reshape(1)
    comps = multiplier.shape[1]
    nodes = displacement.shape[2]
    elems = connect.shape[1]
    iface = send_list.shape[2]
    own = nodes // LANES
    groups = elems // LANES
    slots = thickness.shape[0] * domains
    block = 4 * iface // LANES * 4
    sds = jax.ShapeDtypeStruct

    disp = displacement.reshape(-1, LANES)
    adj = adjoint.reshape(-1, LANES)
    highs = min(HIGHS, own // 2)

    packed, scale, send = pl.pallas_call(
        functools.partial(send_kernel, chunks=own, domains=domains, iface=iface),
        out_shape=(sds((own * 8, LANES), I32), sds((16, LANES), F32), sds((domains, block, LANES), F32)),
        in_specs=[smem()] + [vmem()] * 4,
        out_specs=(vmem(),) * 3,
        name="send_pick",
    )(here, disp, adj, send_list, thickness.reshape(-1, LANES))
    recv = lax.all_to_all(send, "dom", 0, 0, tiled=True)
    got, near_x, near_y = pl.pallas_call(
        functools.partial(own_kernel, chunks=own, groups=groups, highs=highs),
        out_shape=(sds((groups * 32, LANES), I32),) + (sds((groups * 32, LANES), F32),) * 2,
        in_specs=[vmem()] * 4,
        out_specs=(vmem(),) * 3,
        scratch_shapes=[pltpu.VMEM((highs * ROWS, 256), F32), pltpu.VMEM((highs * ROWS, 256), BF16)],
        name="own_pick",
        cost_estimate=pl.CostEstimate(flops=0, transcendentals=0, bytes_accessed=60_000_000),
    )(packed, disp, adj, connect)
    comp = elem_comp.reshape(-1, LANES)
    dv = elem_dv.reshape(-1, LANES)
    stats, slope, fixed = pl.pallas_call(
        functools.partial(main_kernel, own=own, groups=groups, domains=domains, iface=iface, comps=comps, highs=highs),
        out_shape=(sds((domains, 8, LANES), F32), sds((groups, LANES), F32), sds((groups, LANES), F32)),
        in_specs=[smem()] + [vmem()] * 12,
        out_specs=(vmem(),) * 3,
        scratch_shapes=[
            pltpu.VMEM((len(OFFSETS) * iface // LANES * 8, LANES), I32),
            pltpu.VMEM((32, LANES), F32),
            pltpu.VMEM((32, LANES), F32),
            pltpu.VMEM((groups, LANES), F32),
            pltpu.VMEM((groups, LANES), F32),
            pltpu.VMEM((comps, LANES), F32),
        ],
        name="element_work",
    )(here, recv, scale, got, near_x, near_y, connect, comp, dv, s_memb, s_bend, k_memb, k_bend)
    everyone = lax.all_to_all(stats, "dom", 0, 0, tiled=True)
    ks_value, sums = pl.pallas_call(
        functools.partial(last_kernel, domains=domains, comps=comps, groups=groups, slots=slots),
        out_shape=(sds((1, comps), F32), sds((slots // 256, 256), F32)),
        in_specs=[smem()] + [vmem()] * 6,
        out_specs=(vmem(),) * 2,
        scratch_shapes=[pltpu.VMEM((groups, LANES), F32)],
        name="weigh_and_sum",
    )(here, everyone, multiplier, comp, dv, slope, fixed)
    arrived = lax.all_to_all(sums.reshape(domains, -1, 256), "dom", 0, 0, tiled=True)
    owned = arrived.sum(axis=0)
    sensitivity = from_everyone(owned, "load").sum(axis=0).reshape(-1)
    return ks_value, sensitivity


def solution(mesh):
    in_specs = (
        P("load", None, "dom"),
        P("load", None, "dom"),
        P("dom", None, None),
        P(None, "dom"),
        P("dom"),
        P("dom"),
        P("dom"),
        P("load", None),
        P(),
        P(),
        P(),
        P(),
    )
    return jax.shard_map(
        per_device, mesh=mesh, in_specs=in_specs, out_specs=(P("load", None), P("dom")), check_vma=False
    )
```

time: 141 us -> 110 us (0.78)
  Pallas kernels: 83.3 us -> 55.7 us
  blocking collectives: 28.1 us -> 43.3 us
  starting transfers between devices: 16.1 us -> 8.58 us
  waiting for transfers between devices: 7.09 us -> 0.01 us
  local copies, waits for them, and re-layouts: 4.3 us -> 1.59 us
    all_to_all x1 -> x2, blocking collectives: 13 us -> 28.1 us  [the longest x1 15.2 us: per_device(): everyone = lax.all_to_all(stats, 'dom', 0, 0, tiled=True)]
    pallas_call x1, Pallas kernels: 38.6 us -> 24.6 us  [per_device(): pl.pallas_call(functools.partial(main_kernel, own=own, groups=groups, dom...]
    pallas_call x1, Pallas kernels: 32.8 us -> 20 us  [per_device(): pl.pallas_call(functools.partial(own_kernel, chunks=own, groups=groups, h...]
    all_to_all x1 -> x0, starting transfers between devices: 7.51 us -> none  [per_device(): everyone = lax.all_to_all(stats, 'dom', 0, 0, tiled=True)]
    all_to_all x1 -> x0, waiting for transfers between devices: 7.08 us -> none  [per_device(): everyone = lax.all_to_all(stats, 'dom', 0, 0, tiled=True)]
    unnamed x7 -> x3, local copies, waits for them, and re-layouts: 3.72 us -> 1.58 us
  transfers between devices with their start and end apart: 2 -> 1, of which waited for: 1 -> 0; matrix products, arithmetic and copies ran while one was open for 0% -> 0% of each run, Pallas kernels for 23% -> 18%
where the time goes in v2:
time: 110 us
  Pallas kernels  55.7 us (51%)
  blocking collectives  43.3 us (39%)
  starting transfers between devices  8.58 us (8%)
  local copies, waits for them, and re-layouts  1.59 us (1%)
    pallas_call x1, Pallas kernels, per_device(): pl.pallas_call(functools.partial(main_kernel, own=own, groups=groups, dom...  24.6 us
    pallas_call x1, Pallas kernels, per_device(): pl.pallas_call(functools.partial(own_kernel, chunks=own, groups=groups, h...  20 us
    all_to_all x1, blocking collectives, per_device(): everyone = lax.all_to_all(stats, 'dom', 0, 0, tiled=True)  15.2 us
    all_to_all x1, blocking collectives, from_everyone(): lax.all_to_all(jnp.broadcast_to(x[None], (count, *x.shape)), axis, 0, 0,...  15.2 us
    all_to_all x1, blocking collectives, per_device(): lax.all_to_all(sums.reshape(domains, -1, 256), 'dom', 0, 0, tiled=True)  13 us
    all_to_all x1, starting transfers between devices, per_device(): recv = lax.all_to_all(send, 'dom', 0, 0, tiled=True)  8.58 us
    pallas_call x1, Pallas kernels, per_device(): pl.pallas_call(functools.partial(last_kernel, domains=domains, comps=comp...  5.68 us
    pallas_call x1, Pallas kernels, per_device(): pl.pallas_call(functools.partial(send_kernel, chunks=own, domains=domains...  5.53 us
  transfers between devices with their start and end apart: 1, of which 0 were waited for; matrix products, arithmetic and copies ran while one was open for 0% of the time, Pallas kernels for 18%

profile of v2, /device:TPU:1, one launch (start us, length us, event | category | flops | bytes accessed | tf_op | source)
XLA Modules:
  0.0 109.9 jit_solution(3518290205334706627)
XLA Ops:
  0.6 5.5 %send_pick.1 = (s32[512,128]{1,0:T(8,128)}, f32[16,128]{1,0:T(8,128)}, f32[32,64,128]{2,1,0:T(8,128)}) custom-call(s32[1]{0:T(128)} %bitcast.here_ref, f32[384,128]{1,0:T(8,128)} %bitcast.9, f32[384,128]{1,0:T(8,128)} %bitcast.11, s32[1,32,512]{2,1,0:T(8,128)} %list_ref.1, f32[16,128]{1,0:T(8,128)} %bitcast.19), custom_call_target="tpu_custom_call" | custom-call | tf_op jit(solution)/shard_map/send_pick/pallas_call | solution.py:514
  6.2 8.6 %all-to-all-start = ((f32[32,64,128]{2,1,0:T(8,128)}), f32[32,64,128]{2,1,0:T(8,128)S(1)}, u32[]{:S(2)}, u32[]{:S(2)}) async-start(f32[32,64,128]{2,1,0:T(8,128)} %get-tuple-element.13), calls=%async_computation | async-start | bytes 2097152 | tf_op jit(solution)/shard_map/all_to_all | solution.py:521
  14.7 20.0 %own_pick.1 = (s32[2048,128]{1,0:T(8,128)}, f32[2048,128]{1,0:T(8,128)}, f32[2048,128]{1,0:T(8,128)}) custom-call(s32[512,128]{1,0:T(8,128)} %get-tuple-element.15.packed_ref, f32[384,128]{1,0:T(8,128)} %bitcast.10, f32[384,128]{1,0:T(8,128)} %bitcast.12, s32[4,8192]{1,0:T(4,128)} %connect_ref.3), custom_call_target="tpu_custom_call" | custom-call | bytes 60000000 | tf_op jit(solution)/shard_map/own_pick/pallas_call | solution.py:522
  34.7 0.0 all-to-all-done.recv_ref
  34.7 0.0 copy-start
  34.7 1.0 copy-done
  35.7 24.6 %element_work.1 = (f32[32,8,128]{2,1,0:T(8,128)}, f32[64,128]{1,0:T(8,128)}, f32[64,128]{1,0:T(8,128)}) custom-call(s32[1]{0:T(128)} %bitcast.here_ref, f32[32,64,128]{2,1,0:T(8,128)} %copy-done, f32[16,128]{1,0:T(8,128)} %get-tuple-element.14.packed_scale_ref, s32[2048,128]{1,0:T(8,128)} %get-tuple-element.16.got_ref, ...), custom_call_target="tpu_custom_call" | custom-call | tf_op jit(solution)/shard_map/element_work/pallas_call | solution.py:533
  60.2 15.2 %all_to_all.20.stats_ref = f32[32,8,128]{2,1,0:T(8,128)} all-to-all(f32[32,8,128]{2,1,0:T(8,128)} %get-tuple-element.19), channel_id=1, replica_groups=mesh['load'=8,'dom'=32] {'dom'}, dimensions={0} | all-to-all | bytes 262144 | tf_op jit(solution)/shard_map/all_to_all | solution.py:548
  75.4 5.7 %weigh_and_sum.1 = (f32[1,400]{1,0:T(1,128)}, f32[256,256]{1,0:T(8,128)}) custom-call(s32[1]{0:T(128)} %bitcast.here_ref, f32[32,8,128]{2,1,0:T(8,128)} %all_to_all.20.stats_ref, f32[1,400]{1,0:T(1,128)} %mult_ref.1, s32[64,128]{1,0:T(8,128)} %bitcast.15, s32[64,128]{1,0:T(8,128)} %bitcast.17, f32[64,128]{1,0:T(8,128)} %get-tuple-element.20.slope_ref, ...), custom_call_target="tpu_custom_call" | custom-call | tf_op jit(solution)/shard_map/weigh_and_sum/pallas_call | solution.py:549
  81.1 13.0 %all_to_all.21 = f32[32,8,256]{2,1,0:T(8,128)S(1)} all-to-all(f32[32,8,256]{2,1,0:T(8,128)} %bitcast.13), channel_id=1, replica_groups=mesh['load'=8,'dom'=32] {'dom'}, dimensions={0} | all-to-all | bytes 524288 | tf_op jit(solution)/shard_map/all_to_all | solution.py:557
  94.1 15.2 %all_to_all.22 = f32[8,8,256]{2,1,0:T(8,128)S(1)} all-to-all(f32[8,8,256]{2,1,0:T(8,128)S(1)} %broadcast_in_dim.2), channel_id=1, replica_groups=mesh['load'=8,'dom'=32] {'load'}, dimensions={0} | all-to-all | bytes 131072 | tf_op jit(solution)/shard_map/all_to_all | solution.py:27
  109.3 0.6 copy.14
  (3 shorter events, 0.1 us)
Async XLA Ops:
  6.2 28.5 %all-to-all-start = ((f32[32,64,128]{2,1,0:T(8,128)}), f32[32,64,128]{2,1,0:T(8,128)S(1)}, u32[]{:S(2)}, u32[]{:S(2)}) async-start(f32[32,64,128]{2,1,0:T(8,128)} %get-tuple-element.13), calls=%async_computation | async-start | bytes 2097152 | tf_op jit(solution)/shard_map/all_to_all | solution.py:521
  34.7 1.0 copy-start

commit v3 on v2

--- a/solution.py
+++ b/solution.py
@@ -10,6 +10,8 @@
 NBR = 3
 ROWS = 24
 HIGHS = 14
+SLICE = 1024
+CAP = 64
 SHARP = 50.0
 LOW = -1e30
 LANES = 128
@@ -20,11 +22,6 @@
 I32 = jnp.int32
 F32 = jnp.float32
 BF16 = jnp.bfloat16
-
-
-def from_everyone(x, axis):
-    count = lax.axis_size(axis)
-    return lax.all_to_all(jnp.broadcast_to(x[None], (count, *x.shape)), axis, 0, 0, tiled=True)
 
 
 def lane_pick(table, index):
@@ -239,15 +236,16 @@
     s_bend_ref,
     k_memb_ref,
     k_bend_ref,
-    stats_ref,
-    slope_ref,
-    fixed_ref,
+    out_ref,
     ghost_ref,
     move_ref,
     cost_ref,
     panel_ref,
     fail_ref,
     best_ref,
+    slope_ref,
+    fixed_ref,
+    stats_ref,
     *,
     own,
     groups,
@@ -255,6 +253,9 @@
     iface,
     comps,
     highs,
+    owned,
+    slots,
+    cap,
 ):
     rows = iface // LANES
     ghosts = len(OFFSETS) * rows
@@ -412,25 +413,83 @@
             at = (half * part_of + c) * 8
             best_ref[at : at + 8] = totals[c]
     to_rows(jnp.sum, 4)
+
+    shift = owned.bit_length() - 1
+    owner_ids = lax.broadcasted_iota(I32, (domains, LANES), 0)
+    owner_names = owner_ids.astype(F32).astype(BF16)
+    rank_names = lax.broadcasted_iota(I32, (cap, LANES), 0).astype(F32).astype(BF16)
+    one = jnp.ones((cap, LANES), BF16)
+    zero = jnp.zeros((cap, LANES), BF16)
+    none = jnp.zeros((domains, LANES), BF16)
+    before = lax.broadcasted_iota(I32, (LANES, LANES), 0) < lax.broadcasted_iota(I32, (LANES, LANES), 1)
+    before = jnp.concatenate(
+        [jnp.where(before, 1.0, 0.0).astype(BF16), jnp.ones((LANES, LANES), BF16)], axis=1
+    )
+    block_rows = slots // LANES
+
+    @pl.loop(0, groups // (2 * block_rows))
+    def _(pair):
+        sums = []
+        for parity in range(2):
+            at = [pair * 2 * block_rows + parity * block_rows + j for j in range(block_rows)]
+            places = [dv_ref[pl.ds(r, 1)] for r in at]
+            owners = [jnp.where(owner_ids == (place >> shift), 1.0, 0.0) for place in places]
+            counts = jnp.dot(
+                jnp.concatenate([o.astype(BF16) for o in owners], axis=0), before, preferred_element_type=F32
+            )
+            base = jnp.zeros((domains, LANES), F32)
+            left = []
+            right = []
+            for j in range(block_rows):
+                count = counts[j * domains : (j + 1) * domains]
+                rank = jnp.sum(owners[j] * (count[:, 0:LANES] + base), axis=0, keepdims=True)
+                base = base + count[:, LANES : 2 * LANES]
+                right.append(jnp.where(rank_names == tall_row(rank, cap), one, zero))
+                hit = owner_names == tall_row((places[j] >> shift).astype(F32), domains)
+                row = pl.ds(at[j], 1)
+                values = (
+                    fixed_ref[row],
+                    slope_ref[row],
+                    (places[j] & (owned - 1)).astype(F32),
+                    comp_ref[row].astype(F32),
+                )
+                pieces = []
+                for value in values:
+                    rough = value.astype(BF16).astype(F32)
+                    pieces.append(jnp.where(hit, tall_row(rough, domains), none))
+                    pieces.append(jnp.where(hit, tall_row(value - rough, domains), none))
+                left.append(jnp.concatenate(pieces, axis=0))
+            moved = lax.dot_general(
+                jnp.concatenate(left, axis=1),
+                jnp.concatenate(right, axis=1),
+                (((1,), (1,)), ((), ())),
+                preferred_element_type=F32,
+            )
+            parts = [moved[p * domains : (p + 1) * domains] for p in range(8)]
+            sums.append([parts[2 * v] + parts[2 * v + 1] for v in range(4)])
+        for v in range(4):
+            out_ref[pl.ds(v * 4 + pair, domains, stride=24)] = jnp.concatenate([sums[0][v], sums[1][v]], axis=1)
+
     mine = stats_ref[0]
-    for d in range(1, domains):
-        stats_ref[d] = mine
-
-
-def last_kernel(
-    here_ref, stats_ref, mult_ref, comp_ref, dv_ref, slope_ref, fixed_ref, ks_ref, sum_ref, term_ref, *, domains, comps, groups, slots
-):
-    here = here_ref[0]
-    peak = stats_ref[0, 0:4]
+    for d in range(domains):
+        out_ref[d * 24 + 16 : d * 24 + 24] = mine
+
+
+def tall_row(row, many):
+    tile = jnp.broadcast_to(row, (16, LANES)).astype(BF16)
+    return jnp.concatenate([tile] * (many // 16), axis=0)
+
+
+def last_kernel(recv_ref, mult_ref, ks_ref, sum_ref, fold_ref, *, domains, comps, owned):
+    peak = recv_ref[0, 16:20]
     for s in range(1, domains):
-        peak = jnp.maximum(peak, stats_ref[s, 0:4])
+        peak = jnp.maximum(peak, recv_ref[s, 16:20])
     total = jnp.zeros_like(peak)
     for s in range(domains):
-        total = total + stats_ref[s, 4:8] * jnp.exp(SHARP * (stats_ref[s, 0:4] - peak))
+        total = total + recv_ref[s, 20:24] * jnp.exp(SHARP * (recv_ref[s, 16:20] - peak))
     ks = peak + jnp.log(total) / SHARP
-    share = jnp.exp(SHARP * (stats_ref[here, 0:4] - peak)) / total
     bands = (comps + LANES - 1) // LANES
-    weights = []
+    mults = []
     for band in range(bands):
         many = min(LANES, comps - band * LANES)
         span = slice(band * LANES, band * LANES + many)
@@ -438,50 +497,66 @@
         mult = mult_ref[0:1, span]
         if many < LANES:
             mult = jnp.concatenate([mult, jnp.zeros((1, LANES - many), F32)], axis=1)
-        weights.append(jnp.broadcast_to(share[band : band + 1] * mult, (8, LANES)))
-    tiles = groups // 8
-    for t in range(tiles):
-        block = slice(t * 8, t * 8 + 8)
-        comp = comp_ref[block]
-        low = comp & 127
-        high = comp >> 7
-        weight = jnp.zeros((8, LANES), F32)
-        for band in range(bands):
-            weight = jnp.where(high == band, lane_pick(weights[band], low), weight)
-        term_ref[block] = weight * slope_ref[block] + fixed_ref[block]
-    sum_ref[...] = jnp.zeros(sum_ref.shape, F32)
-    outer = slots // 256
+        mults.append(mult)
+    factor = jnp.concatenate(mults, axis=0) / total[0:bands]
+    half = LANES // 2
+    outer = owned // half
     outer_ids = lax.broadcasted_iota(I32, (outer, LANES), 0).astype(F32).astype(BF16)
-    inner_ids = lax.broadcasted_iota(I32, (256, LANES), 0).astype(F32).astype(BF16)
-
-    def tall(row, many):
-        tile = jnp.broadcast_to(row.astype(F32), (16, LANES)).astype(BF16)
-        return jnp.concatenate([tile] * (many // 16), axis=0)
-
-    @pl.loop(0, tiles)
-    def _(t):
-        highs = []
-        lows = []
-        for j in range(8):
-            place = dv_ref[pl.ds(t * 8 + j, 1)]
-            value = term_ref[pl.ds(t * 8 + j, 1)]
-            rough = value.astype(BF16).astype(F32)
-            one = jnp.ones((outer, LANES), BF16)
-            highs.append(jnp.where(outer_ids == tall(place >> 8, outer), one, jnp.zeros_like(one)))
-            hit = inner_ids == tall(place & 255, 256)
-            none = jnp.zeros((256, LANES), BF16)
-            lows.append(
-                jnp.concatenate(
-                    [jnp.where(hit, tall(rough, 256), none), jnp.where(hit, tall(value - rough, 256), none)], axis=0
+    inner_ids = lax.broadcasted_iota(I32, (half, LANES), 0).astype(F32).astype(BF16)
+    one = jnp.ones((half, LANES), BF16)
+    zero = jnp.zeros((half, LANES), BF16)
+    none = jnp.zeros((outer, LANES), BF16)
+
+    def part_sum(sources):
+        left = []
+        right = []
+        for s in sources:
+            share = jnp.exp(SHARP * (recv_ref[s, 16 : 16 + bands] - peak[0:bands])) * factor
+            values = recv_ref[s, 0:8]
+            labels = recv_ref[s, 8:16].astype(I32)
+            low = labels & 127
+            high = labels >> 7
+            weight = jnp.zeros((8, LANES), F32)
+            for band in range(bands):
+                tile = jnp.broadcast_to(share[band : band + 1], (8, LANES))
+                weight = jnp.where(high == band, lane_pick(tile, low), weight)
+            terms = values + jnp.roll(weight * values, 4, axis=0)
+            roughs = terms.astype(BF16).astype(F32)
+            fines = terms - roughs
+            outers = (labels >> 6).astype(F32)
+            inners = (labels & 63).astype(F32)
+            for r in range(4):
+                row = slice(r, r + 1)
+                hit = outer_ids == tall_row(outers[row], outer)
+                left.append(
+                    jnp.concatenate(
+                        [
+                            jnp.where(hit, tall_row(roughs[row], outer), none),
+                            jnp.where(hit, tall_row(fines[row], outer), none),
+                        ],
+                        axis=0,
+                    )
                 )
-            )
+                right.append(jnp.where(inner_ids == tall_row(inners[row], half), one, zero))
         both = lax.dot_general(
-            jnp.concatenate(highs, axis=1),
-            jnp.concatenate(lows, axis=1),
+            jnp.concatenate(left, axis=1),
+            jnp.concatenate(right, axis=1),
             (((1,), (1,)), ((), ())),
             preferred_element_type=F32,
         )
-        sum_ref[...] += both[:, 0:256] + both[:, 256:512]
+        return both[0:outer] + both[outer : 2 * outer]
+
+    def step(turn, sums):
+        return tuple(sums[m] + part_sum([turn * 4 + m * 2 + j for j in range(2)]) for m in range(2))
+
+    empty = jnp.zeros((outer, half), F32)
+    sums = lax.fori_loop(0, domains // 4, step, (empty, empty))
+    fold_ref[:, 0:half] = sums[0] + sums[1]
+    folded = jnp.concatenate(
+        [fold_ref[pl.ds(parity, outer // 2, stride=2)][:, 0:half] for parity in range(2)], axis=1
+    )
+    for l in range(sum_ref.shape[0]):
+        sum_ref[l] = folded
 
 
 def vmem():
@@ -503,7 +578,6 @@
     iface = send_list.shape[2]
     own = nodes // LANES
     groups = elems // LANES
-    slots = thickness.shape[0] * domains
     block = 4 * iface // LANES * 4
     sds = jax.ShapeDtypeStruct
 
@@ -530,11 +604,23 @@
     )(packed, disp, adj, connect)
     comp = elem_comp.reshape(-1, LANES)
     dv = elem_dv.reshape(-1, LANES)
-    stats, slope, fixed = pl.pallas_call(
-        functools.partial(main_kernel, own=own, groups=groups, domains=domains, iface=iface, comps=comps, highs=highs),
-        out_shape=(sds((domains, 8, LANES), F32), sds((groups, LANES), F32), sds((groups, LANES), F32)),
+    owned = thickness.shape[0]
+    mine = pl.pallas_call(
+        functools.partial(
+            main_kernel,
+            own=own,
+            groups=groups,
+            domains=domains,
+            iface=iface,
+            comps=comps,
+            highs=highs,
+            owned=owned,
+            slots=SLICE,
+            cap=CAP,
+        ),
+        out_shape=sds((domains * 24, LANES), F32),
         in_specs=[smem()] + [vmem()] * 12,
-        out_specs=(vmem(),) * 3,
+        out_specs=vmem(),
         scratch_shapes=[
             pltpu.VMEM((len(OFFSETS) * iface // LANES * 8, LANES), I32),
             pltpu.VMEM((32, LANES), F32),
@@ -542,21 +628,23 @@
             pltpu.VMEM((groups, LANES), F32),
             pltpu.VMEM((groups, LANES), F32),
             pltpu.VMEM((comps, LANES), F32),
+            pltpu.VMEM((groups, LANES), F32),
+            pltpu.VMEM((groups, LANES), F32),
+            pltpu.VMEM((1, 8, LANES), F32),
         ],
         name="element_work",
     )(here, recv, scale, got, near_x, near_y, connect, comp, dv, s_memb, s_bend, k_memb, k_bend)
-    everyone = lax.all_to_all(stats, "dom", 0, 0, tiled=True)
+    everyone = lax.all_to_all(mine.reshape(domains, 24, LANES), "dom", 0, 0, tiled=True)
+    loads = lax.axis_size("load")
     ks_value, sums = pl.pallas_call(
-        functools.partial(last_kernel, domains=domains, comps=comps, groups=groups, slots=slots),
-        out_shape=(sds((1, comps), F32), sds((slots // 256, 256), F32)),
-        in_specs=[smem()] + [vmem()] * 6,
+        functools.partial(last_kernel, domains=domains, comps=comps, owned=owned),
+        out_shape=(sds((1, comps), F32), sds((loads, owned // LANES, LANES), F32)),
+        in_specs=[vmem()] * 2,
         out_specs=(vmem(),) * 2,
-        scratch_shapes=[pltpu.VMEM((groups, LANES), F32)],
+        scratch_shapes=[pltpu.VMEM((owned * 2 // LANES, LANES), F32)],
         name="weigh_and_sum",
-    )(here, everyone, multiplier, comp, dv, slope, fixed)
-    arrived = lax.all_to_all(sums.reshape(domains, -1, 256), "dom", 0, 0, tiled=True)
-    owned = arrived.sum(axis=0)
-    sensitivity = from_everyone(owned, "load").sum(axis=0).reshape(-1)
+    )(everyone, multiplier)
+    sensitivity = lax.all_to_all(sums, "load", 0, 0, tiled=True).sum(axis=0).reshape(-1)
     return ks_value, sensitivity
 
 

time: 110 us -> 101 us (0.918)
  blocking collectives: 43.3 us -> 33.1 us
  Pallas kernels: 55.7 us -> 57.1 us
    all_to_all x3 -> x2, blocking collectives: 43.3 us -> 33.1 us  [the longest x1 17.8 us: per_device(): lax.all_to_all(mine.reshape(domains, 24, LANES), 'dom', 0, 0, tiled=True)]
    pallas_call x1, Pallas kernels: 24.6 us -> 27.4 us  [per_device(): pl.pallas_call(functools.partial(main_kernel, own=own, groups=groups, dom...]
    pallas_call x1, Pallas kernels: 5.68 us -> 4.15 us  [per_device(): pl.pallas_call(functools.partial(last_kernel, domains=domains, comps=comp...]
  transfers between devices with their start and end apart: 1 -> 1, of which waited for: 0 -> 0; matrix products, arithmetic and copies ran while one was open for 0% -> 0% of each run, Pallas kernels for 18% -> 20%
where the time goes in v3:
time: 101 us
  Pallas kernels  57.1 us (57%)
  blocking collectives  33.1 us (33%)
  starting transfers between devices  8.58 us (8%)
    pallas_call x1, Pallas kernels, per_device(): pl.pallas_call(functools.partial(main_kernel, own=own, groups=groups, dom...  27.4 us
    pallas_call x1, Pallas kernels, per_device(): pl.pallas_call(functools.partial(own_kernel, chunks=own, groups=groups, h...  20 us
    all_to_all x1, blocking collectives, per_device(): lax.all_to_all(mine.reshape(domains, 24, LANES), 'dom', 0, 0, tiled=True)  17.8 us
    all_to_all x1, blocking collectives, per_device(): lax.all_to_all(sums, 'load', 0, 0, tiled=True).sum(axis=0).reshape(-1)  15.3 us
    all_to_all x1, starting transfers between devices, per_device(): recv = lax.all_to_all(send, 'dom', 0, 0, tiled=True)  8.58 us
    pallas_call x1, Pallas kernels, per_device(): pl.pallas_call(functools.partial(send_kernel, chunks=own, domains=domains...  5.53 us
    pallas_call x1, Pallas kernels, per_device(): pl.pallas_call(functools.partial(last_kernel, domains=domains, comps=comp...  4.15 us
  transfers between devices with their start and end apart: 1, of which 0 were waited for; matrix products, arithmetic and copies ran while one was open for 0% of the time, Pallas kernels for 20%

profile of v3, /device:TPU:1, one launch (start us, length us, event | category | flops | bytes accessed | tf_op | source)
XLA Modules:
  0.0 101.0 jit_solution(4134231131282104649)
XLA Ops:
  0.6 5.5 %send_pick.1 = (s32[512,128]{1,0:T(8,128)}, f32[16,128]{1,0:T(8,128)}, f32[32,64,128]{2,1,0:T(8,128)}) custom-call(s32[1]{0:T(128)} %bitcast.here_ref, f32[384,128]{1,0:T(8,128)} %bitcast.9, f32[384,128]{1,0:T(8,128)} %bitcast.11, s32[1,32,512]{2,1,0:T(8,128)} %list_ref.1, f32[16,128]{1,0:T(8,128)} %bitcast.15), custom_call_target="tpu_custom_call" | custom-call | tf_op jit(solution)/shard_map/send_pick/pallas_call | solution.py:588
  6.2 8.6 %all-to-all-start = ((f32[32,64,128]{2,1,0:T(8,128)}), f32[32,64,128]{2,1,0:T(8,128)S(1)}, u32[]{:S(2)}, u32[]{:S(2)}) async-start(f32[32,64,128]{2,1,0:T(8,128)} %get-tuple-element.10), calls=%async_computation | async-start | bytes 2097152 | tf_op jit(solution)/shard_map/all_to_all | solution.py:595
  14.8 20.0 %own_pick.1 = (s32[2048,128]{1,0:T(8,128)}, f32[2048,128]{1,0:T(8,128)}, f32[2048,128]{1,0:T(8,128)}) custom-call(s32[512,128]{1,0:T(8,128)} %get-tuple-element.12.packed_ref, f32[384,128]{1,0:T(8,128)} %bitcast.10, f32[384,128]{1,0:T(8,128)} %bitcast.12, s32[4,8192]{1,0:T(4,128)} %connect_ref.3), custom_call_target="tpu_custom_call" | custom-call | bytes 60000000 | tf_op jit(solution)/shard_map/own_pick/pallas_call | solution.py:596
  34.7 0.0 all-to-all-done.recv_ref
  34.7 0.0 copy-start
  34.7 1.0 copy-done
  35.7 27.4 %element_work.1 = f32[768,128]{1,0:T(8,128)} custom-call(s32[1]{0:T(128)} %bitcast.here_ref, f32[32,64,128]{2,1,0:T(8,128)} %copy-done, f32[16,128]{1,0:T(8,128)} %get-tuple-element.11.packed_scale_ref, s32[2048,128]{1,0:T(8,128)} %get-tuple-element.13.got_ref, f32[2048,128]{1,0:T(8,128)} %get-tuple-element.14.near_x_ref, ...), custom_call_target="tpu_custom_call" | custom-call | tf_op jit(solution)/shard_map/element_work/pallas_call | solution.py:608
  63.1 17.8 %all_to_all.15.recv_ref = f32[32,24,128]{2,1,0:T(8,128)} all-to-all(f32[32,24,128]{2,1,0:T(8,128)} %bitcast.8), channel_id=1, replica_groups=mesh['load'=8,'dom'=32] {'dom'}, dimensions={0} | all-to-all | bytes 786432 | tf_op jit(solution)/shard_map/all_to_all | solution.py:637
  80.9 4.1 %weigh_and_sum.1 = (f32[1,400]{1,0:T(1,128)}, f32[8,16,128]{2,1,0:T(8,128)}) custom-call(f32[32,24,128]{2,1,0:T(8,128)} %all_to_all.15.recv_ref, f32[1,400]{1,0:T(1,128)} %mult_ref.1), custom_call_target="tpu_custom_call" | custom-call | tf_op jit(solution)/shard_map/weigh_and_sum/pallas_call | solution.py:639
  85.0 15.3 %all_to_all.16 = f32[8,16,128]{2,1,0:T(8,128)S(1)} all-to-all(f32[8,16,128]{2,1,0:T(8,128)} %get-tuple-element.17), channel_id=1, replica_groups=mesh['load'=8,'dom'=32] {'load'}, dimensions={0} | all-to-all | bytes 131072 | tf_op jit(solution)/shard_map/all_to_all | solution.py:647
  100.4 0.6 reduce_sum.9
Async XLA Ops:
  6.2 28.5 %all-to-all-start = ((f32[32,64,128]{2,1,0:T(8,128)}), f32[32,64,128]{2,1,0:T(8,128)S(1)}, u32[]{:S(2)}, u32[]{:S(2)}) async-start(f32[32,64,128]{2,1,0:T(8,128)} %get-tuple-element.10), calls=%async_computation | async-start | bytes 2097152 | tf_op jit(solution)/shard_map/all_to_all | solution.py:595
  34.7 1.0 copy-start

commit v4 on v3

--- a/solution.py
+++ b/solution.py
@@ -10,6 +10,7 @@
 NBR = 3
 ROWS = 24
 HIGHS = 14
+GHOST_HIGHS = 6
 SLICE = 1024
 CAP = 64
 SHARP = 50.0
@@ -33,9 +34,9 @@
     return (row % 3) * 10
 
 
-def scales_of(x_of, count, top):
-    best = jnp.abs(x_of(0))
-    for h in range(1, count):
+def scales_of(x_of, tiles, top):
+    best = jnp.abs(x_of(tiles[0]))
+    for h in tiles[1:]:
         best = jnp.maximum(best, jnp.abs(x_of(h)))
     most = jnp.maximum(jnp.max(best, axis=1, keepdims=True), 1e-30)
     return top / most, most / top
@@ -79,8 +80,8 @@
 def send_kernel(here_ref, disp_ref, adj_ref, list_ref, thick_ref, packed_ref, scale_ref, send_ref, *, chunks, domains, iface):
     rows = iface // LANES
     cut = lambda ref, h: ref[pl.ds(h, 6, stride=chunks)]
-    x_inv, x_scale = scales_of(lambda h: cut(disp_ref, h), chunks, DISP_TOP)
-    y_inv, y_scale = scales_of(lambda h: cut(adj_ref, h), chunks, ADJ_TOP)
+    x_inv, x_scale = scales_of(lambda h: cut(disp_ref, h), range(chunks), DISP_TOP)
+    y_inv, y_scale = scales_of(lambda h: cut(adj_ref, h), range(chunks), ADJ_TOP)
     scale_ref[0:8] = pad_rows(x_scale)
     scale_ref[8:16] = pad_rows(y_scale)
     xs = scale_ref[0:8]
@@ -140,52 +141,59 @@
     lax.fori_loop(0, turns, body, fetch(jnp.int32(0)))
 
 
-def own_kernel(
-    packed_ref, disp_ref, adj_ref, connect_ref, got_ref, near_x_ref, near_y_ref, wide_ref, table_ref, *, chunks, groups, highs
-):
+def fill_table(x_of, y_of, highs, wide_ref, table_ref):
     for high in range(highs):
         for half in range(2):
             lanes = slice(half * LANES, half * LANES + LANES)
-            x = disp_ref[pl.ds(high * 2 + half, 6, stride=chunks)]
-            y = adj_ref[pl.ds(high * 2 + half, 6, stride=chunks)]
+            x = x_of(high * 2 + half)
+            y = y_of(high * 2 + half)
             xh = x.astype(BF16).astype(F32)
             yh = y.astype(BF16).astype(F32)
             xl = x - xh
             yl = y - yh
-            pieces = (xh, yh[0:2], yl[4:6], yh[2:6], yl[2:4], xl, yl[0:2])
             at = high * ROWS
-            for piece in pieces:
+            for piece in (xh, yh[0:2], yl[4:6], yh[2:6], yl[2:4], xl, yl[0:2]):
                 wide_ref[at : at + piece.shape[0], lanes] = piece
                 at += piece.shape[0]
     table_ref[...] = wide_ref[...].astype(BF16)
+
+
+def matrix_pick(table_ref, indices, highs, first_high):
     row_ids = lax.broadcasted_iota(I32, (8, LANES), 0)
     names = lax.broadcasted_iota(I32, (256, LANES), 0).astype(F32).astype(BF16)
     one = jnp.ones((256, LANES), BF16)
     none = jnp.zeros((256, LANES), BF16)
-
-    def one_hot(index):
-        tile = jnp.broadcast_to((index[0:1] & 255).astype(F32), (16, LANES)).astype(BF16)
-        return jnp.where(names == jnp.concatenate([tile] * 16, axis=0), one, none)
+    hot = [jnp.where(names == tall_row((i[0:1] & 255).astype(F32), 256), one, none) for i in indices]
+    every = jnp.dot(table_ref[...], jnp.concatenate(hot, axis=1), preferred_element_type=F32)
+    found = []
+    for a, index in enumerate(indices):
+        held = [jnp.zeros((8, LANES), F32)] * 3
+        for high in range(highs):
+            hit = (index >> 8) == high + first_high
+            for v in range(3):
+                at = high * ROWS + v * 8
+                held[v] = jnp.where(hit, every[at : at + 8, a * LANES : (a + 1) * LANES], held[v])
+        first = held[0] + held[2]
+        second = held[1] + jnp.roll(held[1], 4, axis=0)
+        found.append((first, jnp.where(row_ids < 2, jnp.roll(first, 2, axis=0), second)))
+    return found
+
+
+def own_kernel(
+    packed_ref, scale_ref, disp_ref, adj_ref, connect_ref, own_x_ref, own_y_ref, wide_ref, table_ref, *, chunks, groups, highs
+):
+    fill_table(
+        lambda h: disp_ref[pl.ds(h, 6, stride=chunks)], lambda h: adj_ref[pl.ds(h, 6, stride=chunks)], highs, wide_ref, table_ref
+    )
+    xs = scale_ref[0:8]
+    ys = scale_ref[8:16]
 
     def fetch(b):
         rows = connect_ref[:, pl.ds(pl.multiple_of(b * LANES, LANES), LANES)]
         return tuple(jnp.broadcast_to(rows[a : a + 1], (8, LANES)) for a in range(4))
 
     def body(b, indices):
-        hot = jnp.concatenate([one_hot(i) for i in indices], axis=1)
-        every = jnp.dot(table_ref[...], hot, preferred_element_type=F32)
-        for a in range(4):
-            held = [jnp.zeros((8, LANES), F32)] * 3
-            for high in range(highs):
-                hit = (indices[a] >> 8) == high
-                for v in range(3):
-                    at = high * ROWS + v * 8
-                    held[v] = jnp.where(hit, every[at : at + 8, a * LANES : (a + 1) * LANES], held[v])
-            first = held[0] + held[2]
-            second = held[1] + jnp.roll(held[1], 4, axis=0)
-            at = pl.ds(pl.multiple_of(b * 32 + a * 8, 8), 8)
-            near_x_ref[at] = first
-            near_y_ref[at] = jnp.where(row_ids < 2, jnp.roll(first, 2, axis=0), second)
+        near = matrix_pick(table_ref, indices, highs, 0)
         found = pick(
             lambda h: packed_ref[(2 * highs + h) * 8 : (2 * highs + h) * 8 + 8],
             chunks - 2 * highs,
@@ -195,10 +203,19 @@
             True,
         )
         for a in range(4):
-            got_ref[pl.ds(pl.multiple_of(b * 32 + a * 8, 8), 8)] = found[a]
+            x, y = unpack_tile(found[a], xs, ys)
+            first = indices[a] < highs * 256
+            at = pl.ds(pl.multiple_of(b * 32 + a * 8, 8), 8)
+            own_x_ref[at] = jnp.where(first, near[a][0], x)
+            own_y_ref[at] = jnp.where(first, near[a][1], y)
         return fetch(jnp.minimum(b + 1, groups - 1))
 
-    lax.fori_loop(0, groups, body, fetch(jnp.int32(0)))
+    def several(turn, indices):
+        for k in range(4):
+            indices = body(turn * 4 + k, indices)
+        return indices
+
+    lax.fori_loop(0, groups // 4, several, fetch(jnp.int32(0)))
 
 
 def spread_matrix(flip):
@@ -225,10 +242,8 @@
 def main_kernel(
     here_ref,
     recv_ref,
-    packed_scale_ref,
-    got_ref,
-    near_x_ref,
-    near_y_ref,
+    own_x_ref,
+    own_y_ref,
     connect_ref,
     comp_ref,
     dv_ref,
@@ -238,6 +253,8 @@
     k_bend_ref,
     out_ref,
     ghost_ref,
+    wide_ref,
+    table_ref,
     move_ref,
     cost_ref,
     panel_ref,
@@ -252,7 +269,7 @@
     domains,
     iface,
     comps,
-    highs,
+    ghost_highs,
     owned,
     slots,
     cap,
@@ -268,40 +285,37 @@
     def y_of(h):
         return recv_ref[sources[h // rows], (h % rows) * 16 + 8 : (h % rows) * 16 + 14]
 
-    x_inv, x_scale = scales_of(x_of, ghosts, DISP_TOP)
-    y_inv, y_scale = scales_of(y_of, ghosts, ADJ_TOP)
+    fill_table(x_of, y_of, ghost_highs, wide_ref, table_ref)
+    kept = range(2 * ghost_highs, ghosts)
+    x_inv, x_scale = scales_of(x_of, kept, DISP_TOP)
+    y_inv, y_scale = scales_of(y_of, kept, ADJ_TOP)
     gx = pad_rows(x_scale)
     gy = pad_rows(y_scale)
     x_inv = jnp.broadcast_to(x_inv, (6, LANES))
     y_inv = jnp.broadcast_to(y_inv, (6, LANES))
-    for h in range(ghosts):
+    for h in kept:
 
         def store(row, many, value, h=h):
-            ghost_ref[h * 8 + row : h * 8 + row + many] = value
+            at = (h - kept[0]) * 8 + row
+            ghost_ref[at : at + many] = value
 
         pack_tile(x_of(h), y_of(h), x_inv, y_inv, store)
-    ox = packed_scale_ref[0:8]
-    oy = packed_scale_ref[8:16]
     tiles = groups // 8
     panel_ref[...] = jnp.zeros(panel_ref.shape, F32)
-    span = 8
-
-    @pl.loop(0, tiles // 2 * (domains // span))
-    def _(turn):
-        first = turn // (tiles // 2) * span
-        block = lax.rem(turn, tiles // 2) * 16
-        at = [pl.ds(pl.multiple_of(block + u * 8, 8), 8) for u in range(2)]
+
+    def panel_step(tile, first, span):
+        at = pl.ds(pl.multiple_of(tile * 8, 8), 8)
 
         def row_of(h):
             k = h % 16
             row = (k // 4) * 16 + (k % 4 // 2) * 8 + 6 + k % 2
             return jnp.broadcast_to(recv_ref[first + h // 16, row : row + 1], (8, LANES))
 
-        found = pick(
-            row_of, span * 16, first * 16, [dv_ref[at[u]] for u in range(2)], [panel_ref[at[u]] for u in range(2)], False
-        )
-        for u in range(2):
-            panel_ref[at[u]] = found[u]
+        panel_ref[at] = pick(row_of, span * 16, first * 16, [dv_ref[at]], [panel_ref[at]], True)[0]
+
+    @pl.loop(0, domains // 8)
+    def _(turn):
+        panel_step(0, turn * 8, 8)
 
     wide = spread_matrix(False)
     tall = spread_matrix(True)
@@ -324,21 +338,23 @@
         lanes = pl.ds(pl.multiple_of(b * LANES, LANES), LANES)
         rows = connect_ref[:, lanes]
         indices = [jnp.broadcast_to(rows[a : a + 1], (8, LANES)) for a in range(4)]
-        found = pick(
+        found = matrix_pick(table_ref, indices, ghost_highs, own // 2)
+        words = pick(
             lambda h: ghost_ref[h * 8 : h * 8 + 8],
-            ghosts,
-            own,
+            len(kept),
+            own + kept[0],
             indices,
-            [got_ref[pl.ds(pl.multiple_of(b * 32 + a * 8, 8), 8)] for a in range(4)],
+            [jnp.zeros((8, LANES), I32)] * 4,
             True,
         )
         for a in range(4):
+            x, y = unpack_tile(words[a], gx, gy)
             far = indices[a] >= own * LANES
-            x, y = unpack_tile(found[a], jnp.where(far, gx, ox), jnp.where(far, gy, oy))
-            near = indices[a] < highs * 256
+            farther = indices[a] >= (own + kept[0]) * LANES
             at = pl.ds(pl.multiple_of(b * 32 + a * 8, 8), 8)
-            move_ref[a * 8 : a * 8 + 8] = jnp.where(near, near_x_ref[at], x)
-            cost_ref[a * 8 : a * 8 + 8] = jnp.where(near, near_y_ref[at], y)
+            move_ref[a * 8 : a * 8 + 8] = jnp.where(farther, x, jnp.where(far, found[a][0], own_x_ref[at]))
+            cost_ref[a * 8 : a * 8 + 8] = jnp.where(farther, y, jnp.where(far, found[a][1], own_y_ref[at]))
+        panel_step(jnp.minimum(b // 8 + 1, tiles - 1), lax.rem(b, 8) * (domains // 8), domains // 8)
 
     def dense(b):
         x = three_parts(move_ref[...])
@@ -361,12 +377,13 @@
             held = best_ref[c * 8 : c * 8 + 8]
             best_ref[c * 8 : c * 8 + 8] = jnp.maximum(held, jnp.where(away == c * 8, failure, LOW))
 
-    gather(0)
-
-    @pl.loop(1, groups)
-    def _(b):
-        dense(b - 1)
-        gather(b)
+    gather(jnp.int32(0))
+
+    @pl.loop(0, (groups - 1) // 3)
+    def _(turn):
+        for k in range(3):
+            dense(turn * 3 + k)
+            gather(turn * 3 + k + 1)
 
     dense(groups - 1)
 
@@ -583,7 +600,8 @@
 
     disp = displacement.reshape(-1, LANES)
     adj = adjoint.reshape(-1, LANES)
-    highs = min(HIGHS, own // 2)
+    highs = HIGHS
+    ghost_highs = GHOST_HIGHS
 
     packed, scale, send = pl.pallas_call(
         functools.partial(send_kernel, chunks=own, domains=domains, iface=iface),
@@ -593,15 +611,15 @@
         name="send_pick",
     )(here, disp, adj, send_list, thickness.reshape(-1, LANES))
     recv = lax.all_to_all(send, "dom", 0, 0, tiled=True)
-    got, near_x, near_y = pl.pallas_call(
+    own_x, own_y = pl.pallas_call(
         functools.partial(own_kernel, chunks=own, groups=groups, highs=highs),
-        out_shape=(sds((groups * 32, LANES), I32),) + (sds((groups * 32, LANES), F32),) * 2,
-        in_specs=[vmem()] * 4,
-        out_specs=(vmem(),) * 3,
+        out_shape=(sds((groups * 32, LANES), F32),) * 2,
+        in_specs=[vmem()] * 5,
+        out_specs=(vmem(),) * 2,
         scratch_shapes=[pltpu.VMEM((highs * ROWS, 256), F32), pltpu.VMEM((highs * ROWS, 256), BF16)],
         name="own_pick",
         cost_estimate=pl.CostEstimate(flops=0, transcendentals=0, bytes_accessed=60_000_000),
-    )(packed, disp, adj, connect)
+    )(packed, scale, disp, adj, connect)
     comp = elem_comp.reshape(-1, LANES)
     dv = elem_dv.reshape(-1, LANES)
     owned = thickness.shape[0]
@@ -613,16 +631,18 @@
             domains=domains,
             iface=iface,
             comps=comps,
-            highs=highs,
+            ghost_highs=ghost_highs,
             owned=owned,
             slots=SLICE,
             cap=CAP,
         ),
         out_shape=sds((domains * 24, LANES), F32),
-        in_specs=[smem()] + [vmem()] * 12,
+        in_specs=[smem()] + [vmem()] * 10,
         out_specs=vmem(),
         scratch_shapes=[
-            pltpu.VMEM((len(OFFSETS) * iface // LANES * 8, LANES), I32),
+            pltpu.VMEM(((len(OFFSETS) * iface // LANES - 2 * ghost_highs) * 8, LANES), I32),
+            pltpu.VMEM((ghost_highs * ROWS, 256), F32),
+            pltpu.VMEM((ghost_highs * ROWS, 256), BF16),
             pltpu.VMEM((32, LANES), F32),
             pltpu.VMEM((32, LANES), F32),
             pltpu.VMEM((groups, LANES), F32),
@@ -633,7 +653,7 @@
             pltpu.VMEM((1, 8, LANES), F32),
         ],
         name="element_work",
-    )(here, recv, scale, got, near_x, near_y, connect, comp, dv, s_memb, s_bend, k_memb, k_bend)
+    )(here, recv, own_x, own_y, connect, comp, dv, s_memb, s_bend, k_memb, k_bend)
     everyone = lax.all_to_all(mine.reshape(domains, 24, LANES), "dom", 0, 0, tiled=True)
     loads = lax.axis_size("load")
     ks_value, sums = pl.pallas_call(

time: 101 us -> 92.6 us (0.917)
  Pallas kernels: 57.1 us -> 48.3 us
  blocking collectives: 33.1 us -> 31.2 us
  waiting for transfers between devices: 0.01 us -> 1.84 us
    pallas_call x1, Pallas kernels: 20 us -> 15.1 us  [per_device(): pl.pallas_call(functools.partial(own_kernel, chunks=own, groups=groups, h...]
    pallas_call x1, Pallas kernels: 27.4 us -> 23.5 us  [per_device(): pl.pallas_call(functools.partial(main_kernel, own=own, groups=groups, dom...]
    all_to_all x1, blocking collectives: 17.8 us -> 15.9 us  [per_device(): lax.all_to_all(mine.reshape(domains, 24, LANES), 'dom', 0, 0, tiled=True)]
    all_to_all x1, waiting for transfers between devices: 0.01 us -> 1.84 us  [per_device(): recv = lax.all_to_all(send, 'dom', 0, 0, tiled=True)]
  transfers between devices with their start and end apart: 1 -> 1, of which waited for: 0 -> 1; matrix products, arithmetic and copies ran while one was open for 0% -> 0% of each run, Pallas kernels for 20% -> 16%
where the time goes in v4:
time: 92.6 us; the launch traced here: 92.2 us
  Pallas kernels  48.3 us (52%)
  blocking collectives  31.2 us (34%)
  starting transfers between devices  8.58 us (9%)
  waiting for transfers between devices  1.84 us (2%)
  local copies, waits for them, and re-layouts  1 us (1%)
    pallas_call x1, Pallas kernels, per_device(): pl.pallas_call(functools.partial(main_kernel, own=own, groups=groups, dom...  23.5 us
    all_to_all x1, blocking collectives, per_device(): lax.all_to_all(mine.reshape(domains, 24, LANES), 'dom', 0, 0, tiled=True)  15.9 us
    all_to_all x1, blocking collectives, per_device(): lax.all_to_all(sums, 'load', 0, 0, tiled=True).sum(axis=0).reshape(-1)  15.3 us
    pallas_call x1, Pallas kernels, per_device(): pl.pallas_call(functools.partial(own_kernel, chunks=own, groups=groups, h...  15.1 us
    all_to_all x1, starting transfers between devices, per_device(): recv = lax.all_to_all(send, 'dom', 0, 0, tiled=True)  8.58 us
    pallas_call x1, Pallas kernels, per_device(): pl.pallas_call(functools.partial(send_kernel, chunks=own, domains=domains...  5.54 us
    pallas_call x1, Pallas kernels, per_device(): pl.pallas_call(functools.partial(last_kernel, domains=domains, comps=comp...  4.15 us
  transfers between devices with their start and end apart: 1, of which 1 were waited for; matrix products, arithmetic and copies ran while one was open for 0% of the time, Pallas kernels for 16%

profile of v4, /device:TPU:1, one launch (start us, length us, event | category | flops | bytes accessed | tf_op | source)
XLA Modules:
  0.0 92.2 jit_solution(15590565755811044260)
XLA Ops:
  0.6 5.5 %send_pick.1 = (s32[512,128]{1,0:T(8,128)}, f32[16,128]{1,0:T(8,128)}, f32[32,64,128]{2,1,0:T(8,128)}) custom-call(s32[1]{0:T(128)} %bitcast.here_ref, f32[384,128]{1,0:T(8,128)} %bitcast.9, f32[384,128]{1,0:T(8,128)} %bitcast.11, s32[1,32,512]{2,1,0:T(8,128)} %list_ref.1, f32[16,128]{1,0:T(8,128)} %bitcast.15), custom_call_target="tpu_custom_call" | custom-call | tf_op jit(solution)/shard_map/send_pick/pallas_call | solution.py:606
  6.2 8.6 %all-to-all-start = ((f32[32,64,128]{2,1,0:T(8,128)}), f32[32,64,128]{2,1,0:T(8,128)S(1)}, u32[]{:S(2)}, u32[]{:S(2)}) async-start(f32[32,64,128]{2,1,0:T(8,128)} %get-tuple-element.9), calls=%async_computation | async-start | bytes 2097152 | tf_op jit(solution)/shard_map/all_to_all | solution.py:613
  14.8 15.1 %own_pick.1 = (f32[2048,128]{1,0:T(8,128)}, f32[2048,128]{1,0:T(8,128)}) custom-call(s32[512,128]{1,0:T(8,128)} %get-tuple-element.10.packed_ref, f32[16,128]{1,0:T(8,128)} %get-tuple-element.11.scale_ref, f32[384,128]{1,0:T(8,128)} %bitcast.10, f32[384,128]{1,0:T(8,128)} %bitcast.12, s32[4,8192]{1,0:T(4,128)} %connect_ref.3), custom_call_target="tpu_custom_call" | custom-call | bytes 60000000 | tf_op jit(solution)/shard_map/own_pick/pallas_call | solution.py:614
  29.8 1.8 %all-to-all-done.recv_ref = f32[32,64,128]{2,1,0:T(8,128)S(1)} async-done(((f32[32,64,128]{2,1,0:T(8,128)}), f32[32,64,128]{2,1,0:T(8,128)S(1)}, u32[]{:S(2)}, u32[]{:S(2)}) %all-to-all-start) | async-done | bytes 1048608 | tf_op jit(solution)/shard_map/all_to_all | solution.py:613
  31.7 0.0 copy-start
  31.7 1.0 %copy-done = f32[32,64,128]{2,1,0:T(8,128)} copy-done((f32[32,64,128]{2,1,0:T(8,128)}, f32[32,64,128]{2,1,0:T(8,128)S(1)}, u32[]{:S(2)}) %copy-start) | copy-done | bytes 1048600
  32.7 23.5 %element_work.1 = f32[768,128]{1,0:T(8,128)} custom-call(s32[1]{0:T(128)} %bitcast.here_ref, f32[32,64,128]{2,1,0:T(8,128)} %copy-done, f32[2048,128]{1,0:T(8,128)} %get-tuple-element.12.own_x_ref, f32[2048,128]{1,0:T(8,128)} %get-tuple-element.13.own_y_ref, s32[4,8192]{1,0:T(4,128)} %connect_ref.3, s32[64,128]{1,0:T(8,128)} %bitcast.13, ...), custom_call_target="tpu_custom_call" | custom-call | tf_op jit(solution)/shard_map/element_work/pallas_call | solution.py:626
  56.2 15.9 %all_to_all.15.recv_ref = f32[32,24,128]{2,1,0:T(8,128)} all-to-all(f32[32,24,128]{2,1,0:T(8,128)} %bitcast.8), channel_id=1, replica_groups=mesh['load'=8,'dom'=32] {'dom'}, dimensions={0} | all-to-all | bytes 786432 | tf_op jit(solution)/shard_map/all_to_all | solution.py:657
  72.1 4.2 %weigh_and_sum.1 = (f32[1,400]{1,0:T(1,128)}, f32[8,16,128]{2,1,0:T(8,128)}) custom-call(f32[32,24,128]{2,1,0:T(8,128)} %all_to_all.15.recv_ref, f32[1,400]{1,0:T(1,128)} %mult_ref.1), custom_call_target="tpu_custom_call" | custom-call | tf_op jit(solution)/shard_map/weigh_and_sum/pallas_call | solution.py:659
  76.2 15.3 %all_to_all.16 = f32[8,16,128]{2,1,0:T(8,128)S(1)} all-to-all(f32[8,16,128]{2,1,0:T(8,128)} %get-tuple-element.15), channel_id=1, replica_groups=mesh['load'=8,'dom'=32] {'load'}, dimensions={0} | all-to-all | bytes 131072 | tf_op jit(solution)/shard_map/all_to_all | solution.py:667
  91.6 0.6 reduce_sum.9
Async XLA Ops:
  6.2 25.5 %all-to-all-start = ((f32[32,64,128]{2,1,0:T(8,128)}), f32[32,64,128]{2,1,0:T(8,128)S(1)}, u32[]{:S(2)}, u32[]{:S(2)}) async-start(f32[32,64,128]{2,1,0:T(8,128)} %get-tuple-element.9), calls=%async_computation | async-start | bytes 2097152 | tf_op jit(solution)/shard_map/all_to_all | solution.py:613
  31.7 1.0 %copy-start = (f32[32,64,128]{2,1,0:T(8,128)}, f32[32,64,128]{2,1,0:T(8,128)S(1)}, u32[]{:S(2)}) copy-start(f32[32,64,128]{2,1,0:T(8,128)S(1)} %all-to-all-done.recv_ref) | copy-start | bytes 3145732

commit v5 on v4

--- a/solution.py
+++ b/solution.py
@@ -13,6 +13,7 @@
 GHOST_HIGHS = 6
 SLICE = 1024
 CAP = 64
+ROOM = 16 * 1024 * 1024
 SHARP = 50.0
 LOW = -1e30
 LANES = 128
@@ -597,31 +598,42 @@
     groups = elems // LANES
     block = 4 * iface // LANES * 4
     sds = jax.ShapeDtypeStruct
-
-    disp = displacement.reshape(-1, LANES)
-    adj = adjoint.reshape(-1, LANES)
+    near = pltpu.VMEM
+
+    def close(x):
+        return pltpu.with_memory_space_constraint(x, pltpu.VMEM)
+
+    def far(x):
+        return pltpu.with_memory_space_constraint(x, pltpu.HBM)
+
+
+    disp = far(displacement.reshape(-1, LANES))
+    adj = far(adjoint.reshape(-1, LANES))
+    connect = far(connect)
     highs = HIGHS
     ghost_highs = GHOST_HIGHS
 
     packed, scale, send = pl.pallas_call(
         functools.partial(send_kernel, chunks=own, domains=domains, iface=iface),
-        out_shape=(sds((own * 8, LANES), I32), sds((16, LANES), F32), sds((domains, block, LANES), F32)),
+        out_shape=(pltpu.HBM((own * 8, LANES), I32), pltpu.HBM((16, LANES), F32), sds((domains, block, LANES), F32)),
         in_specs=[smem()] + [vmem()] * 4,
         out_specs=(vmem(),) * 3,
+        compiler_params=pltpu.CompilerParams(vmem_limit_bytes=ROOM),
         name="send_pick",
-    )(here, disp, adj, send_list, thickness.reshape(-1, LANES))
+    )(here, disp, adj, far(send_list), far(thickness.reshape(-1, LANES)))
     recv = lax.all_to_all(send, "dom", 0, 0, tiled=True)
     own_x, own_y = pl.pallas_call(
         functools.partial(own_kernel, chunks=own, groups=groups, highs=highs),
-        out_shape=(sds((groups * 32, LANES), F32),) * 2,
+        out_shape=(near((groups * 32, LANES), F32),) * 2,
         in_specs=[vmem()] * 5,
         out_specs=(vmem(),) * 2,
         scratch_shapes=[pltpu.VMEM((highs * ROWS, 256), F32), pltpu.VMEM((highs * ROWS, 256), BF16)],
+        compiler_params=pltpu.CompilerParams(vmem_limit_bytes=ROOM),
         name="own_pick",
         cost_estimate=pl.CostEstimate(flops=0, transcendentals=0, bytes_accessed=60_000_000),
-    )(packed, scale, disp, adj, connect)
-    comp = elem_comp.reshape(-1, LANES)
-    dv = elem_dv.reshape(-1, LANES)
+    )(far(packed), far(scale), disp, adj, connect)
+    comp = far(elem_comp.reshape(-1, LANES))
+    dv = far(elem_dv.reshape(-1, LANES))
     owned = thickness.shape[0]
     mine = pl.pallas_call(
         functools.partial(
@@ -636,7 +648,7 @@
             slots=SLICE,
             cap=CAP,
         ),
-        out_shape=sds((domains * 24, LANES), F32),
+        out_shape=near((domains * 24, LANES), F32),
         in_specs=[smem()] + [vmem()] * 10,
         out_specs=vmem(),
         scratch_shapes=[
@@ -652,18 +664,20 @@
             pltpu.VMEM((groups, LANES), F32),
             pltpu.VMEM((1, 8, LANES), F32),
         ],
+        compiler_params=pltpu.CompilerParams(vmem_limit_bytes=ROOM),
         name="element_work",
-    )(here, recv, own_x, own_y, connect, comp, dv, s_memb, s_bend, k_memb, k_bend)
+    )(here, close(recv), close(own_x), close(own_y), connect, comp, dv, far(s_memb), far(s_bend), far(k_memb), far(k_bend))
     everyone = lax.all_to_all(mine.reshape(domains, 24, LANES), "dom", 0, 0, tiled=True)
     loads = lax.axis_size("load")
     ks_value, sums = pl.pallas_call(
         functools.partial(last_kernel, domains=domains, comps=comps, owned=owned),
-        out_shape=(sds((1, comps), F32), sds((loads, owned // LANES, LANES), F32)),
+        out_shape=(sds((1, comps), F32), near((loads, owned // LANES, LANES), F32)),
         in_specs=[vmem()] * 2,
         out_specs=(vmem(),) * 2,
         scratch_shapes=[pltpu.VMEM((owned * 2 // LANES, LANES), F32)],
+        compiler_params=pltpu.CompilerParams(vmem_limit_bytes=ROOM),
         name="weigh_and_sum",
-    )(everyone, multiplier)
+    )(close(everyone), far(multiplier))
     sensitivity = lax.all_to_all(sums, "load", 0, 0, tiled=True).sum(axis=0).reshape(-1)
     return ks_value, sensitivity
 

time: 92.6 us -> 87.1 us (0.941)
  Pallas kernels: 48.3 us -> 44.3 us
  blocking collectives: 31.2 us -> 29.4 us
  waiting for transfers between devices: 1.84 us -> 3.17 us
  local copies, waits for them, and re-layouts: 1 us -> 0 us
    pallas_call x1, Pallas kernels: 23.5 us -> 21.6 us  [per_device(): pl.pallas_call(functools.partial(main_kernel, own=own, groups=groups, dom...]
    all_to_all x1, blocking collectives: 15.9 us -> 14.3 us  [per_device(): lax.all_to_all(mine.reshape(domains, 24, LANES), 'dom', 0, 0, tiled=True)]
    pallas_call x1, Pallas kernels: 15.1 us -> 13.7 us  [per_device(): pl.pallas_call(functools.partial(own_kernel, chunks=own, groups=groups, h...]
    all_to_all x1, waiting for transfers between devices: 1.84 us -> 3.17 us  [per_device(): recv = lax.all_to_all(send, 'dom', 0, 0, tiled=True)]
    unnamed x2 -> x0, local copies, waits for them, and re-layouts: 1 us -> none
where the time goes in v5:
time: 87.1 us; the launch traced here: 86.8 us
  Pallas kernels  44.3 us (51%)
  blocking collectives  29.4 us (34%)
  starting transfers between devices  8.58 us (10%)
  waiting for transfers between devices  3.17 us (4%)
    pallas_call x1, Pallas kernels, per_device(): pl.pallas_call(functools.partial(main_kernel, own=own, groups=groups, dom...  21.6 us
    all_to_all x1, blocking collectives, per_device(): lax.all_to_all(sums, 'load', 0, 0, tiled=True).sum(axis=0).reshape(-1)  15.1 us
    all_to_all x1, blocking collectives, per_device(): lax.all_to_all(mine.reshape(domains, 24, LANES), 'dom', 0, 0, tiled=True)  14.3 us
    pallas_call x1, Pallas kernels, per_device(): pl.pallas_call(functools.partial(own_kernel, chunks=own, groups=groups, h...  13.7 us
    all_to_all x1, starting transfers between devices, per_device(): recv = lax.all_to_all(send, 'dom', 0, 0, tiled=True)  8.58 us
    pallas_call x1, Pallas kernels, per_device(): pl.pallas_call(functools.partial(send_kernel, chunks=own, domains=domains...  5.52 us
    pallas_call x1, Pallas kernels, per_device(): pl.pallas_call(functools.partial(last_kernel, domains=domains, comps=comp...  3.43 us
    all_to_all x1, waiting for transfers between devices, per_device(): recv = lax.all_to_all(send, 'dom', 0, 0, tiled=True)  3.17 us
  transfers between devices with their start and end apart: 1, of which 1 were waited for; matrix products, arithmetic and copies ran while one was open for 0% of the time, Pallas kernels for 16%

profile of v5, /device:TPU:1, one launch (start us, length us, event | category | flops | bytes accessed | tf_op | source)
XLA Modules:
  0.0 86.8 jit_solution(2446679966237246696)
XLA Ops:
  0.6 5.5 %send_pick.1 = (s32[512,128]{1,0:T(8,128)}, f32[16,128]{1,0:T(8,128)}, f32[32,64,128]{2,1,0:T(8,128)}) custom-call(s32[1]{0:T(128)} %bitcast.here_ref, f32[384,128]{1,0:T(8,128)} %bitcast.9, f32[384,128]{1,0:T(8,128)} %bitcast.11, s32[1,32,512]{2,1,0:T(8,128)} %list_ref.1, f32[16,128]{1,0:T(8,128)} %bitcast.15), custom_call_target="tpu_custom_call" | custom-call | tf_op jit(solution)/shard_map/send_pick/pallas_call | solution.py:616
  6.2 8.6 %all-to-all-start = ((f32[32,64,128]{2,1,0:T(8,128)}), f32[32,64,128]{2,1,0:T(8,128)S(1)}, u32[]{:S(2)}, u32[]{:S(2)}) async-start(f32[32,64,128]{2,1,0:T(8,128)} %get-tuple-element.9), calls=%async_computation | async-start | bytes 2097152 | tf_op jit(solution)/shard_map/all_to_all | solution.py:624
  14.7 13.7 %own_pick.1 = (f32[2048,128]{1,0:T(8,128)S(1)}, f32[2048,128]{1,0:T(8,128)S(1)}) custom-call(s32[512,128]{1,0:T(8,128)} %get-tuple-element.10.packed_ref, f32[16,128]{1,0:T(8,128)} %get-tuple-element.11.scale_ref, f32[384,128]{1,0:T(8,128)} %bitcast.10, f32[384,128]{1,0:T(8,128)} %bitcast.12, s32[4,8192]{1,0:T(4,128)} %connect_ref.3), custom_call_target="tpu_custom_call" | custom-call | bytes 60000000 | tf_op jit(solution)/shard_map/own_pick/pallas_call | solution.py:625
  28.5 3.2 %all-to-all-done.recv_ref = f32[32,64,128]{2,1,0:T(8,128)S(1)} async-done(((f32[32,64,128]{2,1,0:T(8,128)}), f32[32,64,128]{2,1,0:T(8,128)S(1)}, u32[]{:S(2)}, u32[]{:S(2)}) %all-to-all-start) | async-done | bytes 1048608 | tf_op jit(solution)/shard_map/all_to_all | solution.py:624
  31.6 21.6 %element_work.1 = f32[768,128]{1,0:T(8,128)S(1)} custom-call(s32[1]{0:T(128)} %bitcast.here_ref, f32[32,64,128]{2,1,0:T(8,128)S(1)} %all-to-all-done.recv_ref, f32[2048,128]{1,0:T(8,128)S(1)} %get-tuple-element.12.own_x_ref, f32[2048,128]{1,0:T(8,128)S(1)} %get-tuple-element.13.own_y_ref, s32[4,8192]{1,0:T(4,128)} %connect_ref.3, s32[64,128]{1,0:T(8,128)} %bitcast.13, ...), custom_call_target="tpu_custom_call" | custom-call | tf_op jit(solution)/shard_map/element_work/pallas_call | solution.py:638
  53.3 14.3 %all_to_all.15.recv_ref = f32[32,24,128]{2,1,0:T(8,128)S(1)} all-to-all(f32[32,24,128]{2,1,0:T(8,128)S(1)} %bitcast.8), channel_id=1, replica_groups=mesh['load'=8,'dom'=32] {'dom'}, dimensions={0} | all-to-all | bytes 786432 | tf_op jit(solution)/shard_map/all_to_all | solution.py:670
  67.6 3.4 %weigh_and_sum.1 = (f32[1,400]{1,0:T(1,128)}, f32[8,16,128]{2,1,0:T(8,128)S(1)}) custom-call(f32[32,24,128]{2,1,0:T(8,128)S(1)} %all_to_all.15.recv_ref, f32[1,400]{1,0:T(1,128)} %mult_ref.1), custom_call_target="tpu_custom_call" | custom-call | tf_op jit(solution)/shard_map/weigh_and_sum/pallas_call | solution.py:672
  71.0 15.1 %all_to_all.16 = f32[8,16,128]{2,1,0:T(8,128)S(1)} all-to-all(f32[8,16,128]{2,1,0:T(8,128)S(1)} %get-tuple-element.15), channel_id=1, replica_groups=mesh['load'=8,'dom'=32] {'load'}, dimensions={0} | all-to-all | bytes 131072 | tf_op jit(solution)/shard_map/all_to_all | solution.py:681
  86.1 0.6 reduce_sum.9
Async XLA Ops:
  6.2 25.5 %all-to-all-start = ((f32[32,64,128]{2,1,0:T(8,128)}), f32[32,64,128]{2,1,0:T(8,128)S(1)}, u32[]{:S(2)}, u32[]{:S(2)}) async-start(f32[32,64,128]{2,1,0:T(8,128)} %get-tuple-element.9), calls=%async_computation | async-start | bytes 2097152 | tf_op jit(solution)/shard_map/all_to_all | solution.py:624

commit v6 on v5

--- a/solution.py
+++ b/solution.py
@@ -9,7 +9,7 @@
 
 NBR = 3
 ROWS = 24
-HIGHS = 14
+HIGHS = 18
 GHOST_HIGHS = 6
 SLICE = 1024
 CAP = 64
@@ -78,7 +78,23 @@
     return found
 
 
-def send_kernel(here_ref, disp_ref, adj_ref, list_ref, thick_ref, packed_ref, scale_ref, send_ref, *, chunks, domains, iface):
+def send_kernel(
+    here_ref,
+    disp_ref,
+    adj_ref,
+    list_ref,
+    thick_ref,
+    packed_ref,
+    scale_ref,
+    table_ref,
+    send_ref,
+    wide_ref,
+    *,
+    chunks,
+    domains,
+    iface,
+    highs,
+):
     rows = iface // LANES
     cut = lambda ref, h: ref[pl.ds(h, 6, stride=chunks)]
     x_inv, x_scale = scales_of(lambda h: cut(disp_ref, h), range(chunks), DISP_TOP)
@@ -109,37 +125,25 @@
 
     here = here_ref[0]
     row_ids = lax.broadcasted_iota(I32, (8, LANES), 0)
-    turns = len(OFFSETS) * rows // 2
-
-    def target_of(turn):
-        j = turn // (rows // 2)
-        offset = j - NBR + jnp.where(j >= NBR, 1, 0)
-        return lax.rem(here - offset + domains, domains)
-
-    def fetch(turn):
-        target = target_of(turn)
-        base = pl.multiple_of(target // 8 * 8, 8)
-        found = []
-        for u in range(2):
-            k = lax.rem(turn, rows // 2) * 2 + u
-            tile = list_ref[0, pl.ds(base, 8), pl.ds(pl.multiple_of(k * LANES, LANES), LANES)]
-            row = jnp.sum(jnp.where(row_ids == target - base, tile, 0), axis=0, keepdims=True)
-            found.append(jnp.broadcast_to(row, (8, LANES)))
-        return tuple(found)
-
-    def body(turn, indices):
-        target = target_of(turn)
-        picked = pick(
-            lambda h: packed_ref[h * 8 : h * 8 + 8], chunks, 0, indices, [jnp.zeros((8, LANES), I32)] * 2, False
-        )
-        for u in range(2):
-            k = lax.rem(turn, rows // 2) * 2 + u
-            for half, value in enumerate(unpack_tile(picked[u], xs, ys)):
-                at = pl.ds(pl.multiple_of(k * 16 + half * 8, 8), 8)
-                send_ref[target, at] = jnp.where(row_ids < 6, value, send_ref[target, at])
-        return fetch(jnp.minimum(turn + 1, turns - 1))
-
-    lax.fori_loop(0, turns, body, fetch(jnp.int32(0)))
+    fill_table(lambda h: cut(disp_ref, h), lambda h: cut(adj_ref, h), highs, wide_ref, table_ref)
+
+    @pl.loop(0, len(OFFSETS) // 3)
+    def _(turn):
+        for step in range(3):
+            j = turn * 3 + step
+            offset = j - NBR + jnp.where(j >= NBR, 1, 0)
+            target = lax.rem(here - offset + domains, domains)
+            base = pl.multiple_of(target // 8 * 8, 8)
+            indices = []
+            for k in range(rows):
+                tile = list_ref[0, pl.ds(base, 8), k * LANES : (k + 1) * LANES]
+                row = jnp.sum(jnp.where(row_ids == target - base, tile, 0), axis=0, keepdims=True)
+                indices.append(jnp.broadcast_to(row, (8, LANES)))
+            found = hybrid_pick(packed_ref, table_ref, indices, chunks, highs, xs, ys)
+            for k in range(rows):
+                for half in range(2):
+                    at = slice(k * 16 + half * 8, k * 16 + half * 8 + 8)
+                    send_ref[target, at] = jnp.where(row_ids < 6, found[k][half], send_ref[target, at])
 
 
 def fill_table(x_of, y_of, highs, wide_ref, table_ref):
@@ -180,11 +184,50 @@
     return found
 
 
+def hybrid_pick(packed_ref, table_ref, indices, chunks, highs, xs, ys):
+    near = matrix_pick(table_ref, indices, highs, 0)
+    words = pick(
+        lambda h: packed_ref[(2 * highs + h) * 8 : (2 * highs + h) * 8 + 8],
+        chunks - 2 * highs,
+        2 * highs,
+        indices,
+        [jnp.zeros((8, LANES), I32)] * len(indices),
+        True,
+    )
+    found = []
+    for a, index in enumerate(indices):
+        first = index < highs * 256
+        x, y = unpack_tile(words[a], xs, ys)
+        found.append((jnp.where(first, near[a][0], x), jnp.where(first, near[a][1], y)))
+    return found
+
+
 def own_kernel(
-    packed_ref, scale_ref, disp_ref, adj_ref, connect_ref, own_x_ref, own_y_ref, wide_ref, table_ref, *, chunks, groups, highs
+    packed_ref,
+    scale_ref,
+    table_ref,
+    connect_ref,
+    comp_ref,
+    dv_ref,
+    own_x_ref,
+    own_y_ref,
+    rank_ref,
+    ids_ref,
+    *,
+    chunks,
+    groups,
+    highs,
+    **sizes,
 ):
-    fill_table(
-        lambda h: disp_ref[pl.ds(h, 6, stride=chunks)], lambda h: adj_ref[pl.ds(h, 6, stride=chunks)], highs, wide_ref, table_ref
+    slot_loop(
+        dv_ref,
+        lambda row, place: ((place & (sizes["owned"] - 1)).astype(F32), comp_ref[row].astype(F32)),
+        None,
+        rank_ref,
+        ids_ref,
+        8,
+        groups=groups,
+        **sizes,
     )
     xs = scale_ref[0:8]
     ys = scale_ref[8:16]
@@ -194,21 +237,11 @@
         return tuple(jnp.broadcast_to(rows[a : a + 1], (8, LANES)) for a in range(4))
 
     def body(b, indices):
-        near = matrix_pick(table_ref, indices, highs, 0)
-        found = pick(
-            lambda h: packed_ref[(2 * highs + h) * 8 : (2 * highs + h) * 8 + 8],
-            chunks - 2 * highs,
-            2 * highs,
-            indices,
-            [jnp.zeros((8, LANES), I32)] * 4,
-            True,
-        )
+        found = hybrid_pick(packed_ref, table_ref, indices, chunks, highs, xs, ys)
         for a in range(4):
-            x, y = unpack_tile(found[a], xs, ys)
-            first = indices[a] < highs * 256
             at = pl.ds(pl.multiple_of(b * 32 + a * 8, 8), 8)
-            own_x_ref[at] = jnp.where(first, near[a][0], x)
-            own_y_ref[at] = jnp.where(first, near[a][1], y)
+            own_x_ref[at] = found[a][0]
+            own_y_ref[at] = found[a][1]
         return fetch(jnp.minimum(b + 1, groups - 1))
 
     def several(turn, indices):
@@ -217,6 +250,65 @@
         return indices
 
     lax.fori_loop(0, groups // 4, several, fetch(jnp.int32(0)))
+
+
+def slot_loop(dv_ref, values_of, rank_ref, write_rank_ref, out_ref, stride, *, domains, groups, owned, slots, cap):
+    shift = owned.bit_length() - 1
+    owner_ids = lax.broadcasted_iota(I32, (domains, LANES), 0)
+    owner_names = owner_ids.astype(F32).astype(BF16)
+    rank_names = lax.broadcasted_iota(I32, (cap, LANES), 0).astype(F32).astype(BF16)
+    one = jnp.ones((cap, LANES), BF16)
+    zero = jnp.zeros((cap, LANES), BF16)
+    none = jnp.zeros((domains, LANES), BF16)
+    before = lax.broadcasted_iota(I32, (LANES, LANES), 0) < lax.broadcasted_iota(I32, (LANES, LANES), 1)
+    before = jnp.concatenate(
+        [jnp.where(before, 1.0, 0.0).astype(BF16), jnp.ones((LANES, LANES), BF16)], axis=1
+    )
+    block_rows = slots // LANES
+
+    def ranks_of(places):
+        owners = [jnp.where(owner_ids == (place >> shift), 1.0, 0.0) for place in places]
+        counts = jnp.dot(
+            jnp.concatenate([o.astype(BF16) for o in owners], axis=0), before, preferred_element_type=F32
+        )
+        base = jnp.zeros((domains, LANES), F32)
+        ranks = []
+        for j in range(block_rows):
+            count = counts[j * domains : (j + 1) * domains]
+            ranks.append(jnp.sum(owners[j] * (count[:, 0:LANES] + base), axis=0, keepdims=True))
+            base = base + count[:, LANES : 2 * LANES]
+        return ranks
+
+    @pl.loop(0, groups // (2 * block_rows))
+    def _(pair):
+        sums = []
+        for parity in range(2):
+            rows = [pl.ds(pair * 2 * block_rows + parity * block_rows + j, 1) for j in range(block_rows)]
+            places = [dv_ref[row] for row in rows]
+            ranks = [rank_ref[row] for row in rows] if write_rank_ref is None else ranks_of(places)
+            left = []
+            right = []
+            for row, place, rank in zip(rows, places, ranks):
+                if write_rank_ref is not None:
+                    write_rank_ref[row] = rank
+                right.append(jnp.where(rank_names == tall_row(rank, cap), one, zero))
+                hit = owner_names == tall_row((place >> shift).astype(F32), domains)
+                pieces = []
+                for value in values_of(row, place):
+                    rough = value.astype(BF16).astype(F32)
+                    pieces.append(jnp.where(hit, tall_row(rough, domains), none))
+                    pieces.append(jnp.where(hit, tall_row(value - rough, domains), none))
+                left.append(jnp.concatenate(pieces, axis=0))
+            moved = lax.dot_general(
+                jnp.concatenate(left, axis=1),
+                jnp.concatenate(right, axis=1),
+                (((1,), (1,)), ((), ())),
+                preferred_element_type=F32,
+            )
+            parts = [moved[p * domains : (p + 1) * domains] for p in range(4)]
+            sums.append([parts[2 * v] + parts[2 * v + 1] for v in range(2)])
+        for v in range(2):
+            out_ref[pl.ds(v * 4 + pair, domains, stride=stride)] = jnp.concatenate([sums[0][v], sums[1][v]], axis=1)
 
 
 def spread_matrix(flip):
@@ -245,6 +337,8 @@
     recv_ref,
     own_x_ref,
     own_y_ref,
+    rank_ref,
+    ids_ref,
     connect_ref,
     comp_ref,
     dv_ref,
@@ -256,8 +350,6 @@
     ghost_ref,
     wide_ref,
     table_ref,
-    move_ref,
-    cost_ref,
     panel_ref,
     fail_ref,
     best_ref,
@@ -340,6 +432,8 @@
         rows = connect_ref[:, lanes]
         indices = [jnp.broadcast_to(rows[a : a + 1], (8, LANES)) for a in range(4)]
         found = matrix_pick(table_ref, indices, ghost_highs, own // 2)
+        moves = []
+        costs = []
         words = pick(
             lambda h: ghost_ref[h * 8 : h * 8 + 8],
             len(kept),
@@ -353,12 +447,13 @@
             far = indices[a] >= own * LANES
             farther = indices[a] >= (own + kept[0]) * LANES
             at = pl.ds(pl.multiple_of(b * 32 + a * 8, 8), 8)
-            move_ref[a * 8 : a * 8 + 8] = jnp.where(farther, x, jnp.where(far, found[a][0], own_x_ref[at]))
-            cost_ref[a * 8 : a * 8 + 8] = jnp.where(farther, y, jnp.where(far, found[a][1], own_y_ref[at]))
+            moves.append(jnp.where(farther, x, jnp.where(far, found[a][0], own_x_ref[at])))
+            costs.append(jnp.where(farther, y, jnp.where(far, found[a][1], own_y_ref[at])))
         panel_step(jnp.minimum(b // 8 + 1, tiles - 1), lax.rem(b, 8) * (domains // 8), domains // 8)
-
-    def dense(b):
-        x = three_parts(move_ref[...])
+        return jnp.concatenate(moves, axis=0), jnp.concatenate(costs, axis=0)
+
+    def dense(b, found):
+        x = three_parts(found[0])
         part = jnp.dot(
             stacked_weights,
             jnp.concatenate([x[0], x[1], x[0], x[2], x[1], x[0]], axis=0),
@@ -371,22 +466,21 @@
         failure = jnp.sum(stress * stress, axis=0, keepdims=True) / 8.0
         slope_ref[row] = jnp.sum(stress * bending, axis=0, keepdims=True) * (2.0 / 8.0)
         stiff = part[16:48] + (3.0 * panel * panel) * part[48:80]
-        fixed_ref[row] = jnp.sum(cost_ref[...] * stiff, axis=0, keepdims=True)
+        fixed_ref[row] = jnp.sum(found[1] * stiff, axis=0, keepdims=True)
         fail_ref[row] = failure
         away = comp_ref[row] - names
         for c in range(combs):
             held = best_ref[c * 8 : c * 8 + 8]
             best_ref[c * 8 : c * 8 + 8] = jnp.maximum(held, jnp.where(away == c * 8, failure, LOW))
 
-    gather(jnp.int32(0))
-
-    @pl.loop(0, (groups - 1) // 3)
-    def _(turn):
+    def several(turn, found):
         for k in range(3):
-            dense(turn * 3 + k)
-            gather(turn * 3 + k + 1)
-
-    dense(groups - 1)
+            later = gather(turn * 3 + k + 1)
+            dense(turn * 3 + k, found)
+            found = later
+        return found
+
+    dense(groups - 1, lax.fori_loop(0, (groups - 1) // 3, several, gather(jnp.int32(0))))
 
     stats_ref[0] = jnp.zeros((8, LANES), F32)
     bands = (comps + LANES - 1) // LANES
@@ -432,64 +526,22 @@
             best_ref[at : at + 8] = totals[c]
     to_rows(jnp.sum, 4)
 
-    shift = owned.bit_length() - 1
-    owner_ids = lax.broadcasted_iota(I32, (domains, LANES), 0)
-    owner_names = owner_ids.astype(F32).astype(BF16)
-    rank_names = lax.broadcasted_iota(I32, (cap, LANES), 0).astype(F32).astype(BF16)
-    one = jnp.ones((cap, LANES), BF16)
-    zero = jnp.zeros((cap, LANES), BF16)
-    none = jnp.zeros((domains, LANES), BF16)
-    before = lax.broadcasted_iota(I32, (LANES, LANES), 0) < lax.broadcasted_iota(I32, (LANES, LANES), 1)
-    before = jnp.concatenate(
-        [jnp.where(before, 1.0, 0.0).astype(BF16), jnp.ones((LANES, LANES), BF16)], axis=1
+    slot_loop(
+        dv_ref,
+        lambda row, place: (fixed_ref[row], slope_ref[row]),
+        rank_ref,
+        None,
+        out_ref,
+        24,
+        domains=domains,
+        groups=groups,
+        owned=owned,
+        slots=slots,
+        cap=cap,
     )
-    block_rows = slots // LANES
-
-    @pl.loop(0, groups // (2 * block_rows))
-    def _(pair):
-        sums = []
-        for parity in range(2):
-            at = [pair * 2 * block_rows + parity * block_rows + j for j in range(block_rows)]
-            places = [dv_ref[pl.ds(r, 1)] for r in at]
-            owners = [jnp.where(owner_ids == (place >> shift), 1.0, 0.0) for place in places]
-            counts = jnp.dot(
-                jnp.concatenate([o.astype(BF16) for o in owners], axis=0), before, preferred_element_type=F32
-            )
-            base = jnp.zeros((domains, LANES), F32)
-            left = []
-            right = []
-            for j in range(block_rows):
-                count = counts[j * domains : (j + 1) * domains]
-                rank = jnp.sum(owners[j] * (count[:, 0:LANES] + base), axis=0, keepdims=True)
-                base = base + count[:, LANES : 2 * LANES]
-                right.append(jnp.where(rank_names == tall_row(rank, cap), one, zero))
-                hit = owner_names == tall_row((places[j] >> shift).astype(F32), domains)
-                row = pl.ds(at[j], 1)
-                values = (
-                    fixed_ref[row],
-                    slope_ref[row],
-                    (places[j] & (owned - 1)).astype(F32),
-                    comp_ref[row].astype(F32),
-                )
-                pieces = []
-                for value in values:
-                    rough = value.astype(BF16).astype(F32)
-                    pieces.append(jnp.where(hit, tall_row(rough, domains), none))
-                    pieces.append(jnp.where(hit, tall_row(value - rough, domains), none))
-                left.append(jnp.concatenate(pieces, axis=0))
-            moved = lax.dot_general(
-                jnp.concatenate(left, axis=1),
-                jnp.concatenate(right, axis=1),
-                (((1,), (1,)), ((), ())),
-                preferred_element_type=F32,
-            )
-            parts = [moved[p * domains : (p + 1) * domains] for p in range(8)]
-            sums.append([parts[2 * v] + parts[2 * v + 1] for v in range(4)])
-        for v in range(4):
-            out_ref[pl.ds(v * 4 + pair, domains, stride=24)] = jnp.concatenate([sums[0][v], sums[1][v]], axis=1)
-
     mine = stats_ref[0]
     for d in range(domains):
+        out_ref[d * 24 + 8 : d * 24 + 16] = ids_ref[d * 8 : d * 8 + 8]
         out_ref[d * 24 + 16 : d * 24 + 24] = mine
 
 
@@ -613,28 +665,35 @@
     highs = HIGHS
     ghost_highs = GHOST_HIGHS
 
-    packed, scale, send = pl.pallas_call(
-        functools.partial(send_kernel, chunks=own, domains=domains, iface=iface),
-        out_shape=(pltpu.HBM((own * 8, LANES), I32), pltpu.HBM((16, LANES), F32), sds((domains, block, LANES), F32)),
+    packed, scale, table, send = pl.pallas_call(
+        functools.partial(send_kernel, chunks=own, domains=domains, iface=iface, highs=highs),
+        out_shape=(
+            pltpu.HBM((own * 8, LANES), I32),
+            pltpu.HBM((16, LANES), F32),
+            pltpu.HBM((highs * ROWS, 256), BF16),
+            sds((domains, block, LANES), F32),
+        ),
         in_specs=[smem()] + [vmem()] * 4,
-        out_specs=(vmem(),) * 3,
+        out_specs=(vmem(),) * 4,
+        scratch_shapes=[pltpu.VMEM((highs * ROWS, 256), F32)],
         compiler_params=pltpu.CompilerParams(vmem_limit_bytes=ROOM),
         name="send_pick",
     )(here, disp, adj, far(send_list), far(thickness.reshape(-1, LANES)))
     recv = lax.all_to_all(send, "dom", 0, 0, tiled=True)
-    own_x, own_y = pl.pallas_call(
-        functools.partial(own_kernel, chunks=own, groups=groups, highs=highs),
-        out_shape=(near((groups * 32, LANES), F32),) * 2,
-        in_specs=[vmem()] * 5,
-        out_specs=(vmem(),) * 2,
-        scratch_shapes=[pltpu.VMEM((highs * ROWS, 256), F32), pltpu.VMEM((highs * ROWS, 256), BF16)],
+    comp = far(elem_comp.reshape(-1, LANES))
+    dv = far(elem_dv.reshape(-1, LANES))
+    owned = thickness.shape[0]
+    own_x, own_y, ranks, ids = pl.pallas_call(
+        functools.partial(
+            own_kernel, chunks=own, groups=groups, highs=highs, domains=domains, owned=owned, slots=SLICE, cap=CAP
+        ),
+        out_shape=(near((groups * 32, LANES), F32),) * 2 + (near((groups, LANES), F32), near((domains * 8, LANES), F32)),
+        in_specs=[vmem()] * 6,
+        out_specs=(vmem(),) * 4,
         compiler_params=pltpu.CompilerParams(vmem_limit_bytes=ROOM),
         name="own_pick",
         cost_estimate=pl.CostEstimate(flops=0, transcendentals=0, bytes_accessed=60_000_000),
-    )(far(packed), far(scale), disp, adj, connect)
-    comp = far(elem_comp.reshape(-1, LANES))
-    dv = far(elem_dv.reshape(-1, LANES))
-    owned = thickness.shape[0]
+    )(far(packed), far(scale), far(table), connect, comp, dv)
     mine = pl.pallas_call(
         functools.partial(
             main_kernel,
@@ -649,14 +708,12 @@
             cap=CAP,
         ),
         out_shape=near((domains * 24, LANES), F32),
-        in_specs=[smem()] + [vmem()] * 10,
+        in_specs=[smem()] + [vmem()] * 12,
         out_specs=vmem(),
         scratch_shapes=[
             pltpu.VMEM(((len(OFFSETS) * iface // LANES - 2 * ghost_highs) * 8, LANES), I32),
             pltpu.VMEM((ghost_highs * ROWS, 256), F32),
             pltpu.VMEM((ghost_highs * ROWS, 256), BF16),
-            pltpu.VMEM((32, LANES), F32),
-            pltpu.VMEM((32, LANES), F32),
             pltpu.VMEM((groups, LANES), F32),
             pltpu.VMEM((groups, LANES), F32),
             pltpu.VMEM((comps, LANES), F32),
@@ -666,7 +723,7 @@
         ],
         compiler_params=pltpu.CompilerParams(vmem_limit_bytes=ROOM),
         name="element_work",
-    )(here, close(recv), close(own_x), close(own_y), connect, comp, dv, far(s_memb), far(s_bend), far(k_memb), far(k_bend))
+    )(here, close(recv), close(own_x), close(own_y), close(ranks), close(ids), connect, comp, dv, far(s_memb), far(s_bend), far(k_memb), far(k_bend))
     everyone = lax.all_to_all(mine.reshape(domains, 24, LANES), "dom", 0, 0, tiled=True)
     loads = lax.axis_size("load")
     ks_value, sums = pl.pallas_call(

time: 87.1 us -> 82.4 us (0.946)
  Pallas kernels: 44.3 us -> 39.6 us
    pallas_call x1, Pallas kernels: 21.6 us -> 18.3 us  [per_device(): pl.pallas_call(functools.partial(main_kernel, own=own, groups=groups, dom...]
    pallas_call x1, Pallas kernels: 5.52 us -> 4.18 us  [per_device(): pl.pallas_call(functools.partial(send_kernel, chunks=own, domains=domains...]
  transfers between devices with their start and end apart: 1 -> 1, of which waited for: 1 -> 1; matrix products, arithmetic and copies ran while one was open for 0% -> 0% of each run, Pallas kernels for 16% -> 17%
where the time goes in v6:
time: 82.4 us; the launch traced here: 82 us
  Pallas kernels  39.6 us (48%)
  blocking collectives  29.3 us (36%)
  starting transfers between devices  8.57 us (10%)
  waiting for transfers between devices  3.26 us (4%)
    pallas_call x1, Pallas kernels, per_device(): pl.pallas_call(functools.partial(main_kernel, own=own, groups=groups, dom...  18.3 us
    all_to_all x1, blocking collectives, per_device(): lax.all_to_all(sums, 'load', 0, 0, tiled=True).sum(axis=0).reshape(-1)  15.1 us
    all_to_all x1, blocking collectives, per_device(): lax.all_to_all(mine.reshape(domains, 24, LANES), 'dom', 0, 0, tiled=True)  14.2 us
    pallas_call x1, Pallas kernels, per_device(): pl.pallas_call(functools.partial(own_kernel, chunks=own, groups=groups, h...  13.6 us
    all_to_all x1, starting transfers between devices, per_device(): recv = lax.all_to_all(send, 'dom', 0, 0, tiled=True)  8.57 us
    pallas_call x1, Pallas kernels, per_device(): pl.pallas_call(functools.partial(send_kernel, chunks=own, domains=domains...  4.18 us
    pallas_call x1, Pallas kernels, per_device(): pl.pallas_call(functools.partial(last_kernel, domains=domains, comps=comp...  3.42 us
    all_to_all x1, waiting for transfers between devices, per_device(): recv = lax.all_to_all(send, 'dom', 0, 0, tiled=True)  3.26 us
  transfers between devices with their start and end apart: 1, of which 1 were waited for; matrix products, arithmetic and copies ran while one was open for 0% of the time, Pallas kernels for 17%

profile of v6, /device:TPU:1, one launch (start us, length us, event | category | flops | bytes accessed | tf_op | source)
XLA Modules:
  0.0 82.0 jit_solution(11824433704725785972)
XLA Ops:
  0.6 4.2 %send_pick.1 = (s32[512,128]{1,0:T(8,128)}, f32[16,128]{1,0:T(8,128)}, bf16[432,256]{1,0:T(8,128)(2,1)}, f32[32,64,128]{2,1,0:T(8,128)}) custom-call(s32[1]{0:T(128)} %bitcast.here_ref, f32[384,128]{1,0:T(8,128)} %bitcast.9, f32[384,128]{1,0:T(8,128)} %bitcast.10, s32[1,32,512]{2,1,0:T(8,128)} %list_ref.1, f32[16,128]{1,0:T(8,128)} %bitcast.15), custom_call_target="tpu_custom_call" | custom-call | tf_op jit(solution)/shard_map/send_pick/pallas_call | solution.py:668
  4.8 8.6 %all-to-all-start = ((f32[32,64,128]{2,1,0:T(8,128)}), f32[32,64,128]{2,1,0:T(8,128)S(1)}, u32[]{:S(2)}, u32[]{:S(2)}) async-start(f32[32,64,128]{2,1,0:T(8,128)} %get-tuple-element.12), calls=%async_computation | async-start | bytes 2097152 | tf_op jit(solution)/shard_map/all_to_all | solution.py:682
  13.4 13.6 %own_pick.1 = (f32[2048,128]{1,0:T(8,128)S(1)}, f32[2048,128]{1,0:T(8,128)S(1)}, f32[64,128]{1,0:T(8,128)S(1)}, f32[256,128]{1,0:T(8,128)S(1)}) custom-call(s32[512,128]{1,0:T(8,128)} %get-tuple-element.13.packed_ref, f32[16,128]{1,0:T(8,128)} %get-tuple-element.14.scale_ref, bf16[432,256]{1,0:T(8,128)(2,1)} %get-tuple-element.15.table_ref, ...), custom_call_target="tpu_custom_call" | custom-call | bytes 60000000 | tf_op jit(solution)/shard_map/own_pick/pallas_call | solution.py:686
  27.0 3.3 %all-to-all-done.recv_ref = f32[32,64,128]{2,1,0:T(8,128)S(1)} async-done(((f32[32,64,128]{2,1,0:T(8,128)}), f32[32,64,128]{2,1,0:T(8,128)S(1)}, u32[]{:S(2)}, u32[]{:S(2)}) %all-to-all-start) | async-done | bytes 1048608 | tf_op jit(solution)/shard_map/all_to_all | solution.py:682
  30.3 18.3 %element_work.1 = f32[768,128]{1,0:T(8,128)S(1)} custom-call(s32[1]{0:T(128)} %bitcast.here_ref, f32[32,64,128]{2,1,0:T(8,128)S(1)} %all-to-all-done.recv_ref, f32[2048,128]{1,0:T(8,128)S(1)} %get-tuple-element.16.own_x_ref, f32[2048,128]{1,0:T(8,128)S(1)} %get-tuple-element.17.own_y_ref, f32[64,128]{1,0:T(8,128)S(1)} %get-tuple-element.18.rank_ref, ...), custom_call_target="tpu_custom_call" | custom-call | tf_op jit(solution)/shard_map/element_work/pallas_call | solution.py:697
  48.7 14.2 %all_to_all.15.recv_ref = f32[32,24,128]{2,1,0:T(8,128)S(1)} all-to-all(f32[32,24,128]{2,1,0:T(8,128)S(1)} %bitcast.8), channel_id=1, replica_groups=mesh['load'=8,'dom'=32] {'dom'}, dimensions={0} | all-to-all | bytes 786432 | tf_op jit(solution)/shard_map/all_to_all | solution.py:727
  62.9 3.4 %weigh_and_sum.1 = (f32[1,400]{1,0:T(1,128)}, f32[8,16,128]{2,1,0:T(8,128)S(1)}) custom-call(f32[32,24,128]{2,1,0:T(8,128)S(1)} %all_to_all.15.recv_ref, f32[1,400]{1,0:T(1,128)} %mult_ref.1), custom_call_target="tpu_custom_call" | custom-call | tf_op jit(solution)/shard_map/weigh_and_sum/pallas_call | solution.py:729
  66.3 15.1 %all_to_all.16 = f32[8,16,128]{2,1,0:T(8,128)S(1)} all-to-all(f32[8,16,128]{2,1,0:T(8,128)S(1)} %get-tuple-element.21), channel_id=1, replica_groups=mesh['load'=8,'dom'=32] {'load'}, dimensions={0} | all-to-all | bytes 131072 | tf_op jit(solution)/shard_map/all_to_all | solution.py:738
  81.4 0.6 reduce_sum.9
Async XLA Ops:
  4.8 25.5 %all-to-all-start = ((f32[32,64,128]{2,1,0:T(8,128)}), f32[32,64,128]{2,1,0:T(8,128)S(1)}, u32[]{:S(2)}, u32[]{:S(2)}) async-start(f32[32,64,128]{2,1,0:T(8,128)} %get-tuple-element.12), calls=%async_computation | async-start | bytes 2097152 | tf_op jit(solution)/shard_map/all_to_all | solution.py:682

commit v7 on v6

--- a/solution.py
+++ b/solution.py
@@ -10,7 +10,7 @@
 NBR = 3
 ROWS = 24
 HIGHS = 18
-GHOST_HIGHS = 6
+GHOST_HIGHS = 8
 SLICE = 1024
 CAP = 64
 ROOM = 16 * 1024 * 1024
@@ -245,11 +245,11 @@
         return fetch(jnp.minimum(b + 1, groups - 1))
 
     def several(turn, indices):
-        for k in range(4):
-            indices = body(turn * 4 + k, indices)
+        for k in range(16):
+            indices = body(turn * 16 + k, indices)
         return indices
 
-    lax.fori_loop(0, groups // 4, several, fetch(jnp.int32(0)))
+    lax.fori_loop(0, groups // 16, several, fetch(jnp.int32(0)))
 
 
 def slot_loop(dv_ref, values_of, rank_ref, write_rank_ref, out_ref, stride, *, domains, groups, owned, slots, cap):
@@ -474,13 +474,13 @@
             best_ref[c * 8 : c * 8 + 8] = jnp.maximum(held, jnp.where(away == c * 8, failure, LOW))
 
     def several(turn, found):
-        for k in range(3):
-            later = gather(turn * 3 + k + 1)
-            dense(turn * 3 + k, found)
+        for k in range(21):
+            later = gather(turn * 21 + k + 1)
+            dense(turn * 21 + k, found)
             found = later
         return found
 
-    dense(groups - 1, lax.fori_loop(0, (groups - 1) // 3, several, gather(jnp.int32(0))))
+    dense(groups - 1, lax.fori_loop(0, (groups - 1) // 21, several, gather(jnp.int32(0))))
 
     stats_ref[0] = jnp.zeros((8, LANES), F32)
     bands = (comps + LANES - 1) // LANES
@@ -512,15 +512,15 @@
 
         def total_step(step, totals, half=half):
             totals = list(totals)
-            for g in range(2):
-                row = pl.ds(step * 2 + g, 1)
+            for g in range(4):
+                row = pl.ds(step * 4 + g, 1)
                 away = comp_ref[row] - names
                 value = fail_ref[row]
                 for c in range(part_of):
                     totals[c] = totals[c] + jnp.where(away == (half * part_of + c) * 8, value, 0.0)
             return tuple(totals)
 
-        totals = lax.fori_loop(0, groups // 2, total_step, (jnp.zeros((8, LANES), F32),) * part_of)
+        totals = lax.fori_loop(0, groups // 4, total_step, (jnp.zeros((8, LANES), F32),) * part_of)
         for c in range(part_of):
             at = (half * part_of + c) * 8
             best_ref[at : at + 8] = totals[c]
@@ -617,11 +617,11 @@
         return both[0:outer] + both[outer : 2 * outer]
 
     def step(turn, sums):
-        return tuple(sums[m] + part_sum([turn * 4 + m * 2 + j for j in range(2)]) for m in range(2))
+        return tuple(sums[m] + part_sum([turn * 8 + m * 2 + j for j in range(2)]) for m in range(4))
 
     empty = jnp.zeros((outer, half), F32)
-    sums = lax.fori_loop(0, domains // 4, step, (empty, empty))
-    fold_ref[:, 0:half] = sums[0] + sums[1]
+    sums = lax.fori_loop(0, domains // 8, step, (empty,) * 4)
+    fold_ref[:, 0:half] = (sums[0] + sums[1]) + (sums[2] + sums[3])
     folded = jnp.concatenate(
         [fold_ref[pl.ds(parity, outer // 2, stride=2)][:, 0:half] for parity in range(2)], axis=1
     )

time: 82.4 us -> 78 us (0.947)
  Pallas kernels: 39.6 us -> 34.1 us
  waiting for transfers between devices: 3.26 us -> 4.61 us
    pallas_call x1, Pallas kernels: 18.3 us -> 15.2 us  [per_device(): pl.pallas_call(functools.partial(main_kernel, own=own, groups=groups, dom...]
    all_to_all x1, waiting for transfers between devices: 3.26 us -> 4.61 us  [per_device(): recv = lax.all_to_all(send, 'dom', 0, 0, tiled=True)]
    pallas_call x1, Pallas kernels: 13.6 us -> 12.3 us  [per_device(): pl.pallas_call(functools.partial(own_kernel, chunks=own, groups=groups, h...]
    pallas_call x1, Pallas kernels: 3.42 us -> 2.45 us  [per_device(): pl.pallas_call(functools.partial(last_kernel, domains=domains, comps=comp...]
  transfers between devices with their start and end apart: 1 -> 1, of which waited for: 1 -> 1; matrix products, arithmetic and copies ran while one was open for 0% -> 0% of each run, Pallas kernels for 17% -> 16%
where the time goes in v7:
time: 78 us; the launch traced here: 77.7 us
  Pallas kernels  34.1 us (44%)
  blocking collectives  29.1 us (37%)
  starting transfers between devices  8.57 us (11%)
  waiting for transfers between devices  4.61 us (6%)
    pallas_call x1, Pallas kernels, per_device(): pl.pallas_call(functools.partial(main_kernel, own=own, groups=groups, dom...  15.2 us
    all_to_all x1, blocking collectives, per_device(): lax.all_to_all(sums, 'load', 0, 0, tiled=True).sum(axis=0).reshape(-1)  15.1 us
    all_to_all x1, blocking collectives, per_device(): lax.all_to_all(mine.reshape(domains, 24, LANES), 'dom', 0, 0, tiled=True)  14 us
    pallas_call x1, Pallas kernels, per_device(): pl.pallas_call(functools.partial(own_kernel, chunks=own, groups=groups, h...  12.3 us
    all_to_all x1, starting transfers between devices, per_device(): recv = lax.all_to_all(send, 'dom', 0, 0, tiled=True)  8.57 us
    all_to_all x1, waiting for transfers between devices, per_device(): recv = lax.all_to_all(send, 'dom', 0, 0, tiled=True)  4.61 us
    pallas_call x1, Pallas kernels, per_device(): pl.pallas_call(functools.partial(send_kernel, chunks=own, domains=domains...  4.18 us
    pallas_call x1, Pallas kernels, per_device(): pl.pallas_call(functools.partial(last_kernel, domains=domains, comps=comp...  2.45 us
  transfers between devices with their start and end apart: 1, of which 1 were waited for; matrix products, arithmetic and copies ran while one was open for 0% of the time, Pallas kernels for 16%

profile of v7, /device:TPU:1, one launch (start us, length us, event | category | flops | bytes accessed | tf_op | source)
XLA Modules:
  0.0 77.7 jit_solution(6161409455932306831)
XLA Ops:
  0.6 4.2 %send_pick.1 = (s32[512,128]{1,0:T(8,128)}, f32[16,128]{1,0:T(8,128)}, bf16[432,256]{1,0:T(8,128)(2,1)}, f32[32,64,128]{2,1,0:T(8,128)}) custom-call(s32[1]{0:T(128)} %bitcast.here_ref, f32[384,128]{1,0:T(8,128)} %bitcast.9, f32[384,128]{1,0:T(8,128)} %bitcast.10, s32[1,32,512]{2,1,0:T(8,128)} %list_ref.1, f32[16,128]{1,0:T(8,128)} %bitcast.15), custom_call_target="tpu_custom_call" | custom-call | tf_op jit(solution)/shard_map/send_pick/pallas_call | solution.py:668
  4.8 8.6 %all-to-all-start = ((f32[32,64,128]{2,1,0:T(8,128)}), f32[32,64,128]{2,1,0:T(8,128)S(1)}, u32[]{:S(2)}, u32[]{:S(2)}) async-start(f32[32,64,128]{2,1,0:T(8,128)} %get-tuple-element.12), calls=%async_computation | async-start | bytes 2097152 | tf_op jit(solution)/shard_map/all_to_all | solution.py:682
  13.4 12.3 %own_pick.1 = (f32[2048,128]{1,0:T(8,128)S(1)}, f32[2048,128]{1,0:T(8,128)S(1)}, f32[64,128]{1,0:T(8,128)S(1)}, f32[256,128]{1,0:T(8,128)S(1)}) custom-call(s32[512,128]{1,0:T(8,128)} %get-tuple-element.13.packed_ref, f32[16,128]{1,0:T(8,128)} %get-tuple-element.14.scale_ref, bf16[432,256]{1,0:T(8,128)(2,1)} %get-tuple-element.15.table_ref, ...), custom_call_target="tpu_custom_call" | custom-call | bytes 60000000 | tf_op jit(solution)/shard_map/own_pick/pallas_call | solution.py:686
  25.7 4.6 %all-to-all-done.recv_ref = f32[32,64,128]{2,1,0:T(8,128)S(1)} async-done(((f32[32,64,128]{2,1,0:T(8,128)}), f32[32,64,128]{2,1,0:T(8,128)S(1)}, u32[]{:S(2)}, u32[]{:S(2)}) %all-to-all-start) | async-done | bytes 1048608 | tf_op jit(solution)/shard_map/all_to_all | solution.py:682
  30.3 15.2 %element_work.1 = f32[768,128]{1,0:T(8,128)S(1)} custom-call(s32[1]{0:T(128)} %bitcast.here_ref, f32[32,64,128]{2,1,0:T(8,128)S(1)} %all-to-all-done.recv_ref, f32[2048,128]{1,0:T(8,128)S(1)} %get-tuple-element.16.own_x_ref, f32[2048,128]{1,0:T(8,128)S(1)} %get-tuple-element.17.own_y_ref, f32[64,128]{1,0:T(8,128)S(1)} %get-tuple-element.18.rank_ref, ...), custom_call_target="tpu_custom_call" | custom-call | tf_op jit(solution)/shard_map/element_work/pallas_call | solution.py:697
  45.5 14.0 %all_to_all.15.recv_ref = f32[32,24,128]{2,1,0:T(8,128)S(1)} all-to-all(f32[32,24,128]{2,1,0:T(8,128)S(1)} %bitcast.8), channel_id=1, replica_groups=mesh['load'=8,'dom'=32] {'dom'}, dimensions={0} | all-to-all | bytes 786432 | tf_op jit(solution)/shard_map/all_to_all | solution.py:727
  59.5 2.4 %weigh_and_sum.1 = (f32[1,400]{1,0:T(1,128)}, f32[8,16,128]{2,1,0:T(8,128)S(1)}) custom-call(f32[32,24,128]{2,1,0:T(8,128)S(1)} %all_to_all.15.recv_ref, f32[1,400]{1,0:T(1,128)} %mult_ref.1), custom_call_target="tpu_custom_call" | custom-call | tf_op jit(solution)/shard_map/weigh_and_sum/pallas_call | solution.py:729
  61.9 15.1 %all_to_all.16 = f32[8,16,128]{2,1,0:T(8,128)S(1)} all-to-all(f32[8,16,128]{2,1,0:T(8,128)S(1)} %get-tuple-element.21), channel_id=1, replica_groups=mesh['load'=8,'dom'=32] {'load'}, dimensions={0} | all-to-all | bytes 131072 | tf_op jit(solution)/shard_map/all_to_all | solution.py:738
  77.1 0.6 reduce_sum.9
Async XLA Ops:
  4.8 25.5 %all-to-all-start = ((f32[32,64,128]{2,1,0:T(8,128)}), f32[32,64,128]{2,1,0:T(8,128)S(1)}, u32[]{:S(2)}, u32[]{:S(2)}) async-start(f32[32,64,128]{2,1,0:T(8,128)} %get-tuple-element.12), calls=%async_computation | async-start | bytes 2097152 | tf_op jit(solution)/shard_map/all_to_all | solution.py:682

commit v8 on v7

--- a/solution.py
+++ b/solution.py
@@ -209,16 +209,34 @@
     connect_ref,
     comp_ref,
     dv_ref,
+    s_memb_ref,
+    s_bend_ref,
+    k_memb_ref,
+    k_bend_ref,
     own_x_ref,
     own_y_ref,
     rank_ref,
     ids_ref,
+    weight_ref,
     *,
     chunks,
     groups,
     highs,
     **sizes,
 ):
+    wide = spread_matrix(False)
+    tall = spread_matrix(True)
+    weights = jnp.concatenate(
+        [
+            dot(s_memb_ref[...], wide),
+            dot(s_bend_ref[...], wide),
+            dot(tall, dot(k_memb_ref[...], wide)),
+            dot(tall, dot(k_bend_ref[...], wide)),
+        ],
+        axis=0,
+    )
+    w = three_parts(weights)
+    weight_ref[...] = jnp.concatenate([w[0], w[0], w[1], w[0], w[1], w[2]], axis=1)
     slot_loop(
         dv_ref,
         lambda row, place: ((place & (sizes["owned"] - 1)).astype(F32), comp_ref[row].astype(F32)),
@@ -342,10 +360,7 @@
     connect_ref,
     comp_ref,
     dv_ref,
-    s_memb_ref,
-    s_bend_ref,
-    k_memb_ref,
-    k_bend_ref,
+    weight_ref,
     out_ref,
     ghost_ref,
     wide_ref,
@@ -410,19 +425,7 @@
     def _(turn):
         panel_step(0, turn * 8, 8)
 
-    wide = spread_matrix(False)
-    tall = spread_matrix(True)
-    weights = jnp.concatenate(
-        [
-            dot(s_memb_ref[...], wide),
-            dot(s_bend_ref[...], wide),
-            dot(tall, dot(k_memb_ref[...], wide)),
-            dot(tall, dot(k_bend_ref[...], wide)),
-        ],
-        axis=0,
-    )
-    w = three_parts(weights)
-    stacked_weights = jnp.concatenate([w[0], w[0], w[1], w[0], w[1], w[2]], axis=1)
+    stacked_weights = weight_ref[...]
     names = lax.broadcasted_iota(I32, (8, LANES), 0)
     combs = comps // 8
     best_ref[...] = jnp.full(best_ref.shape, LOW, F32)
@@ -683,17 +686,17 @@
     comp = far(elem_comp.reshape(-1, LANES))
     dv = far(elem_dv.reshape(-1, LANES))
     owned = thickness.shape[0]
-    own_x, own_y, ranks, ids = pl.pallas_call(
+    own_x, own_y, ranks, ids, weights = pl.pallas_call(
         functools.partial(
             own_kernel, chunks=own, groups=groups, highs=highs, domains=domains, owned=owned, slots=SLICE, cap=CAP
         ),
-        out_shape=(near((groups * 32, LANES), F32),) * 2 + (near((groups, LANES), F32), near((domains * 8, LANES), F32)),
-        in_specs=[vmem()] * 6,
-        out_specs=(vmem(),) * 4,
+        out_shape=(near((groups * 32, LANES), F32),) * 2 + (near((groups, LANES), F32), near((domains * 8, LANES), F32), near((80, 192), BF16)),
+        in_specs=[vmem()] * 10,
+        out_specs=(vmem(),) * 5,
         compiler_params=pltpu.CompilerParams(vmem_limit_bytes=ROOM),
         name="own_pick",
         cost_estimate=pl.CostEstimate(flops=0, transcendentals=0, bytes_accessed=60_000_000),
-    )(far(packed), far(scale), far(table), connect, comp, dv)
+    )(far(packed), far(scale), far(table), connect, comp, dv, far(s_memb), far(s_bend), far(k_memb), far(k_bend))
     mine = pl.pallas_call(
         functools.partial(
             main_kernel,
@@ -708,7 +711,7 @@
             cap=CAP,
         ),
         out_shape=near((domains * 24, LANES), F32),
-        in_specs=[smem()] + [vmem()] * 12,
+        in_specs=[smem()] + [vmem()] * 9,
         out_specs=vmem(),
         scratch_shapes=[
             pltpu.VMEM(((len(OFFSETS) * iface // LANES - 2 * ghost_highs) * 8, LANES), I32),
@@ -723,7 +726,7 @@
         ],
         compiler_params=pltpu.CompilerParams(vmem_limit_bytes=ROOM),
         name="element_work",
-    )(here, close(recv), close(own_x), close(own_y), close(ranks), close(ids), connect, comp, dv, far(s_memb), far(s_bend), far(k_memb), far(k_bend))
+    )(here, close(recv), close(own_x), close(own_y), close(ranks), close(ids), connect, comp, dv, close(weights))
     everyone = lax.all_to_all(mine.reshape(domains, 24, LANES), "dom", 0, 0, tiled=True)
     loads = lax.axis_size("load")
     ks_value, sums = pl.pallas_call(

time: 78 us -> 77.5 us (level)
  transfers between devices with their start and end apart: 1 -> 1, of which waited for: 1 -> 1; matrix products, arithmetic and copies ran while one was open for 0% -> 0% of each run, Pallas kernels for 16% -> 17%
where the time goes in v8:
time: 77.5 us; the launch traced here: 77.2 us
  Pallas kernels  34.3 us (44%)
  blocking collectives  29.1 us (38%)
  starting transfers between devices  8.57 us (11%)
  waiting for transfers between devices  3.93 us (5%)
    all_to_all x1, blocking collectives, per_device(): lax.all_to_all(sums, 'load', 0, 0, tiled=True).sum(axis=0).reshape(-1)  15.1 us
    pallas_call x1, Pallas kernels, per_device(): pl.pallas_call(functools.partial(main_kernel, own=own, groups=groups, dom...  14.7 us
    all_to_all x1, blocking collectives, per_device(): lax.all_to_all(mine.reshape(domains, 24, LANES), 'dom', 0, 0, tiled=True)  14 us
    pallas_call x1, Pallas kernels, per_device(): pl.pallas_call(functools.partial(own_kernel, chunks=own, groups=groups, h...  13 us
    all_to_all x1, starting transfers between devices, per_device(): recv = lax.all_to_all(send, 'dom', 0, 0, tiled=True)  8.57 us
    pallas_call x1, Pallas kernels, per_device(): pl.pallas_call(functools.partial(send_kernel, chunks=own, domains=domains...  4.18 us
    all_to_all x1, waiting for transfers between devices, per_device(): recv = lax.all_to_all(send, 'dom', 0, 0, tiled=True)  3.93 us
    pallas_call x1, Pallas kernels, per_device(): pl.pallas_call(functools.partial(last_kernel, domains=domains, comps=comp...  2.45 us
  transfers between devices with their start and end apart: 1, of which 1 were waited for; matrix products, arithmetic and copies ran while one was open for 0% of the time, Pallas kernels for 17%

profile of v8, /device:TPU:1, one launch (start us, length us, event | category | flops | bytes accessed | tf_op | source)
XLA Modules:
  0.0 77.2 jit_solution(17293475193822015168)
XLA Ops:
  0.6 4.2 %send_pick.1 = (s32[512,128]{1,0:T(8,128)}, f32[16,128]{1,0:T(8,128)}, bf16[432,256]{1,0:T(8,128)(2,1)}, f32[32,64,128]{2,1,0:T(8,128)}) custom-call(s32[1]{0:T(128)} %bitcast.here_ref, f32[384,128]{1,0:T(8,128)} %bitcast.9, f32[384,128]{1,0:T(8,128)} %bitcast.10, s32[1,32,512]{2,1,0:T(8,128)} %list_ref.1, f32[16,128]{1,0:T(8,128)} %bitcast.15), custom_call_target="tpu_custom_call" | custom-call | tf_op jit(solution)/shard_map/send_pick/pallas_call | solution.py:671
  4.8 8.6 %all-to-all-start = ((f32[32,64,128]{2,1,0:T(8,128)}), f32[32,64,128]{2,1,0:T(8,128)S(1)}, u32[]{:S(2)}, u32[]{:S(2)}) async-start(f32[32,64,128]{2,1,0:T(8,128)} %get-tuple-element.13), calls=%async_computation | async-start | bytes 2097152 | tf_op jit(solution)/shard_map/all_to_all | solution.py:685
  13.4 13.0 %own_pick.1 = (f32[2048,128]{1,0:T(8,128)S(1)}, f32[2048,128]{1,0:T(8,128)S(1)}, f32[64,128]{1,0:T(8,128)S(1)}, f32[256,128]{1,0:T(8,128)S(1)}, bf16[80,192]{1,0:T(8,128)(2,1)S(1)}) custom-call(s32[512,128]{1,0:T(8,128)} %get-tuple-element.14.packed_ref, f32[16,128]{1,0:T(8,128)} %get-tuple-element.15.scale_ref, ...), custom_call_target="tpu_custom_call" | custom-call | bytes 60000000 | tf_op jit(solution)/shard_map/own_pick/pallas_call | solution.py:689
  26.4 3.9 %all-to-all-done.recv_ref = f32[32,64,128]{2,1,0:T(8,128)S(1)} async-done(((f32[32,64,128]{2,1,0:T(8,128)}), f32[32,64,128]{2,1,0:T(8,128)S(1)}, u32[]{:S(2)}, u32[]{:S(2)}) %all-to-all-start) | async-done | bytes 1048608 | tf_op jit(solution)/shard_map/all_to_all | solution.py:685
  30.3 14.7 %element_work.1 = f32[768,128]{1,0:T(8,128)S(1)} custom-call(s32[1]{0:T(128)} %bitcast.here_ref, f32[32,64,128]{2,1,0:T(8,128)S(1)} %all-to-all-done.recv_ref, f32[2048,128]{1,0:T(8,128)S(1)} %get-tuple-element.17.own_x_ref, f32[2048,128]{1,0:T(8,128)S(1)} %get-tuple-element.18.own_y_ref, f32[64,128]{1,0:T(8,128)S(1)} %get-tuple-element.19.rank_ref, ...), custom_call_target="tpu_custom_call" | custom-call | tf_op jit(solution)/shard_map/element_work/pallas_call | solution.py:700
  45.0 14.0 %all_to_all.15.recv_ref = f32[32,24,128]{2,1,0:T(8,128)S(1)} all-to-all(f32[32,24,128]{2,1,0:T(8,128)S(1)} %bitcast.8), channel_id=1, replica_groups=mesh['load'=8,'dom'=32] {'dom'}, dimensions={0} | all-to-all | bytes 786432 | tf_op jit(solution)/shard_map/all_to_all | solution.py:730
  59.0 2.5 %weigh_and_sum.1 = (f32[1,400]{1,0:T(1,128)}, f32[8,16,128]{2,1,0:T(8,128)S(1)}) custom-call(f32[32,24,128]{2,1,0:T(8,128)S(1)} %all_to_all.15.recv_ref, f32[1,400]{1,0:T(1,128)} %mult_ref.1), custom_call_target="tpu_custom_call" | custom-call | tf_op jit(solution)/shard_map/weigh_and_sum/pallas_call | solution.py:732
  61.5 15.1 %all_to_all.16 = f32[8,16,128]{2,1,0:T(8,128)S(1)} all-to-all(f32[8,16,128]{2,1,0:T(8,128)S(1)} %get-tuple-element.23), channel_id=1, replica_groups=mesh['load'=8,'dom'=32] {'load'}, dimensions={0} | all-to-all | bytes 131072 | tf_op jit(solution)/shard_map/all_to_all | solution.py:741
  76.6 0.6 reduce_sum.9
Async XLA Ops:
  4.8 25.5 %all-to-all-start = ((f32[32,64,128]{2,1,0:T(8,128)}), f32[32,64,128]{2,1,0:T(8,128)S(1)}, u32[]{:S(2)}, u32[]{:S(2)}) async-start(f32[32,64,128]{2,1,0:T(8,128)} %get-tuple-element.13), calls=%async_computation | async-start | bytes 2097152 | tf_op jit(solution)/shard_map/all_to_all | solution.py:685
